TPU v7x, 32 devices: a whole 2x2x4 slice. The times are simulated.
32 devices in a mesh: row: 2 (over x), col: 4 (over z), freq: 4 (over y, core).
Axes of the slice: x: 2, y: 2, z: 4, core: 2. Of those that a mesh axis runs over, the one named last changes fastest.
Arguments:
- data: bfloat16 [2, 4, 2048, 2048], P(None, 'freq', 'row', 'col'), may hold values from -4.7729708 to 4.7729708, as said below
- primaries: bfloat16 [2, 4, 2048, 2048], P(None, 'freq', 'row', 'col'), may hold values from -6 to 6
Outputs:
- updated_primaries: bfloat16 [2, 4, 2048, 2048], P(None, 'freq', 'row', 'col')
- updated_residual: float32 [2, 4, 2048, 2048], P(None, 'freq', 'row', 'col')
Inputs may be any that keep to these rules, and one draw needn't show every extreme that they name: `data`: magnitudes vary by source, receiver and frequency.
All inputs are finite; a program needn't handle non-finite values.
Results may differ from a plain program's by a relative error of at most 0.0045.
Values may be sent and summed in bfloat16 or wider, within the bound.
No kernel may reach another device: no remote copies, remote signals or barrier semaphores. Data moves between devices by JAX's collectives and lax.ppermute only.
A program may use at most 128 MiB of HBM per device.

v0:
```python
import jax
import jax.numpy as jnp
from jax import lax
from jax.sharding import PartitionSpec as P


def batched(left, right):
    return jnp.einsum("fik,fkj->fij", left, right, preferred_element_type=jnp.float32)


def complex_product(left, right):
    real = batched(left[0], right[0]) - batched(left[1], right[1])
    imag = batched(left[0], right[1]) + batched(left[1], right[0])
    return jnp.stack([real, imag])


def gradient_step(data_part, primary_part):
    src_rows = data_part.shape[2]
    columns = lax.all_gather(data_part, "row", axis=2, tiled=True)

    def add_block(piece):
        return complex_product(piece, columns)

    forward = add_block(lax.all_gather(primary_part, "col", axis=3, tiled=True))
    residual = data_part.astype(jnp.float32) - primary_part.astype(jnp.float32) + forward
    rounded = residual.astype(jnp.bfloat16)
    real = jnp.einsum("fjk,fik->jfi", columns[0], rounded[0], preferred_element_type=jnp.float32)
    real = real + jnp.einsum(
        "fjk,fik->jfi", columns[1], rounded[1], preferred_element_type=jnp.float32
    )
    imag = jnp.einsum("fjk,fik->jfi", columns[0], rounded[1], preferred_element_type=jnp.float32)
    imag = imag - jnp.einsum(
        "fjk,fik->jfi", columns[1], rounded[0], preferred_element_type=jnp.float32
    )
    summed = lax.psum_scatter(
        jnp.concatenate([real, imag], axis=2), "col", scatter_dimension=0, tiled=True
    )
    adjoint = jnp.stack([summed[:, :, :src_rows], summed[:, :, src_rows:]]).transpose(0, 2, 3, 1)
    gradient = (adjoint - residual).astype(jnp.bfloat16)
    moved = add_block(lax.all_gather(gradient, "col", axis=3, tiled=True))
    change = moved - gradient.astype(jnp.float32)
    return (residual, gradient, change)


def local(data, primaries):
    res, grad, chg = gradient_step(data, primaries)
    inner_local = jnp.sum(chg * res)
    energy_local = jnp.sum(chg * chg)
    inner, energy = lax.psum((inner_local, energy_local), ("row", "col", "freq"))
    step = -inner / (energy + 1e-06)
    updated_primaries = (primaries.astype(jnp.float32) + step * grad.astype(jnp.float32)).astype(
        jnp.bfloat16
    )
    updated_residual = res + step * chg
    return (updated_primaries, updated_residual)


def solution(mesh):
    in_specs = (P(None, "freq", "row", "col"), P(None, "freq", "row", "col"))
    out_specs = (P(None, "freq", "row", "col"), P(None, "freq", "row", "col"))
    return jax.shard_map(local, mesh=mesh, in_specs=in_specs, out_specs=out_specs, check_vma=False)
```

profile of v0, /device:TPU:20, one launch (start us, length us, event | category | flops | bytes accessed | tf_op | source)
XLA Modules:
  0.0 758.3 jit_solution(8041567438124025095)
XLA Ops:
  7.2 0.0 all-gather.6.cloned.1.call-start
  7.2 0.7 all-gather.6.cloned.1.call-update
  7.9 0.0 all-gather.4.cloned.1.call-start
  7.9 0.7 all-gather.4.cloned.1.call-update
  8.6 0.0 reduce-scatter.2.cloned.1.call-start
  8.7 58.7 %all-gather.6.cloned.1.call-done = bf16[2,1,2048,512]{3,2,1,0:T(8,128)(2,1)} async-done(((bf16[2,1,1024,512]{3,2,1,0:T(8,128)(2,1)}), bf16[2,1,2048,512]{3,2,1,0:T(8,128)(2,1)}) %all-gather.6.cloned.1.call-update) | async-done | bytes 4194320 | tf_op jit(solution)/shard_map/all_gather | solution.py:19
  67.3 149.4 %all-gather.4.cloned.1.call-done = bf16[2,1,1024,2048]{3,2,1,0:T(8,128)(2,1)} async-done(((bf16[2,1,1024,512]{3,2,1,0:T(8,128)(2,1)}), bf16[2,1,1024,2048]{3,2,1,0:T(8,128)(2,1)}) %all-gather.4.cloned.1.call-update) | async-done | bytes 8388624 | tf_op jit(solution)/shard_map/all_gather | solution.py:24
  216.8 0.0 copy-start.8
  216.8 0.0 copy-start.10
  216.8 5.3 fusion.4
  222.1 0.0 copy-done.8
  222.1 1.1 copy-done.10
  223.2 2.3 fusion.5
  225.6 2.3 add_bitcast_fusion.2
  227.9 0.0 copy-start.4
  227.9 0.0 copy-start.7
  227.9 2.3 subtract_bitcast_fusion.2
  230.2 0.0 copy-done.4
  230.3 0.0 copy-done.7
  230.3 3.1 fusion.14
  233.3 2.4 fusion.13
  235.7 2.4 fusion.12
  238.1 2.4 subtract_bitcast_fusion
  240.4 2.5 add_bitcast_fusion
  243.0 6.2 pad_maximum_fusion
  249.2 0.0 reduce-scatter.2.cloned.1.call-update
  249.2 0.0 all-gather.8.cloned.1.call-start
  249.3 281.1 %reduce-scatter.2.cloned.1.call-done = f32[512,1,2048]{0,2,1:T(8,128)} async-done(((f32[2048,1,2048]{0,2,1:T(8,128)}), f32[512,1,2048]{0,2,1:T(8,128)}) %reduce-scatter.2.cloned.1.call-update) | async-done | bytes 4194320 | tf_op jit(solution)/shard_map/reduce_scatter | solution.py:35
  530.4 0.0 copy-start
  530.4 2.8 slice_bitcast_fusion.13
  533.3 0.0 copy-start.2
  533.3 1.4 copy-done.2
  534.7 0.0 copy-done
  534.7 2.2 fusion.3
  536.8 0.0 all-gather.8.cloned.1.call-update
  536.8 148.0 %all-gather.8.cloned.1.call-done = bf16[2,1,1024,2048]{3,2,1,0:T(8,128)(2,1)} async-done(((bf16[2,1,1024,512]{3,2,1,0:T(8,128)(2,1)}), bf16[2,1,1024,2048]{3,2,1,0:T(8,128)(2,1)}) %all-gather.8.cloned.1.call-update) | async-done | bytes 8388624 | tf_op jit(solution)/shard_map/all_gather | solution.py:40
  684.8 0.0 copy-start.9
  684.8 0.0 copy-start.11
  684.8 5.3 fusion.8
  690.1 0.0 copy-done.9
  690.1 1.1 copy-done.11
  691.3 2.3 fusion.9
  693.6 2.3 add_bitcast_fusion.1
  695.9 0.0 copy-start.5
  695.9 0.0 copy-start.1
  695.9 0.0 copy-start.3
  695.9 2.3 subtract_bitcast_fusion.1
  698.3 0.0 copy-done.5
  698.3 0.6 copy-done.1
  698.9 0.7 copy-done.3
  699.5 0.0 copy-start.6
  699.5 2.3 multiply_reduce_fusion
  701.8 0.0 copy-done.6
  701.8 41.4 %all-reduce = (f32[]{:T(128)}, f32[]{:T(128)}) all-reduce(f32[]{:T(128)} %get-tuple-element.3, f32[]{:T(128)} %get-tuple-element.2), channel_id=1, replica_groups=mesh['row'=2,'col'=4,'freq'=4] {'row','col','freq'}, use_global_device_ids=true, to_apply=%region_2.0 | all-reduce | flops 2 | bytes 16 | tf_op jit(solution)/shard_map/psum | solution.py:49
  744.5 7.2 multiply_add_fusion
Async XLA Ops:
  7.2 60.2 %all-gather.6.cloned.1.call-start = ((), (), s32[]{:S(2)}) async-start(), calls=%async_computation.2 | async-start | bytes 6291456 | tf_op jit(solution)/shard_map/all_gather | solution.py:19
  7.9 208.9 %all-gather.4.cloned.1.call-start = ((), (), s32[]{:S(2)}) async-start(), calls=%async_computation.1 | async-start | bytes 10485760 | tf_op jit(solution)/shard_map/all_gather | solution.py:24
  8.6 521.8 %reduce-scatter.2.cloned.1.call-start = ((), (), s32[]{:S(2)}) async-start(), calls=%async_computation.3 | async-start | bytes 20971520 | tf_op jit(solution)/shard_map/reduce_scatter | solution.py:35
  216.8 5.3 copy-start.8
  216.8 6.4 copy-start.10
  227.9 2.4 copy-start.4
  227.9 2.4 copy-start.7
  249.2 435.6 %all-gather.8.cloned.1.call-start = ((), (), s32[]{:S(2)}) async-start(), calls=%async_computation.4 | async-start | bytes 10485760 | tf_op jit(solution)/shard_map/all_gather | solution.py:40
  530.4 4.2 copy-start
  533.3 1.4 copy-start.2
  684.8 5.3 copy-start.9
  684.8 6.4 copy-start.11
  695.9 2.4 copy-start.5
  695.9 2.9 copy-start.1
  695.9 3.6 copy-start.3
  699.5 2.3 copy-start.6
Sparse Core Ops, SparseCore 0:
  9.5 57.7 all-gather.5
  68.9 147.8 all-gather.3
  249.4 281.0 reduce-scatter.1
  537.0 147.7 all-gather.7
where the time goes:
time: 760 us; the launch traced here: 758 us
  waiting for transfers between devices  639 us (84%)
  blocking collectives  41.4 us (5%)
  matrix products  34.2 us (5%)
  other arithmetic  20.9 us (3%)
  between operations  15.2 us (2%)
  local copies, waits for them, and re-layouts  7.7 us (1%)
    reduce_scatter x1, waiting for transfers between devices, gradient_step(): lax.psum_scatter(jnp.concatenate([real, imag], axis=2), 'col', scatter_di...  281 us
    all_gather x1, waiting for transfers between devices, gradient_step(): forward = add_block(lax.all_gather(primary_part, 'col', axis=3, tiled=True))  149 us
    all_gather x1, waiting for transfers between devices, gradient_step(): moved = add_block(lax.all_gather(gradient, 'col', axis=3, tiled=True))  148 us
    all_gather x1, waiting for transfers between devices, gradient_step(): columns = lax.all_gather(data_part, 'row', axis=2, tiled=True)  58.7 us
    psum x1, blocking collectives, local(): lax.psum((inner_local, energy_local), ('row', 'col', 'freq'))  41.4 us
    dot_general x8, matrix products, batched(): jnp.einsum('fik,fkj->fij', left, right, preferred_element_type=jnp.float32)  24.6 us
  transfers between devices with their start and end apart: 4, of which 4 were waited for; matrix products, arithmetic and copies ran while one was open for 0% of the time, Pallas kernels for 0%

commit v1 on v0

--- a/solution.py
+++ b/solution.py
@@ -1,7 +1,12 @@
 import jax
 import jax.numpy as jnp
 from jax import lax
+from jax.experimental import pallas as pl
+from jax.experimental.pallas import tpu as pltpu
 from jax.sharding import PartitionSpec as P
+
+VMEM_BYTES = 56 * 1024 * 1024
+MESSAGE_GROUPS = ((0, 1), (2, 3))
 
 
 def batched(left, right):
@@ -14,7 +19,7 @@
     return jnp.stack([real, imag])
 
 
-def gradient_step(data_part, primary_part):
+def blocked_gradient(data_part, primary_part):
     src_rows = data_part.shape[2]
     columns = lax.all_gather(data_part, "row", axis=2, tiled=True)
 
@@ -42,8 +47,8 @@
     return (residual, gradient, change)
 
 
-def local(data, primaries):
-    res, grad, chg = gradient_step(data, primaries)
+def blocked(data, primaries):
+    res, grad, chg = blocked_gradient(data, primaries)
     inner_local = jnp.sum(chg * res)
     energy_local = jnp.sum(chg * chg)
     inner, energy = lax.psum((inner_local, energy_local), ("row", "col", "freq"))
@@ -55,7 +60,290 @@
     return (updated_primaries, updated_residual)
 
 
+class Plan:
+    def __init__(self, rows, cols, freqs):
+        self.rows, self.cols, self.freqs = rows, cols, freqs
+
+    def send(self, k):
+        pairs = []
+        for z in range(self.cols):
+            for f in range(self.freqs):
+                part, half = z ^ k, f % 2
+                home = half * self.cols // 2 + part // 2
+                pairs.append((z * self.freqs + f, home * self.freqs + f // 2 * 2 + part % 2))
+        return pairs
+
+    def to_home(self, blocks, z, k):
+        piece = lax.dynamic_index_in_dim(blocks, z ^ k, 1, keepdims=False)
+        return lax.ppermute(piece, ("col", "freq"), self.send(k))
+
+    def from_home(self, piece, k):
+        return lax.ppermute(piece, ("col", "freq"), [(b, a) for a, b in self.send(k)])
+
+    def over_row(self, value):
+        return lax.ppermute(value, "row", [(i, i ^ 1) for i in range(self.rows)])
+
+    def over_core(self, value):
+        return lax.ppermute(value, "freq", [(i, i ^ 1) for i in range(self.freqs)])
+
+    def over_freq(self, value):
+        return lax.ppermute(value, "freq", [(i, i ^ 2) for i in range(self.freqs)])
+
+    def over_col(self, value, by):
+        return lax.ppermute(value, "col", [(i, i ^ by) for i in range(self.cols)])
+
+    def total(self, value):
+        value = value + self.over_core(value)
+        value = value + self.over_col(value, 1)
+        value = value + self.over_col(value, 2)
+        value = value + self.over_row(value)
+        return value + self.over_freq(value)
+
+
+def place_copies(where, buffers, slots, data_v, sems, rows):
+    row_index, part = where
+    copies = {}
+    for number, (slot, (dx, dp, k)) in enumerate(slots):
+        ref, sub = buffers[slot[0]], slot[1]
+        start = ((row_index ^ dx) * 4 + (part ^ dp)) * rows
+        target = data_v.at[dp ^ k, :, pl.ds(pl.multiple_of(start, rows), rows), :]
+        source = ref if sub is None else ref.at[sub]
+        copies.setdefault(dp ^ k, []).append(pltpu.make_async_copy(source, target, sems.at[number]))
+    return copies
+
+
+def product(stacked, right, rows):
+    one = jnp.dot(stacked, right[0], preferred_element_type=jnp.float32)
+    two = jnp.dot(stacked, right[1], preferred_element_type=jnp.float32)
+    return one[:rows] - two[rows:], one[rows:] + two[:rows]
+
+
+def residual_gradient_kernel(slots, n_buffers, rows, width, where_ref, *refs):
+    buffers, refs = refs[:n_buffers], refs[n_buffers:]
+    x_refs, refs = refs[:4], refs[4:]
+    r_out, refs = refs[0], refs[1:]
+    g_outs, refs = refs[:4], refs[4:]
+    data_v, rows_v, x_v, r_v, rb_v, g_v, sems, x_sems, out_sems = refs
+    row_index, part = where_ref[0], where_ref[1]
+    copies = place_copies((row_index, part), buffers, slots, data_v, sems, rows)
+    x_copies = []
+    for k in range(4):
+        at = pl.ds(pl.multiple_of((part ^ k) * width, width), width)
+        for i in range(2):
+            x_copies.append(
+                pltpu.make_async_copy(
+                    x_refs[k].at[i], rows_v.at[pl.ds(i * rows, rows), at], x_sems.at[3 * k + i]
+                )
+            )
+        x_copies.append(pltpu.make_async_copy(x_refs[k], x_v.at[k], x_sems.at[3 * k + 2]))
+    for copy in x_copies:
+        copy.start()
+    for t in range(4):
+        for copy in copies[t]:
+            copy.start()
+    for copy in x_copies:
+        copy.wait()
+    own = pl.ds(pl.multiple_of((row_index * 4 + part) * rows, rows), rows)
+    outs = []
+    for t in range(4):
+        for copy in copies[t]:
+            copy.wait()
+        forward = product(rows_v[...], (data_v[t, 0], data_v[t, 1]), rows)
+        for i in range(2):
+            residual = (
+                data_v[t, i, own, :].astype(jnp.float32)
+                - x_v[t, i].astype(jnp.float32)
+                + forward[i]
+            )
+            r_v[t, i] = residual
+            rb_v[t, i * rows : (i + 1) * rows, :] = residual.astype(jnp.bfloat16)
+        copy = pltpu.make_async_copy(r_v.at[t], r_out.at[t], out_sems.at[t])
+        copy.start()
+        outs.append(copy)
+
+    def against(left, right):
+        return lax.dot_general(
+            left, right, (((1,), (1,)), ((), ())), preferred_element_type=jnp.float32
+        )
+
+    for k in range(4):
+        at = pl.ds(pl.multiple_of((part ^ k) * width, width), width)
+        one = against(rb_v[0], data_v[0, 0, at, :])
+        two = against(rb_v[0], data_v[0, 1, at, :])
+        for t in range(1, 4):
+            one = one + against(rb_v[t], data_v[t, 0, at, :])
+            two = two + against(rb_v[t], data_v[t, 1, at, :])
+        g_v[k, 0] = (one[:rows] + two[rows:] - r_v[k, 0]).astype(jnp.bfloat16)
+        g_v[k, 1] = (one[rows:] - two[:rows] - r_v[k, 1]).astype(jnp.bfloat16)
+        copy = pltpu.make_async_copy(g_v.at[k], g_outs[k], out_sems.at[4 + k])
+        copy.start()
+        outs.append(copy)
+    for copy in outs:
+        copy.wait()
+
+
+def change_kernel(slots, n_buffers, rows, width, where_ref, *refs):
+    buffers, refs = refs[:n_buffers], refs[n_buffers:]
+    g_refs, refs = refs[:4], refs[4:]
+    r_in, c_out, sums_out, refs = refs[0], refs[1], refs[2], refs[3:]
+    data_v, rows_v, g_v, r_v, c_v, sems, g_sems, r_sems, out_sems = refs
+    row_index, part = where_ref[0], where_ref[1]
+    copies = place_copies((row_index, part), buffers, slots, data_v, sems, rows)
+    g_copies = []
+    for k in range(4):
+        at = pl.ds(pl.multiple_of((part ^ k) * width, width), width)
+        for i in range(2):
+            g_copies.append(
+                pltpu.make_async_copy(
+                    g_refs[k].at[i], rows_v.at[pl.ds(i * rows, rows), at], g_sems.at[3 * k + i]
+                )
+            )
+        g_copies.append(pltpu.make_async_copy(g_refs[k], g_v.at[k], g_sems.at[3 * k + 2]))
+    for copy in g_copies:
+        copy.start()
+    r_copies = []
+    for t in range(4):
+        for copy in copies[t]:
+            copy.start()
+        r_copies.append(pltpu.make_async_copy(r_in.at[t], r_v.at[t], r_sems.at[t]))
+        r_copies[t].start()
+    for copy in g_copies:
+        copy.wait()
+    inner = jnp.float32(0)
+    energy = jnp.float32(0)
+    outs = []
+    for t in range(4):
+        for copy in copies[t]:
+            copy.wait()
+        moved = product(rows_v[...], (data_v[t, 0], data_v[t, 1]), rows)
+        r_copies[t].wait()
+        for i in range(2):
+            change = moved[i] - g_v[t, i].astype(jnp.float32)
+            c_v[t, i] = change
+            inner = inner + jnp.sum(change * r_v[t, i])
+            energy = energy + jnp.sum(change * change)
+        copy = pltpu.make_async_copy(c_v.at[t], c_out.at[t], out_sems.at[t])
+        copy.start()
+        outs.append(copy)
+    sums_out[0] = inner
+    sums_out[1] = energy
+    for copy in outs:
+        copy.wait()
+
+
+def whole_rows(plan, data, primaries):
+    z = lax.axis_index("col")
+    row_index = lax.axis_index("row")
+    part = z % (plan.cols // 2) * 2 + lax.axis_index("freq") % 2
+    n_rows, width = data.shape[2], data.shape[3]
+    rows = n_rows // plan.cols
+    where = jnp.stack([row_index, part]).astype(jnp.int32)
+    data_blocks = data.reshape(2, plan.cols, rows, width)
+    prim_blocks = primaries.reshape(2, plan.cols, rows, width)
+
+    buffers, slots = [], []
+    arrived = None
+    for group in MESSAGE_GROUPS:
+        own = [plan.to_home(data_blocks, z, k) for k in group]
+        arrived = own
+        own = own[0] if len(group) == 1 else jnp.stack(own)
+        held = {(0, 0): own}
+        held[(0, 2)] = plan.over_col(own, 1)
+        held.update({(1, dp): plan.over_row(v) for (_, dp), v in list(held.items())})
+        held.update({(dx, dp ^ 1): plan.over_core(v) for (dx, dp), v in list(held.items())})
+        for (dx, dp), value in held.items():
+            for sub, k in enumerate(group):
+                slots.append(((len(buffers), None if len(group) == 1 else sub), (dx, dp, k)))
+            buffers.append(value)
+
+    later, _ = lax.optimization_barrier((prim_blocks, arrived))
+    x_parts = [plan.to_home(later, z, k) for k in range(4)]
+
+    hbm = pl.BlockSpec(memory_space=pl.ANY)
+    smem = pl.BlockSpec(memory_space=pltpu.SMEM)
+    message = jax.ShapeDtypeStruct((2, rows, width), jnp.bfloat16)
+    wide = jax.ShapeDtypeStruct((4, 2, rows, width), jnp.float32)
+    params = pltpu.CompilerParams(vmem_limit_bytes=VMEM_BYTES)
+    n_buffers = len(buffers)
+    data_scratch = pltpu.VMEM((4, 2, 8 * rows, width), jnp.bfloat16)
+    sems = pltpu.SemaphoreType.DMA((len(slots),))
+
+    def first(*refs):
+        residual_gradient_kernel(slots, n_buffers, rows, width, *refs)
+
+    residual, *gradient = pl.pallas_call(
+        first,
+        in_specs=[smem] + [hbm] * (n_buffers + 4),
+        out_specs=[hbm] * 5,
+        out_shape=[wide] + [message] * 4,
+        scratch_shapes=[
+            data_scratch,
+            pltpu.VMEM((2 * rows, 4 * width), jnp.bfloat16),
+            pltpu.VMEM((4, 2, rows, width), jnp.bfloat16),
+            pltpu.VMEM((4, 2, rows, width), jnp.float32),
+            pltpu.VMEM((4, 2 * rows, width), jnp.bfloat16),
+            pltpu.VMEM((4, 2, rows, width), jnp.bfloat16),
+            sems,
+            pltpu.SemaphoreType.DMA((12,)),
+            pltpu.SemaphoreType.DMA((8,)),
+        ],
+        compiler_params=params,
+        name="residual_gradient",
+    )(where, *buffers, *x_parts)
+
+    returned = [plan.from_home(gradient[k], k) for k in range(4)]
+
+    def second(*refs):
+        change_kernel(slots, n_buffers, rows, width, *refs)
+
+    change, sums = pl.pallas_call(
+        second,
+        in_specs=[smem] + [hbm] * (n_buffers + 5),
+        out_specs=[hbm, smem],
+        out_shape=[wide, jax.ShapeDtypeStruct((2,), jnp.float32)],
+        scratch_shapes=[
+            data_scratch,
+            pltpu.VMEM((2 * rows, 4 * width), jnp.bfloat16),
+            pltpu.VMEM((4, 2, rows, width), jnp.bfloat16),
+            pltpu.VMEM((4, 2, rows, width), jnp.float32),
+            pltpu.VMEM((4, 2, rows, width), jnp.float32),
+            sems,
+            pltpu.SemaphoreType.DMA((12,)),
+            pltpu.SemaphoreType.DMA((4,)),
+            pltpu.SemaphoreType.DMA((4,)),
+        ],
+        compiler_params=params,
+        name="change",
+    )(where, *buffers, *gradient, residual)
+
+    sums = plan.total(sums)
+    step = -sums[0] / (sums[1] + 1e-06)
+
+    new_primaries = jnp.zeros((2, plan.cols, rows, width), jnp.bfloat16)
+    new_residual = jnp.zeros((2, plan.cols, rows, width), jnp.float32)
+    updated = [(residual[k] + step * change[k]).astype(jnp.bfloat16) for k in range(4)]
+    updated = [plan.from_home(updated[k], k) for k in range(4)]
+    for k in range(4):
+        old = lax.dynamic_index_in_dim(prim_blocks, z ^ k, 1, keepdims=False)
+        new = old.astype(jnp.float32) + step * returned[k].astype(jnp.float32)
+        new_primaries = lax.dynamic_update_index_in_dim(
+            new_primaries, new.astype(jnp.bfloat16), z ^ k, 1
+        )
+        new_residual = lax.dynamic_update_index_in_dim(
+            new_residual, updated[k].astype(jnp.float32), z ^ k, 1
+        )
+    return new_primaries.reshape(data.shape), new_residual.reshape(data.shape)
+
+
 def solution(mesh):
-    in_specs = (P(None, "freq", "row", "col"), P(None, "freq", "row", "col"))
-    out_specs = (P(None, "freq", "row", "col"), P(None, "freq", "row", "col"))
-    return jax.shard_map(local, mesh=mesh, in_specs=in_specs, out_specs=out_specs, check_vma=False)
+    rows, cols, freqs = (mesh.shape[name] for name in ("row", "col", "freq"))
+
+    def local(data, primaries):
+        if (rows, cols, freqs) == (2, 4, 4):
+            return whole_rows(Plan(rows, cols, freqs), data, primaries)
+        return blocked(data, primaries)
+
+    spec = P(None, "freq", "row", "col")
+    return jax.shard_map(
+        local, mesh=mesh, in_specs=(spec, spec), out_specs=(spec, spec), check_vma=False
+    )

time: 760 us -> 313 us (0.41)
  waiting for transfers between devices: 639 us -> 150 us
  starting transfers between devices: 0.16 us -> 97.8 us
  Pallas kernels: 0 us -> 49 us
  blocking collectives: 41.4 us -> 0 us
  matrix products: 34.2 us -> 0 us
  other arithmetic: 20.9 us -> 5.96 us
  between operations: 15.2 us -> 2.4 us
    all_gather x3 -> x0, waiting for transfers between devices: 356 us -> none  [the longest x1 149 us: gradient_step(): forward = add_block(lax.all_gather(primary_part, 'col', axis=3, tiled=True))]
    reduce_scatter x1 -> x0, waiting for transfers between devices: 281 us -> none  [gradient_step(): lax.psum_scatter(jnp.concatenate([real, imag], axis=2), 'col', scatter_di...]
    ppermute x0 -> x35, waiting for transfers between devices: none -> 150 us  [the longest x8 56.3 us: to_home(): return lax.ppermute(piece, ('col', 'freq'), self.send(k))]
    ppermute x0 -> x35, starting transfers between devices: none -> 97.8 us  [the longest x8 35.9 us: to_home(): return lax.ppermute(piece, ('col', 'freq'), self.send(k))]
    pallas_call x0 -> x2, Pallas kernels: none -> 49 us  [the longest x1 27.2 us: whole_rows(): pl.pallas_call(first, in_specs=[smem] + [hbm] * (n_buffers + 4), out_spec...]
    psum x1 -> x0, blocking collectives: 41.4 us -> none  [local(): lax.psum((inner_local, energy_local), ('row', 'col', 'freq'))]
    dot_general x12 -> x0, matrix products: 34.2 us -> none  [the longest x8 24.6 us: batched(): jnp.einsum('fik,fkj->fij', left, right, preferred_element_type=jnp.float32)]
  transfers between devices with their start and end apart: 4 -> 35, of which waited for: 4 -> 19; matrix products, arithmetic and copies ran while one was open for 0% -> 3% of each run, Pallas kernels for 0% -> 7%
where the time goes in v1:
time: 313 us; the launch traced here: 312 us
  waiting for transfers between devices  150 us (48%)
  starting transfers between devices  97.8 us (31%)
  Pallas kernels  49 us (16%)
  local copies, waits for them, and re-layouts  6.94 us (2%)
  other arithmetic  5.96 us (2%)
    ppermute x8, waiting for transfers between devices, to_home(): return lax.ppermute(piece, ('col', 'freq'), self.send(k))  56.3 us
    ppermute x8, waiting for transfers between devices, from_home(): lax.ppermute(piece, ('col', 'freq'), [(b, a) for a, b in self.send(k)])  39.9 us
    ppermute x8, starting transfers between devices, to_home(): return lax.ppermute(piece, ('col', 'freq'), self.send(k))  35.9 us
    ppermute x5, waiting for transfers between devices, over_row(): return lax.ppermute(value, 'row', [(i, i ^ 1) for i in range(self.rows)])  33.1 us
    pallas_call x1, Pallas kernels, whole_rows(): pl.pallas_call(first, in_specs=[smem] + [hbm] * (n_buffers + 4), out_spec...  27.2 us
    ppermute x8, starting transfers between devices, from_home(): lax.ppermute(piece, ('col', 'freq'), [(b, a) for a, b in self.send(k)])  21.9 us
    pallas_call x1, Pallas kernels, whole_rows(): pl.pallas_call(second, in_specs=[smem] + [hbm] * (n_buffers + 5), out_spe...  21.8 us
    ppermute x4, starting transfers between devices, over_col(): return lax.ppermute(value, 'col', [(i, i ^ by) for i in range(self.cols)])  17.4 us
  transfers between devices with their start and end apart: 35, of which 19 were waited for; matrix products, arithmetic and copies ran while one was open for 3% of the time, Pallas kernels for 7%

profile of v1, /device:TPU:20, one launch (start us, length us, event | category | flops | bytes accessed | tf_op | source)
XLA Modules:
  0.0 311.8 jit_solution(3356610077556373354)
XLA Ops:
  0.7 1.8 dynamic-slice_bitcast_fusion.5
  2.5 0.4 collective-permute-start.9
  2.9 5.2 %collective-permute-start.10 = (bf16[2,256,512]{2,1,0:T(8,128)(2,1)S(1)}, bf16[2,256,512]{2,1,0:T(8,128)(2,1)S(1)}, u32[]{:S(2)}, u32[]{:S(2)}) collective-permute-start(bf16[2,256,512]{2,1,0:T(8,128)(2,1)S(1)} %get-tuple-element.29), channel_id=1, source_target_pairs={{0,5},{1,13},{2,7},{3,15},{4,4},{5,12},{6,6},{7,14},{8,1},{9,9},{1... | collective-permute-start | bytes 1572872 | tf_op jit(solution)/shard_map/ppermute | solution.py:78
  8.1 1.9 collective-permute-start
  10.1 4.4 %collective-permute-done.9 = bf16[2,256,512]{2,1,0:T(8,128)(2,1)S(1)} collective-permute-done((bf16[2,256,512]{2,1,0:T(8,128)(2,1)S(1)}, bf16[2,256,512]{2,1,0:T(8,128)(2,1)S(1)}, u32[]{:S(2)}, u32[]{:S(2)}) %collective-permute-start.9) | collective-permute-done | bytes 524320 | tf_op jit(solution)/shard_map/ppermute | solution.py:78
  14.5 12.3 %collective-permute-done.10 = bf16[2,256,512]{2,1,0:T(8,128)(2,1)S(1)} collective-permute-done((bf16[2,256,512]{2,1,0:T(8,128)(2,1)S(1)}, bf16[2,256,512]{2,1,0:T(8,128)(2,1)S(1)}, u32[]{:S(2)}, u32[]{:S(2)}) %collective-permute-start.10) | collective-permute-done | bytes 524320 | tf_op jit(solution)/shard_map/ppermute | solution.py:78
  26.8 0.1 dynamic-slice_bitcast_fusion
  26.9 1.9 collective-permute-start.18
  28.9 0.2 collective-permute-start.19
  29.2 15.7 %collective-permute-start.11 = (bf16[2,2,256,512]{3,2,1,0:T(8,128)(2,1)S(1)}, bf16[2,2,256,512]{3,2,1,0:T(8,128)(2,1)S(1)}, u32[]{:S(2)}, u32[]{:S(2)}) collective-permute-start(bf16[2,2,256,512]{3,2,1,0:T(8,128)(2,1)S(1)} %pad_maximum_fusion.1.refs_9_), channel_id=1, source_target_pairs={{0,4},{4,0},{8,12},{12,8},{1,5},{5,1},{9,13},{13,9},{2,6},{6,2},{1... | collective-permute-start | bytes 3145736 | tf_op jit(solution)/shard_map/ppermute | solution.py:93
  44.9 15.8 %collective-permute-done.1 = bf16[2,256,512]{2,1,0:T(8,128)(2,1)S(1)} collective-permute-done((bf16[2,256,512]{2,1,0:T(8,128)(2,1)S(1)}, bf16[2,256,512]{2,1,0:T(8,128)(2,1)S(1)}, u32[]{:S(2)}, u32[]{:S(2)}) %collective-permute-start.1) | collective-permute-done | bytes 524320 | tf_op jit(solution)/shard_map/ppermute | solution.py:78
  60.9 4.9 %collective-permute-done.18.refs_17_ = bf16[2,256,512]{2,1,0:T(8,128)(2,1)S(1)} collective-permute-done((bf16[2,256,512]{2,1,0:T(8,128)(2,1)S(1)}, bf16[2,256,512]{2,1,0:T(8,128)(2,1)S(1)}, u32[]{:S(2)}, u32[]{:S(2)}) %collective-permute-start.18) | collective-permute-done | bytes 524320 | tf_op jit(solution)/shard_map/ppermute | solution.py:78
  65.8 1.5 collective-permute-start.12
  67.3 6.1 %collective-permute-done.19.refs_18_ = bf16[2,256,512]{2,1,0:T(8,128)(2,1)S(1)} collective-permute-done((bf16[2,256,512]{2,1,0:T(8,128)(2,1)S(1)}, bf16[2,256,512]{2,1,0:T(8,128)(2,1)S(1)}, u32[]{:S(2)}, u32[]{:S(2)}) %collective-permute-start.19) | collective-permute-done | bytes 524320 | tf_op jit(solution)/shard_map/ppermute | solution.py:78
  73.4 1.5 collective-permute-start.3
  74.9 2.1 collective-permute-done.20.refs_19_
  77.1 26.2 %collective-permute-start.21 = (bf16[2,256,512]{2,1,0:T(8,128)(2,1)S(1)}, bf16[2,256,512]{2,1,0:T(8,128)(2,1)}, u32[]{:S(2)}, u32[]{:S(2)}) collective-permute-start(bf16[2,256,512]{2,1,0:T(8,128)(2,1)S(1)} %get-tuple-element.22), channel_id=1, source_target_pairs={{0,5},{1,13},{2,7},{3,15},{4,4},{5,12},{6,6},{7,14},{8,1},{9,9},{1... | collective-permute-start | bytes 1572872 | tf_op jit(solution)/shard_map/ppermute | solution.py:78
  103.2 10.5 %collective-permute-done.21.refs_20_ = bf16[2,256,512]{2,1,0:T(8,128)(2,1)} collective-permute-done((bf16[2,256,512]{2,1,0:T(8,128)(2,1)S(1)}, bf16[2,256,512]{2,1,0:T(8,128)(2,1)}, u32[]{:S(2)}, u32[]{:S(2)}) %collective-permute-start.21) | collective-permute-done | bytes 524320 | tf_op jit(solution)/shard_map/ppermute | solution.py:78
  113.8 0.5 collective-permute-start.5
  114.3 3.7 %collective-permute-done.2.refs_2_ = bf16[2,2,256,512]{3,2,1,0:T(8,128)(2,1)} collective-permute-done((bf16[2,2,256,512]{3,2,1,0:T(8,128)(2,1)S(1)}, bf16[2,2,256,512]{3,2,1,0:T(8,128)(2,1)}, u32[]{:S(2)}, u32[]{:S(2)}) %collective-permute-start.2) | collective-permute-done | bytes 1048608 | tf_op jit(solution)/shard_map/ppermute | solution.py:93
  118.0 1.5 collective-permute-start.13
  119.5 0.5 collective-permute-start.4
  120.0 4.0 %collective-permute-start.15 = (bf16[2,2,256,512]{3,2,1,0:T(8,128)(2,1)S(1)}, bf16[2,2,256,512]{3,2,1,0:T(8,128)(2,1)S(1)}, u32[]{:S(2)}, u32[]{:S(2)}) collective-permute-start(bf16[2,2,256,512]{3,2,1,0:T(8,128)(2,1)S(1)} %collective-permute-done.11.refs_10_), channel_id=1, source_target_pairs={{0,1},{1,0},{2,3},{3,2},{4,5},{5,4},{6,7},{7,6},{8,9},{9,8},{10,11... | collective-permute-start | bytes 3145736 | tf_op jit(solution)/shard_map/ppermute | solution.py:87
  124.1 0.4 collective-permute-start.16
  124.5 16.0 %collective-permute-done.13.refs_12_ = bf16[2,2,256,512]{3,2,1,0:T(8,128)(2,1)} collective-permute-done((bf16[2,2,256,512]{3,2,1,0:T(8,128)(2,1)S(1)}, bf16[2,2,256,512]{3,2,1,0:T(8,128)(2,1)}, u32[]{:S(2)}, u32[]{:S(2)}) %collective-permute-start.13) | collective-permute-done | bytes 1048608 | tf_op jit(solution)/shard_map/ppermute | solution.py:84
  140.5 7.4 %collective-permute-start.7 = (bf16[2,2,256,512]{3,2,1,0:T(8,128)(2,1)}, bf16[2,2,256,512]{3,2,1,0:T(8,128)(2,1)}, u32[]{:S(2)}, u32[]{:S(2)}) collective-permute-start(bf16[2,2,256,512]{3,2,1,0:T(8,128)(2,1)} %collective-permute-done.3.refs_3_), channel_id=1, source_target_pairs={{0,1},{1,0},{2,3},{3,2},{4,5},{5,4},{6,7},{7,6},{8,9},{9,8},{10,11... | collective-permute-start | bytes 3145736 | tf_op jit(solution)/shard_map/ppermute | solution.py:87
  147.8 15.1 %collective-permute-done.4.refs_4_ = bf16[2,2,256,512]{3,2,1,0:T(8,128)(2,1)} collective-permute-done((bf16[2,2,256,512]{3,2,1,0:T(8,128)(2,1)}, bf16[2,2,256,512]{3,2,1,0:T(8,128)(2,1)}, u32[]{:S(2)}, u32[]{:S(2)}) %collective-permute-start.4) | collective-permute-done | bytes 1048608 | tf_op jit(solution)/shard_map/ppermute | solution.py:84
  162.9 3.5 %collective-permute-start.17 = (bf16[2,2,256,512]{3,2,1,0:T(8,128)(2,1)}, bf16[2,2,256,512]{3,2,1,0:T(8,128)(2,1)}, u32[]{:S(2)}, u32[]{:S(2)}) collective-permute-start(bf16[2,2,256,512]{3,2,1,0:T(8,128)(2,1)} %collective-permute-done.13.refs_12_), channel_id=1, source_target_pairs={{0,1},{1,0},{2,3},{3,2},{4,5},{5,4},{6,7},{7,6},{8,9},{9,8},{10,11... | collective-permute-start | bytes 3145736 | tf_op jit(solution)/shard_map/ppermute | solution.py:87
  166.4 1.0 copy-done.9
  167.4 0.7 pad_add_fusion.refs_0_
  168.1 0.9 collective-permute-done.17.refs_16_
  169.0 1.5 collective-permute-done.8.refs_8_
  170.5 27.2 %residual_gradient.1 = (f32[4,2,256,512]{3,2,1,0:T(8,128)}, bf16[2,256,512]{2,1,0:T(8,128)(2,1)}, bf16[2,256,512]{2,1,0:T(8,128)(2,1)}, bf16[2,256,512]{2,1,0:T(8,128)(2,1)}, bf16[2,256,512]{2,1,0:T(8,128)(2,1)}) custom-call(s32[2]{0:T(128)} %pad_add_fusion.refs_0_, bf16[2,2,256,512]{3,2,1,0:T(8,128)(2,1)} %copy-done.2, ...), custom_call_target="tpu_custom_call" | custom-call | tf_op jit(solution)/shard_map/residual_gradient/pallas_call | solution.py:274
  197.7 9.8 %collective-permute-start.27 = (bf16[2,256,512]{2,1,0:T(8,128)(2,1)}, bf16[2,256,512]{2,1,0:T(8,128)(2,1)S(1)}, u32[]{:S(2)}, u32[]{:S(2)}) collective-permute-start(bf16[2,256,512]{2,1,0:T(8,128)(2,1)} %get-tuple-element.11.refs_17_), channel_id=1, source_target_pairs={{0,0},{8,1},{2,2},{10,3},{1,4},{9,5},{3,6},{11,7},{4,8},{12,9},{6,... | collective-permute-start | bytes 1572872 | tf_op jit(solution)/shard_map/ppermute | solution.py:81
  207.7 4.9 %collective-permute-start.30 = (bf16[2,256,512]{2,1,0:T(8,128)(2,1)}, bf16[2,256,512]{2,1,0:T(8,128)(2,1)S(1)}, u32[]{:S(2)}, u32[]{:S(2)}) collective-permute-start(bf16[2,256,512]{2,1,0:T(8,128)(2,1)} %get-tuple-element.14.refs_20_), channel_id=1, source_target_pairs={{5,0},{13,1},{7,2},{15,3},{4,4},{12,5},{6,6},{14,7},{1,8},{9,9},{3... | collective-permute-start | bytes 1572872 | tf_op jit(solution)/shard_map/ppermute | solution.py:81
  212.6 21.8 %change.1 = (f32[4,2,256,512]{3,2,1,0:T(8,128)}, f32[2]{0:T(128)}) custom-call(s32[2]{0:T(128)} %pad_add_fusion.refs_0_, bf16[2,2,256,512]{3,2,1,0:T(8,128)(2,1)} %copy-done.2, bf16[2,2,256,512]{3,2,1,0:T(8,128)(2,1)} %collective-permute-done.2.refs_2_, bf16[2,2,256,512]{3,2,1,0:T(8,128)(2,1)} %collective-permute-done.3.refs_3_, ...), custom_call_target="tpu_custom_call" | custom-call | tf_op jit(solution)/shard_map/change/pallas_call | solution.py:299
  234.5 1.3 collective-permute-done.22
  235.9 0.6 add.95
  236.5 0.3 collective-permute-start.23
  236.8 4.3 %collective-permute-done.23 = f32[2]{0:T(128)S(1)} collective-permute-done((f32[2]{0:T(128)S(1)}, f32[2]{0:T(128)S(1)}, u32[]{:S(2)}, u32[]{:S(2)}) %collective-permute-start.23) | collective-permute-done | bytes 40 | tf_op jit(solution)/shard_map/ppermute | solution.py:93
  241.0 1.4 collective-permute-start.24
  242.4 5.4 %collective-permute-done.24 = f32[2]{0:T(128)S(1)} collective-permute-done((f32[2]{0:T(128)S(1)}, f32[2]{0:T(128)S(1)}, u32[]{:S(2)}, u32[]{:S(2)}) %collective-permute-start.24) | collective-permute-done | bytes 40 | tf_op jit(solution)/shard_map/ppermute | solution.py:93
  247.8 1.5 collective-permute-start.25
  249.3 2.1 collective-permute-done.25
  251.4 0.3 collective-permute-start.26
  251.6 3.3 %collective-permute-done.26 = f32[2]{0:T(128)S(1)} collective-permute-done((f32[2]{0:T(128)S(1)}, f32[2]{0:T(128)S(1)}, u32[]{:S(2)}, u32[]{:S(2)}) %collective-permute-start.26) | collective-permute-done | bytes 40 | tf_op jit(solution)/shard_map/ppermute | solution.py:90
  254.9 0.6 fusion.16
  256.8 3.3 %fusion.7 = (bf16[2,256,512]{2,1,0:T(8,128)(2,1)S(1)}, bf16[2,256,512]{2,1,0:T(8,128)(2,1)S(1)}, bf16[2,256,512]{2,1,0:T(8,128)(2,1)S(1)}, bf16[2,256,512]{2,1,0:T(8,128)(2,1)S(1)}) fusion(f32[4,2,256,512]{3,2,1,0:T(8,128)} %get-tuple-element.17, f32[4,2,256,512]{3,2,1,0:T(8,128)S(1)} %copy-done, f32[]{:T(128)} %bitcast.17), kind=kLoop, calls=%fused_computation.21 | loop fusion | flops 3145728 | bytes 10485764 | tf_op jit(solution)/shard_map/convert_element_type | solution.py:324
  260.1 2.1 collective-permute-start.31
  262.2 1.5 collective-permute-start.32
  263.7 0.2 broadcast_in_dim.44
  263.9 0.2 fusion.9
  264.1 0.2 fusion.11
  264.3 3.4 %collective-permute-start.34 = (bf16[2,256,512]{2,1,0:T(8,128)(2,1)S(1)}, bf16[2,256,512]{2,1,0:T(8,128)(2,1)S(1)}, u32[]{:S(2)}, u32[]{:S(2)}) collective-permute-start(bf16[2,256,512]{2,1,0:T(8,128)(2,1)S(1)} %get-tuple-element.18), channel_id=1, source_target_pairs={{5,0},{13,1},{7,2},{15,3},{4,4},{12,5},{6,6},{14,7},{1,8},{9,9},{3... | collective-permute-start | bytes 1572872 | tf_op jit(solution)/shard_map/ppermute | solution.py:81
  267.7 0.2 fusion.13
  267.9 0.2 copy.20
  268.2 0.2 fusion.15
  268.3 31.1 %collective-permute-done.31 = bf16[2,256,512]{2,1,0:T(8,128)(2,1)S(1)} collective-permute-done((bf16[2,256,512]{2,1,0:T(8,128)(2,1)S(1)}, bf16[2,256,512]{2,1,0:T(8,128)(2,1)S(1)}, u32[]{:S(2)}, u32[]{:S(2)}) %collective-permute-start.31) | collective-permute-done | bytes 524320 | tf_op jit(solution)/shard_map/ppermute | solution.py:81
  299.4 0.5 broadcast_in_dim.49
  300.0 0.1 convert_dynamic-update-slice_fusion.3
  300.1 8.8 %collective-permute-done.32 = bf16[2,256,512]{2,1,0:T(8,128)(2,1)S(1)} collective-permute-done((bf16[2,256,512]{2,1,0:T(8,128)(2,1)S(1)}, bf16[2,256,512]{2,1,0:T(8,128)(2,1)S(1)}, u32[]{:S(2)}, u32[]{:S(2)}) %collective-permute-start.32) | collective-permute-done | bytes 524320 | tf_op jit(solution)/shard_map/ppermute | solution.py:81
  309.0 0.1 convert_dynamic-update-slice_fusion.1
  309.1 0.4 copy.22
  309.7 2.0 copy-done.5
  (60 shorter events, 1.1 us)
Async XLA Ops:
  0.7 26.1 %copy-start.3 = (bf16[2,1,1024,512]{3,2,1,0:T(8,128)(2,1)S(1)}, bf16[2,1,1024,512]{3,2,1,0:T(8,128)(2,1)}, u32[]{:S(2)}) copy-start(bf16[2,1,1024,512]{3,2,1,0:T(8,128)(2,1)} %param.3) | copy-start | bytes 6291460
  2.5 12.0 %collective-permute-start.9 = (bf16[2,256,512]{2,1,0:T(8,128)(2,1)S(1)}, bf16[2,256,512]{2,1,0:T(8,128)(2,1)S(1)}, u32[]{:S(2)}, u32[]{:S(2)}) collective-permute-start(bf16[2,256,512]{2,1,0:T(8,128)(2,1)S(1)} %get-tuple-element.26), channel_id=1, source_target_pairs={{0,4},{1,12},{2,6},{3,14},{4,5},{5,13},{6,7},{7,15},{8,0},{9,8},{1... | collective-permute-start | bytes 1572872 | tf_op jit(solution)/shard_map/ppermute | solution.py:78
  2.9 23.9 %collective-permute-start.10 = (bf16[2,256,512]{2,1,0:T(8,128)(2,1)S(1)}, bf16[2,256,512]{2,1,0:T(8,128)(2,1)S(1)}, u32[]{:S(2)}, u32[]{:S(2)}) collective-permute-start(bf16[2,256,512]{2,1,0:T(8,128)(2,1)S(1)} %get-tuple-element.29), channel_id=1, source_target_pairs={{0,5},{1,13},{2,7},{3,15},{4,4},{5,12},{6,6},{7,14},{8,1},{9,9},{1... | collective-permute-start | bytes 1572872 | tf_op jit(solution)/shard_map/ppermute | solution.py:78
  8.1 36.7 %collective-permute-start = (bf16[2,256,512]{2,1,0:T(8,128)(2,1)S(1)}, bf16[2,256,512]{2,1,0:T(8,128)(2,1)S(1)}, u32[]{:S(2)}, u32[]{:S(2)}) collective-permute-start(bf16[2,256,512]{2,1,0:T(8,128)(2,1)S(1)} %get-tuple-element.28), channel_id=1, source_target_pairs={{0,0},{1,8},{2,2},{3,10},{4,1},{5,9},{6,3},{7,11},{8,4},{9,12},{10... | collective-permute-start | bytes 1572872 | tf_op jit(solution)/shard_map/ppermute | solution.py:78
  10.0 50.7 %collective-permute-start.1 = (bf16[2,256,512]{2,1,0:T(8,128)(2,1)S(1)}, bf16[2,256,512]{2,1,0:T(8,128)(2,1)S(1)}, u32[]{:S(2)}, u32[]{:S(2)}) collective-permute-start(bf16[2,256,512]{2,1,0:T(8,128)(2,1)S(1)} %get-tuple-element.27), channel_id=1, source_target_pairs={{0,1},{1,9},{2,3},{3,11},{4,0},{5,8},{6,2},{7,10},{8,5},{9,13},{10... | collective-permute-start | bytes 1572872 | tf_op jit(solution)/shard_map/ppermute | solution.py:78
  26.9 38.9 %collective-permute-start.18 = (bf16[2,256,512]{2,1,0:T(8,128)(2,1)S(1)}, bf16[2,256,512]{2,1,0:T(8,128)(2,1)S(1)}, u32[]{:S(2)}, u32[]{:S(2)}) collective-permute-start(bf16[2,256,512]{2,1,0:T(8,128)(2,1)S(1)} %get-tuple-element.25), channel_id=1, source_target_pairs={{0,0},{1,8},{2,2},{3,10},{4,1},{5,9},{6,3},{7,11},{8,4},{9,12},{10... | collective-permute-start | bytes 1572872 | tf_op jit(solution)/shard_map/ppermute | solution.py:78
  28.9 44.6 %collective-permute-start.19 = (bf16[2,256,512]{2,1,0:T(8,128)(2,1)S(1)}, bf16[2,256,512]{2,1,0:T(8,128)(2,1)S(1)}, u32[]{:S(2)}, u32[]{:S(2)}) collective-permute-start(bf16[2,256,512]{2,1,0:T(8,128)(2,1)S(1)} %get-tuple-element.24), channel_id=1, source_target_pairs={{0,1},{1,9},{2,3},{3,11},{4,0},{5,8},{6,2},{7,10},{8,5},{9,13},{10... | collective-permute-start | bytes 1572872 | tf_op jit(solution)/shard_map/ppermute | solution.py:78
  29.2 141.4 %copy-start.1 = (bf16[2,2,256,512]{3,2,1,0:T(8,128)(2,1)}, bf16[2,2,256,512]{3,2,1,0:T(8,128)(2,1)S(1)}, u32[]{:S(2)}) copy-start(bf16[2,2,256,512]{3,2,1,0:T(8,128)(2,1)S(1)} %pad_maximum_fusion.1.refs_9_) | copy-start | bytes 3145732
  29.2 84.6 %collective-permute-start.11 = (bf16[2,2,256,512]{3,2,1,0:T(8,128)(2,1)S(1)}, bf16[2,2,256,512]{3,2,1,0:T(8,128)(2,1)S(1)}, u32[]{:S(2)}, u32[]{:S(2)}) collective-permute-start(bf16[2,2,256,512]{3,2,1,0:T(8,128)(2,1)S(1)} %pad_maximum_fusion.1.refs_9_), channel_id=1, source_target_pairs={{0,4},{4,0},{8,12},{12,8},{1,5},{5,1},{9,13},{13,9},{2,6},{6,2},{1... | collective-permute-start | bytes 3145736 | tf_op jit(solution)/shard_map/ppermute | solution.py:93
  44.8 32.2 %collective-permute-start.20 = (bf16[2,256,512]{2,1,0:T(8,128)(2,1)S(1)}, bf16[2,256,512]{2,1,0:T(8,128)(2,1)S(1)}, u32[]{:S(2)}, u32[]{:S(2)}) collective-permute-start(bf16[2,256,512]{2,1,0:T(8,128)(2,1)S(1)} %get-tuple-element.23), channel_id=1, source_target_pairs={{0,4},{1,12},{2,6},{3,14},{4,5},{5,13},{6,7},{7,15},{8,0},{9,8},{1... | collective-permute-start | bytes 1572872 | tf_op jit(solution)/shard_map/ppermute | solution.py:78
  60.8 109.7 %copy-start.2 = (bf16[2,2,256,512]{3,2,1,0:T(8,128)(2,1)}, bf16[2,2,256,512]{3,2,1,0:T(8,128)(2,1)S(1)}, u32[]{:S(2)}) copy-start(bf16[2,2,256,512]{3,2,1,0:T(8,128)(2,1)S(1)} %pad_maximum_fusion.refs_1_) | copy-start | bytes 3145732
  60.8 57.2 %collective-permute-start.2 = (bf16[2,2,256,512]{3,2,1,0:T(8,128)(2,1)S(1)}, bf16[2,2,256,512]{3,2,1,0:T(8,128)(2,1)}, u32[]{:S(2)}, u32[]{:S(2)}) collective-permute-start(bf16[2,2,256,512]{3,2,1,0:T(8,128)(2,1)S(1)} %pad_maximum_fusion.refs_1_), channel_id=1, source_target_pairs={{0,4},{4,0},{8,12},{12,8},{1,5},{5,1},{9,13},{13,9},{2,6},{6,2},{1... | collective-permute-start | bytes 3145736 | tf_op jit(solution)/shard_map/ppermute | solution.py:93
  65.8 100.6 %copy-start.11 = (bf16[2,256,512]{2,1,0:T(8,128)(2,1)}, bf16[2,256,512]{2,1,0:T(8,128)(2,1)S(1)}, u32[]{:S(2)}) copy-start(bf16[2,256,512]{2,1,0:T(8,128)(2,1)S(1)} %collective-permute-done.18.refs_17_) | copy-start | bytes 1572868
  65.8 53.7 %collective-permute-start.12 = (bf16[2,2,256,512]{3,2,1,0:T(8,128)(2,1)S(1)}, bf16[2,2,256,512]{3,2,1,0:T(8,128)(2,1)}, u32[]{:S(2)}, u32[]{:S(2)}) collective-permute-start(bf16[2,2,256,512]{3,2,1,0:T(8,128)(2,1)S(1)} %pad_maximum_fusion.1.refs_9_), channel_id=1, source_target_pairs={{0,16},{16,0},{1,17},{17,1},{2,18},{18,2},{3,19},{19,3},{4,20},{20... | collective-permute-start | bytes 3145736 | tf_op jit(solution)/shard_map/ppermute | solution.py:84
  73.4 93.0 %copy-start.12 = (bf16[2,256,512]{2,1,0:T(8,128)(2,1)}, bf16[2,256,512]{2,1,0:T(8,128)(2,1)S(1)}, u32[]{:S(2)}) copy-start(bf16[2,256,512]{2,1,0:T(8,128)(2,1)S(1)} %collective-permute-done.19.refs_18_) | copy-start | bytes 1572868
  73.4 46.6 %collective-permute-start.3 = (bf16[2,2,256,512]{3,2,1,0:T(8,128)(2,1)S(1)}, bf16[2,2,256,512]{3,2,1,0:T(8,128)(2,1)}, u32[]{:S(2)}, u32[]{:S(2)}) collective-permute-start(bf16[2,2,256,512]{3,2,1,0:T(8,128)(2,1)S(1)} %pad_maximum_fusion.refs_1_), channel_id=1, source_target_pairs={{0,16},{16,0},{1,17},{17,1},{2,18},{18,2},{3,19},{19,3},{4,20},{20... | collective-permute-start | bytes 3145736 | tf_op jit(solution)/shard_map/ppermute | solution.py:84
  77.1 89.3 %copy-start.13 = (bf16[2,256,512]{2,1,0:T(8,128)(2,1)}, bf16[2,256,512]{2,1,0:T(8,128)(2,1)S(1)}, u32[]{:S(2)}) copy-start(bf16[2,256,512]{2,1,0:T(8,128)(2,1)S(1)} %collective-permute-done.20.refs_19_) | copy-start | bytes 1572868
  77.1 36.7 %collective-permute-start.21 = (bf16[2,256,512]{2,1,0:T(8,128)(2,1)S(1)}, bf16[2,256,512]{2,1,0:T(8,128)(2,1)}, u32[]{:S(2)}, u32[]{:S(2)}) collective-permute-start(bf16[2,256,512]{2,1,0:T(8,128)(2,1)S(1)} %get-tuple-element.22), channel_id=1, source_target_pairs={{0,5},{1,13},{2,7},{3,15},{4,4},{5,12},{6,6},{7,14},{8,1},{9,9},{1... | collective-permute-start | bytes 1572872 | tf_op jit(solution)/shard_map/ppermute | solution.py:78
  113.8 10.2 %collective-permute-start.14 = (bf16[2,2,256,512]{3,2,1,0:T(8,128)(2,1)S(1)}, bf16[2,2,256,512]{3,2,1,0:T(8,128)(2,1)S(1)}, u32[]{:S(2)}, u32[]{:S(2)}) collective-permute-start(bf16[2,2,256,512]{3,2,1,0:T(8,128)(2,1)S(1)} %pad_maximum_fusion.1.refs_9_), channel_id=1, source_target_pairs={{0,1},{1,0},{2,3},{3,2},{4,5},{5,4},{6,7},{7,6},{8,9},{9,8},{10,11... | collective-permute-start | bytes 3145736 | tf_op jit(solution)/shard_map/ppermute | solution.py:87
  113.8 56.7 %copy-start.6 = (bf16[2,2,256,512]{3,2,1,0:T(8,128)(2,1)}, bf16[2,2,256,512]{3,2,1,0:T(8,128)(2,1)S(1)}, u32[]{:S(2)}) copy-start(bf16[2,2,256,512]{3,2,1,0:T(8,128)(2,1)S(1)} %collective-permute-done.11.refs_10_) | copy-start | bytes 3145732
  113.8 10.3 %collective-permute-start.5 = (bf16[2,2,256,512]{3,2,1,0:T(8,128)(2,1)S(1)}, bf16[2,2,256,512]{3,2,1,0:T(8,128)(2,1)S(1)}, u32[]{:S(2)}, u32[]{:S(2)}) collective-permute-start(bf16[2,2,256,512]{3,2,1,0:T(8,128)(2,1)S(1)} %pad_maximum_fusion.refs_1_), channel_id=1, source_target_pairs={{0,1},{1,0},{2,3},{3,2},{4,5},{5,4},{6,7},{7,6},{8,9},{9,8},{10,11... | collective-permute-start | bytes 3145736 | tf_op jit(solution)/shard_map/ppermute | solution.py:87
  118.0 22.5 %collective-permute-start.13 = (bf16[2,2,256,512]{3,2,1,0:T(8,128)(2,1)S(1)}, bf16[2,2,256,512]{3,2,1,0:T(8,128)(2,1)}, u32[]{:S(2)}, u32[]{:S(2)}) collective-permute-start(bf16[2,2,256,512]{3,2,1,0:T(8,128)(2,1)S(1)} %collective-permute-done.11.refs_10_), channel_id=1, source_target_pairs={{0,16},{16,0},{1,17},{17,1},{2,18},{18,2},{3,19},{19,3},{4,20},{20... | collective-permute-start | bytes 3145736 | tf_op jit(solution)/shard_map/ppermute | solution.py:84
  119.5 43.5 %collective-permute-start.4 = (bf16[2,2,256,512]{3,2,1,0:T(8,128)(2,1)}, bf16[2,2,256,512]{3,2,1,0:T(8,128)(2,1)}, u32[]{:S(2)}, u32[]{:S(2)}) collective-permute-start(bf16[2,2,256,512]{3,2,1,0:T(8,128)(2,1)} %collective-permute-done.2.refs_2_), channel_id=1, source_target_pairs={{0,16},{16,0},{1,17},{17,1},{2,18},{18,2},{3,19},{19,3},{4,20},{20... | collective-permute-start | bytes 3145736 | tf_op jit(solution)/shard_map/ppermute | solution.py:84
  120.0 46.4 %collective-permute-start.15 = (bf16[2,2,256,512]{3,2,1,0:T(8,128)(2,1)S(1)}, bf16[2,2,256,512]{3,2,1,0:T(8,128)(2,1)S(1)}, u32[]{:S(2)}, u32[]{:S(2)}) collective-permute-start(bf16[2,2,256,512]{3,2,1,0:T(8,128)(2,1)S(1)} %collective-permute-done.11.refs_10_), channel_id=1, source_target_pairs={{0,1},{1,0},{2,3},{3,2},{4,5},{5,4},{6,7},{7,6},{8,9},{9,8},{10,11... | collective-permute-start | bytes 3145736 | tf_op jit(solution)/shard_map/ppermute | solution.py:87
  124.0 42.4 %copy-start.7 = (bf16[2,2,256,512]{3,2,1,0:T(8,128)(2,1)}, bf16[2,2,256,512]{3,2,1,0:T(8,128)(2,1)S(1)}, u32[]{:S(2)}) copy-start(bf16[2,2,256,512]{3,2,1,0:T(8,128)(2,1)S(1)} %collective-permute-done.14.refs_13_) | copy-start | bytes 3145732
  124.0 44.1 %collective-permute-start.6 = (bf16[2,2,256,512]{3,2,1,0:T(8,128)(2,1)}, bf16[2,2,256,512]{3,2,1,0:T(8,128)(2,1)}, u32[]{:S(2)}, u32[]{:S(2)}) collective-permute-start(bf16[2,2,256,512]{3,2,1,0:T(8,128)(2,1)} %collective-permute-done.2.refs_2_), channel_id=1, source_target_pairs={{0,1},{1,0},{2,3},{3,2},{4,5},{5,4},{6,7},{7,6},{8,9},{9,8},{10,11... | collective-permute-start | bytes 3145736 | tf_op jit(solution)/shard_map/ppermute | solution.py:87
  124.1 42.4 %copy-start.8 = (bf16[2,2,256,512]{3,2,1,0:T(8,128)(2,1)}, bf16[2,2,256,512]{3,2,1,0:T(8,128)(2,1)S(1)}, u32[]{:S(2)}) copy-start(bf16[2,2,256,512]{3,2,1,0:T(8,128)(2,1)S(1)} %collective-permute-done.5.refs_5_) | copy-start | bytes 3145732
  124.1 44.0 %collective-permute-start.16 = (bf16[2,2,256,512]{3,2,1,0:T(8,128)(2,1)}, bf16[2,2,256,512]{3,2,1,0:T(8,128)(2,1)}, u32[]{:S(2)}, u32[]{:S(2)}) collective-permute-start(bf16[2,2,256,512]{3,2,1,0:T(8,128)(2,1)} %collective-permute-done.12.refs_11_), channel_id=1, source_target_pairs={{0,1},{1,0},{2,3},{3,2},{4,5},{5,4},{6,7},{7,6},{8,9},{9,8},{10,11... | collective-permute-start | bytes 3145736 | tf_op jit(solution)/shard_map/ppermute | solution.py:87
  140.5 27.6 %collective-permute-start.7 = (bf16[2,2,256,512]{3,2,1,0:T(8,128)(2,1)}, bf16[2,2,256,512]{3,2,1,0:T(8,128)(2,1)}, u32[]{:S(2)}, u32[]{:S(2)}) collective-permute-start(bf16[2,2,256,512]{3,2,1,0:T(8,128)(2,1)} %collective-permute-done.3.refs_3_), channel_id=1, source_target_pairs={{0,1},{1,0},{2,3},{3,2},{4,5},{5,4},{6,7},{7,6},{8,9},{9,8},{10,11... | collective-permute-start | bytes 3145736 | tf_op jit(solution)/shard_map/ppermute | solution.py:87
  162.9 6.1 %collective-permute-start.17 = (bf16[2,2,256,512]{3,2,1,0:T(8,128)(2,1)}, bf16[2,2,256,512]{3,2,1,0:T(8,128)(2,1)}, u32[]{:S(2)}, u32[]{:S(2)}) collective-permute-start(bf16[2,2,256,512]{3,2,1,0:T(8,128)(2,1)} %collective-permute-done.13.refs_12_), channel_id=1, source_target_pairs={{0,1},{1,0},{2,3},{3,2},{4,5},{5,4},{6,7},{7,6},{8,9},{9,8},{10,11... | collective-permute-start | bytes 3145736 | tf_op jit(solution)/shard_map/ppermute | solution.py:87
  166.4 1.0 copy-start.9
  167.4 3.1 collective-permute-start.8
  197.7 64.5 %collective-permute-start.27 = (bf16[2,256,512]{2,1,0:T(8,128)(2,1)}, bf16[2,256,512]{2,1,0:T(8,128)(2,1)S(1)}, u32[]{:S(2)}, u32[]{:S(2)}) collective-permute-start(bf16[2,256,512]{2,1,0:T(8,128)(2,1)} %get-tuple-element.11.refs_17_), channel_id=1, source_target_pairs={{0,0},{8,1},{2,2},{10,3},{1,4},{9,5},{3,6},{11,7},{4,8},{12,9},{6,... | collective-permute-start | bytes 1572872 | tf_op jit(solution)/shard_map/ppermute | solution.py:81
  207.5 56.5 %collective-permute-start.28 = (bf16[2,256,512]{2,1,0:T(8,128)(2,1)}, bf16[2,256,512]{2,1,0:T(8,128)(2,1)S(1)}, u32[]{:S(2)}, u32[]{:S(2)}) collective-permute-start(bf16[2,256,512]{2,1,0:T(8,128)(2,1)} %get-tuple-element.12.refs_18_), channel_id=1, source_target_pairs={{1,0},{9,1},{3,2},{11,3},{0,4},{8,5},{2,6},{10,7},{5,8},{13,9},{7,... | collective-permute-start | bytes 1572872 | tf_op jit(solution)/shard_map/ppermute | solution.py:81
  207.6 56.7 %collective-permute-start.29 = (bf16[2,256,512]{2,1,0:T(8,128)(2,1)}, bf16[2,256,512]{2,1,0:T(8,128)(2,1)S(1)}, u32[]{:S(2)}, u32[]{:S(2)}) collective-permute-start(bf16[2,256,512]{2,1,0:T(8,128)(2,1)} %get-tuple-element.13.refs_19_), channel_id=1, source_target_pairs={{4,0},{12,1},{6,2},{14,3},{5,4},{13,5},{7,6},{15,7},{0,8},{8,9},{2... | collective-permute-start | bytes 1572872 | tf_op jit(solution)/shard_map/ppermute | solution.py:81
  207.7 60.4 %collective-permute-start.30 = (bf16[2,256,512]{2,1,0:T(8,128)(2,1)}, bf16[2,256,512]{2,1,0:T(8,128)(2,1)S(1)}, u32[]{:S(2)}, u32[]{:S(2)}) collective-permute-start(bf16[2,256,512]{2,1,0:T(8,128)(2,1)} %get-tuple-element.14.refs_20_), channel_id=1, source_target_pairs={{5,0},{13,1},{7,2},{15,3},{4,4},{12,5},{6,6},{14,7},{1,8},{9,9},{3... | collective-permute-start | bytes 1572872 | tf_op jit(solution)/shard_map/ppermute | solution.py:81
  212.6 44.2 %copy-start = (f32[4,2,256,512]{3,2,1,0:T(8,128)S(1)}, f32[4,2,256,512]{3,2,1,0:T(8,128)}, u32[]{:S(2)}) copy-start(f32[4,2,256,512]{3,2,1,0:T(8,128)} %get-tuple-element.15.refs_21_) | copy-start | bytes 12582916
  234.5 1.4 collective-permute-start.22
  236.5 4.6 %collective-permute-start.23 = (f32[2]{0:T(128)S(1)}, f32[2]{0:T(128)S(1)}, u32[]{:S(2)}, u32[]{:S(2)}) collective-permute-start(f32[2]{0:T(128)S(1)} %add.95), channel_id=1, source_target_pairs={{0,4},{4,0},{8,12},{12,8},{1,5},{5,1},{9,13},{13,9},{2,6},{6,2},{1... | collective-permute-start | bytes 32 | tf_op jit(solution)/shard_map/ppermute | solution.py:93
  241.0 6.8 %collective-permute-start.24 = (f32[2]{0:T(128)S(1)}, f32[2]{0:T(128)S(1)}, u32[]{:S(2)}, u32[]{:S(2)}) collective-permute-start(f32[2]{0:T(128)S(1)} %add.96), channel_id=1, source_target_pairs={{0,8},{4,12},{8,0},{12,4},{1,9},{5,13},{9,1},{13,5},{2,10},{6,14},... | collective-permute-start | bytes 32 | tf_op jit(solution)/shard_map/ppermute | solution.py:93
  247.8 3.5 %collective-permute-start.25 = (f32[2]{0:T(128)S(1)}, f32[2]{0:T(128)S(1)}, u32[]{:S(2)}, u32[]{:S(2)}) collective-permute-start(f32[2]{0:T(128)S(1)} %add.97), channel_id=1, source_target_pairs={{0,16},{16,0},{1,17},{17,1},{2,18},{18,2},{3,19},{19,3},{4,20},{20... | collective-permute-start | bytes 32 | tf_op jit(solution)/shard_map/ppermute | solution.py:84
  251.4 3.5 %collective-permute-start.26 = (f32[2]{0:T(128)S(1)}, f32[2]{0:T(128)S(1)}, u32[]{:S(2)}, u32[]{:S(2)}) collective-permute-start(f32[2]{0:T(128)S(1)} %add.98), channel_id=1, source_target_pairs={{0,2},{1,3},{2,0},{3,1},{4,6},{5,7},{6,4},{7,5},{8,10},{9,11},{10,... | collective-permute-start | bytes 32 | tf_op jit(solution)/shard_map/ppermute | solution.py:90
  260.1 3.7 %copy-start.4 = (bf16[2,1,1024,512]{3,2,1,0:T(8,128)(2,1)S(1)}, bf16[2,1,1024,512]{3,2,1,0:T(8,128)(2,1)}, u32[]{:S(2)}) copy-start(bf16[2,1,1024,512]{3,2,1,0:T(8,128)(2,1)} %param.3) | copy-start | bytes 6291460
  260.1 39.3 %collective-permute-start.31 = (bf16[2,256,512]{2,1,0:T(8,128)(2,1)S(1)}, bf16[2,256,512]{2,1,0:T(8,128)(2,1)S(1)}, u32[]{:S(2)}, u32[]{:S(2)}) collective-permute-start(bf16[2,256,512]{2,1,0:T(8,128)(2,1)S(1)} %get-tuple-element.21), channel_id=1, source_target_pairs={{0,0},{8,1},{2,2},{10,3},{1,4},{9,5},{3,6},{11,7},{4,8},{12,9},{6,... | collective-permute-start | bytes 1572872 | tf_op jit(solution)/shard_map/ppermute | solution.py:81
  262.2 46.7 %collective-permute-start.32 = (bf16[2,256,512]{2,1,0:T(8,128)(2,1)S(1)}, bf16[2,256,512]{2,1,0:T(8,128)(2,1)S(1)}, u32[]{:S(2)}, u32[]{:S(2)}) collective-permute-start(bf16[2,256,512]{2,1,0:T(8,128)(2,1)S(1)} %get-tuple-element.20), channel_id=1, source_target_pairs={{1,0},{9,1},{3,2},{11,3},{0,4},{8,5},{2,6},{10,7},{5,8},{13,9},{7,... | collective-permute-start | bytes 1572872 | tf_op jit(solution)/shard_map/ppermute | solution.py:81
  264.1 44.9 %collective-permute-start.33 = (bf16[2,256,512]{2,1,0:T(8,128)(2,1)S(1)}, bf16[2,256,512]{2,1,0:T(8,128)(2,1)S(1)}, u32[]{:S(2)}, u32[]{:S(2)}) collective-permute-start(bf16[2,256,512]{2,1,0:T(8,128)(2,1)S(1)} %get-tuple-element.19), channel_id=1, source_target_pairs={{4,0},{12,1},{6,2},{14,3},{5,4},{13,5},{7,6},{15,7},{0,8},{8,9},{2... | collective-permute-start | bytes 1572872 | tf_op jit(solution)/shard_map/ppermute | solution.py:81
  264.3 45.3 %collective-permute-start.34 = (bf16[2,256,512]{2,1,0:T(8,128)(2,1)S(1)}, bf16[2,256,512]{2,1,0:T(8,128)(2,1)S(1)}, u32[]{:S(2)}, u32[]{:S(2)}) collective-permute-start(bf16[2,256,512]{2,1,0:T(8,128)(2,1)S(1)} %get-tuple-element.18), channel_id=1, source_target_pairs={{5,0},{13,1},{7,2},{15,3},{4,4},{12,5},{6,6},{14,7},{1,8},{9,9},{3... | collective-permute-start | bytes 1572872 | tf_op jit(solution)/shard_map/ppermute | solution.py:81
  268.3 31.6 %copy-start.10 = (bf16[2,4,256,512]{3,2,1,0:T(8,128)(2,1)}, bf16[2,4,256,512]{3,2,1,0:T(8,128)(2,1)S(1)}, u32[]{:S(2)}) copy-start(bf16[2,4,256,512]{3,2,1,0:T(8,128)(2,1)S(1)} %fusion.15) | copy-start | bytes 6291460
  309.7 2.0 copy-start.5

commit v2 on v0

--- a/solution.py
+++ b/solution.py
@@ -1,7 +1,13 @@
 import jax
 import jax.numpy as jnp
+import numpy as np
 from jax import lax
+from jax.experimental import pallas as pl
+from jax.experimental.pallas import tpu as pltpu
+from jax.sharding import Mesh
 from jax.sharding import PartitionSpec as P
+
+VMEM_BYTES = 16 * 1024 * 1024
 
 
 def batched(left, right):
@@ -14,7 +20,7 @@
     return jnp.stack([real, imag])
 
 
-def gradient_step(data_part, primary_part):
+def blocked_gradient(data_part, primary_part):
     src_rows = data_part.shape[2]
     columns = lax.all_gather(data_part, "row", axis=2, tiled=True)
 
@@ -42,8 +48,8 @@
     return (residual, gradient, change)
 
 
-def local(data, primaries):
-    res, grad, chg = gradient_step(data, primaries)
+def blocked(data, primaries):
+    res, grad, chg = blocked_gradient(data, primaries)
     inner_local = jnp.sum(chg * res)
     energy_local = jnp.sum(chg * chg)
     inner, energy = lax.psum((inner_local, energy_local), ("row", "col", "freq"))
@@ -55,7 +61,293 @@
     return (updated_primaries, updated_residual)
 
 
+FINE = ("row", "half", "pair", "twin", "lane")
+HOME = ("row", "pair", "lane")
+MESSAGES = 4
+GROUPS = ((0, 1), (2, 3))
+
+
+def send_pairs(k):
+    pairs = []
+    for z in range(4):
+        for f in range(4):
+            twin, lane, part = f // 2, f % 2, z ^ k
+            pairs.append((z * 4 + f, (lane * 2 + part // 2) * 4 + twin * 2 + part % 2))
+    return pairs
+
+
+COLUMN = ("half", "pair", "twin", "lane")
+
+
+def to_home(blocks, z, k):
+    piece = lax.dynamic_index_in_dim(blocks, z ^ k, 1, keepdims=False)
+    return lax.ppermute(piece, COLUMN, send_pairs(k))
+
+
+def from_home(piece, k):
+    return lax.ppermute(piece, COLUMN, [(b, a) for a, b in send_pairs(k)])
+
+
+def total(value):
+    swap = [(0, 1), (1, 0)]
+    for axis in ("lane", "pair", "half", "row", "twin"):
+        value = value + lax.ppermute(value, axis, swap)
+    return value
+
+
+def place_copies(group, buffer, data_v, sems, rows):
+    copies = [[] for _ in range(4)]
+    number = 0
+    for device in range(8):
+        for sub, k in enumerate(group):
+            row_index, part = device // 4, device % 4
+            at = pl.ds((row_index * 2 + part % 2) * rows, rows)
+            target = data_v.at[part ^ k, :, at, :]
+            copies[part ^ k].append(
+                pltpu.make_async_copy(buffer.at[device, sub], target, sems.at[number])
+            )
+            number += 1
+    return copies
+
+
+def column_place(z):
+    return z % 2 * 2 + z // 2
+
+
+def message_copies(refs, part, wide_v, sems, rows, width):
+    copies = []
+    for k in range(4):
+        start = pl.multiple_of(column_place(part ^ k) * width, width)
+        for i in range(2):
+            target = wide_v.at[pl.ds(i * rows, rows), pl.ds(start, width)]
+            copies.append(pltpu.make_async_copy(refs[k].at[i], target, sems.at[2 * k + i]))
+    return copies
+
+
+def product(stacked, right, n, rows):
+    one = jnp.dot(stacked, right[n, 0], preferred_element_type=jnp.float32)
+    two = jnp.dot(stacked, right[n, 1], preferred_element_type=jnp.float32)
+    return one[:rows] - two[rows:], one[rows:] + two[:rows]
+
+
+def columns_of(wide_v, pair, width):
+    return wide_v[:, pair * 2 * width : (pair + 1) * 2 * width]
+
+
+def against(left, right):
+    dims = (((1,), (1,)), ((), ()))
+    return lax.dot_general(left, right, dims, preferred_element_type=jnp.float32)
+
+
+def gradient_blocks(second, part, a_v, b_v, r_v, rb_v, g_v, g_outs, sems, rows, width):
+    half = part // 2
+    if second:
+        half = 1 - half
+    at = pl.ds(pl.multiple_of(half * width, width), width)
+    for odd in range(2):
+        one = two = None
+        for n in range(4):
+            source = a_v if odd == n // 2 else b_v
+            first_dot = against(rb_v[n], source[n, 0, at, :])
+            second_dot = against(rb_v[n], source[n, 1, at, :])
+            one = first_dot if one is None else one + first_dot
+            two = second_dot if two is None else two + second_dot
+        slot = part % 2 ^ odd
+        k = slot + 2 * second
+        g_v[slot, 0] = (one[:rows] + two[rows:] - r_v[k, 0]).astype(jnp.bfloat16)
+        g_v[slot, 1] = (one[rows:] - two[:rows] - r_v[k, 1]).astype(jnp.bfloat16)
+    outs = [pltpu.make_async_copy(g_v.at[j], g_outs[j], sems.at[j]) for j in range(2)]
+    for copy in outs:
+        copy.start()
+    for copy in outs:
+        copy.wait()
+
+
+def forward_kernel(rows, width, where_ref, a_in, *refs):
+    x_refs, (a_v, wide_v, f_v, sems, x_sems) = refs[:4], refs[4:]
+    copies = place_copies(GROUPS[0], a_in, a_v, sems, rows)
+    x_copies = message_copies(x_refs, where_ref[1], wide_v, x_sems, rows, width)
+    for copy in copies[0] + x_copies + copies[1]:
+        copy.start()
+    for copy in x_copies:
+        copy.wait()
+    for n in range(4):
+        for copy in copies[n]:
+            copy.wait()
+        if n < 2:
+            for copy in copies[n + 2]:
+                copy.start()
+        forward = product(columns_of(wide_v, n // 2, width), a_v, n, rows)
+        for i in range(2):
+            f_v[n, i] = forward[i]
+
+
+def residual_kernel(rows, width, where_ref, b_in, a_v, wide_v, f_v, *refs):
+    b_v, r_v, rb_v, g0, g1, g_v, sems, out_sems = refs
+    row_index, part = where_ref[0], where_ref[1]
+    copies = place_copies(GROUPS[1], b_in, b_v, sems, rows)
+    for copy in copies[0] + copies[1]:
+        copy.start()
+    own = pl.ds(pl.multiple_of((row_index * 2 + part % 2) * rows, rows), rows)
+    for n in range(4):
+        for copy in copies[n]:
+            copy.wait()
+        if n < 2:
+            for copy in copies[n + 2]:
+                copy.start()
+        forward = product(columns_of(wide_v, 1 - n // 2, width), b_v, n, rows)
+        place = column_place(n) * width
+        for i in range(2):
+            data = jnp.where(
+                part // 2 == n // 2,
+                a_v[n, i, own, :].astype(jnp.float32),
+                b_v[n, i, own, :].astype(jnp.float32),
+            )
+            x = wide_v[i * rows : (i + 1) * rows, place : place + width].astype(jnp.float32)
+            residual = data - x + (f_v[n, i] + forward[i])
+            r_v[part ^ n, i] = residual
+            rb_v[n, i * rows : (i + 1) * rows, :] = residual.astype(jnp.bfloat16)
+    gradient_blocks(0, part, a_v, b_v, r_v, rb_v, g_v, (g0, g1), out_sems, rows, width)
+
+
+def gradient_kernel(rows, width, where_ref, a_v, b_v, r_v, rb_v, g2, g3, g_v, out_sems):
+    part = where_ref[1]
+    gradient_blocks(1, part, a_v, b_v, r_v, rb_v, g_v, (g2, g3), out_sems, rows, width)
+
+
+def change_kernel(rows, width, where_ref, a_v, b_v, r_v, *refs):
+    g_refs, (c_v, sums_out, wide_v, g_sems) = refs[:4], refs[4:]
+    part = where_ref[1]
+    g_copies = message_copies(g_refs, part, wide_v, g_sems, rows, width)
+    for copy in g_copies:
+        copy.start()
+    for copy in g_copies:
+        copy.wait()
+    inner = jnp.zeros((rows, width), jnp.float32)
+    energy = jnp.zeros((rows, width), jnp.float32)
+    for n in range(4):
+        from_a = product(columns_of(wide_v, n // 2, width), a_v, n, rows)
+        from_b = product(columns_of(wide_v, 1 - n // 2, width), b_v, n, rows)
+        place = column_place(n) * width
+        for i in range(2):
+            g = wide_v[i * rows : (i + 1) * rows, place : place + width].astype(jnp.float32)
+            change = from_a[i] + from_b[i] - g
+            c_v[part ^ n, i] = change
+            inner = inner + change * r_v[part ^ n, i]
+            energy = energy + change * change
+    sums_out[0] = jnp.sum(inner)
+    sums_out[1] = jnp.sum(energy)
+
+
+def whole_rows(data, primaries):
+    z = lax.axis_index("half") * 2 + lax.axis_index("pair")
+    part = lax.axis_index("pair") * 2 + lax.axis_index("lane")
+    n_rows, width = data.shape[2], data.shape[3]
+    rows = n_rows // MESSAGES
+    where = jnp.stack([lax.axis_index("row"), part]).astype(jnp.int32)
+    data_blocks = data.reshape(2, MESSAGES, rows, width)
+    prim_blocks = primaries.reshape(2, MESSAGES, rows, width)
+
+    arrived = [to_home(data_blocks, z, k) for k in range(MESSAGES)]
+    buffers = []
+    for group in GROUPS:
+        own = jnp.stack([arrived[k] for k in group])
+        buffers.append(lax.all_gather(own, HOME))
+    later, _ = lax.optimization_barrier((prim_blocks, arrived[1]))
+    x_parts = [to_home(later, z, k) for k in range(MESSAGES)]
+
+    hbm = pl.BlockSpec(memory_space=pl.ANY)
+    vmem = pl.BlockSpec(memory_space=pltpu.VMEM)
+    smem = pl.BlockSpec(memory_space=pltpu.SMEM)
+    message = jax.ShapeDtypeStruct((2, rows, width), jnp.bfloat16)
+    f32_blocks = pltpu.VMEM((4, 2, rows, width), jnp.float32)
+    data_half = pltpu.VMEM((4, 2, 4 * rows, width), jnp.bfloat16)
+    wide = pltpu.VMEM((2 * rows, 4 * width), jnp.bfloat16)
+    rounded = pltpu.VMEM((4, 2 * rows, width), jnp.bfloat16)
+    two_messages = pltpu.VMEM((2, 2, rows, width), jnp.bfloat16)
+    dma = pltpu.SemaphoreType.DMA
+    one_product = 8 * rows * (4 * width) * (4 * width)
+
+    def call(kernel, name, products, in_specs, out_specs, out_shape, scratch):
+        return pl.pallas_call(
+            lambda *refs: kernel(rows, width, *refs),
+            in_specs=[smem] + in_specs,
+            out_specs=out_specs,
+            out_shape=out_shape,
+            scratch_shapes=scratch,
+            compiler_params=pltpu.CompilerParams(vmem_limit_bytes=VMEM_BYTES),
+            cost_estimate=pl.CostEstimate(
+                flops=int(products * one_product), transcendentals=0, bytes_accessed=1 << 24
+            ),
+            name=name,
+        )
+
+    data_a, x_wide, partial = call(
+        forward_kernel,
+        "forward",
+        0.5,
+        [hbm] * 5,
+        [vmem] * 3,
+        [data_half, wide, f32_blocks],
+        [dma((16,)), dma((8,))],
+    )(where, buffers[0], *x_parts)
+    data_b, residual, res_rounded, g0, g1 = call(
+        residual_kernel,
+        "residual",
+        1.0,
+        [hbm] + [vmem] * 3,
+        [vmem] * 3 + [hbm] * 2,
+        [data_half, f32_blocks, rounded, message, message],
+        [two_messages, dma((16,)), dma((2,))],
+    )(where, buffers[1], data_a, x_wide, partial)
+    g2, g3 = call(
+        gradient_kernel,
+        "gradient",
+        0.5,
+        [vmem] * 4,
+        [hbm] * 2,
+        [message, message],
+        [two_messages, dma((2,))],
+    )(where, data_a, data_b, residual, res_rounded)
+    gradient = [g0, g1, g2, g3]
+    returned = [from_home(gradient[k], k) for k in range(4)]
+    change, sums = call(
+        change_kernel,
+        "change",
+        1.0,
+        [vmem] * 3 + [hbm] * 4,
+        [vmem, smem],
+        [f32_blocks, jax.ShapeDtypeStruct((2,), jnp.float32)],
+        [wide, dma((8,))],
+    )(where, data_a, data_b, residual, *gradient)
+
+    sums = total(sums)
+    step = -sums[0] / (sums[1] + 1e-06)
+
+    new_primaries = jnp.zeros((2, MESSAGES, rows, width), jnp.bfloat16)
+    new_residual = jnp.zeros((2, MESSAGES, rows, width), jnp.float32)
+    updated = [(residual[k] + step * change[k]).astype(jnp.bfloat16) for k in range(4)]
+    updated = [from_home(updated[k], k) for k in range(4)]
+    for k in range(4):
+        old = lax.dynamic_index_in_dim(prim_blocks, z ^ k, 1, keepdims=False)
+        new = old.astype(jnp.float32) + step * returned[k].astype(jnp.float32)
+        new_primaries = lax.dynamic_update_index_in_dim(
+            new_primaries, new.astype(jnp.bfloat16), z ^ k, 1
+        )
+        new_residual = lax.dynamic_update_index_in_dim(
+            new_residual, updated[k].astype(jnp.float32), z ^ k, 1
+        )
+    return new_primaries.reshape(data.shape), new_residual.reshape(data.shape)
+
+
 def solution(mesh):
-    in_specs = (P(None, "freq", "row", "col"), P(None, "freq", "row", "col"))
-    out_specs = (P(None, "freq", "row", "col"), P(None, "freq", "row", "col"))
-    return jax.shard_map(local, mesh=mesh, in_specs=in_specs, out_specs=out_specs, check_vma=False)
+    shape = tuple(mesh.shape[name] for name in ("row", "col", "freq"))
+    if shape == (2, 4, 4):
+        fine = Mesh(np.asarray(mesh.devices).reshape(2, 2, 2, 2, 2), FINE)
+        spec = P(None, ("twin", "lane"), "row", ("half", "pair"))
+        local = whole_rows
+    else:
+        fine, spec, local = mesh, P(None, "freq", "row", "col"), blocked
+    return jax.shard_map(
+        local, mesh=fine, in_specs=(spec, spec), out_specs=(spec, spec), check_vma=False
+    )

time: 760 us -> 320 us (0.42)
  waiting for transfers between devices: 639 us -> 196 us
  blocking collectives: 41.4 us -> 0 us
  starting transfers between devices: 0.16 us -> 41.3 us
  Pallas kernels: 0 us -> 34.7 us
  matrix products: 34.2 us -> 0 us
  local copies, waits for them, and re-layouts: 7.7 us -> 27.5 us
  other arithmetic: 20.9 us -> 4.62 us
    all_gather x3 -> x2, waiting for transfers between devices: 356 us -> 50.7 us  [whole_rows(): buffers.append(lax.all_gather(own, HOME))]
    reduce_scatter x1 -> x0, waiting for transfers between devices: 281 us -> none  [gradient_step(): lax.psum_scatter(jnp.concatenate([real, imag], axis=2), 'col', scatter_di...]
    ppermute x0 -> x21, waiting for transfers between devices: none -> 145 us  [the longest x8 81 us: to_home(): return lax.ppermute(piece, COLUMN, send_pairs(k))]
    psum x1 -> x0, blocking collectives: 41.4 us -> none  [local(): lax.psum((inner_local, energy_local), ('row', 'col', 'freq'))]
    ppermute x0 -> x21, starting transfers between devices: none -> 41.2 us  [the longest x8 18.8 us: to_home(): return lax.ppermute(piece, COLUMN, send_pairs(k))]
    pallas_call x0 -> x4, Pallas kernels: none -> 34.7 us  [the longest x1 11.8 us: whole_rows(): call(change_kernel, 'change', 1.0, [vmem] * 3 + [hbm] * 4, [vmem, smem],...]
    dot_general x12 -> x0, matrix products: 34.2 us -> none  [the longest x8 24.6 us: batched(): jnp.einsum('fik,fkj->fij', left, right, preferred_element_type=jnp.float32)]
    unnamed x24, local copies, waits for them, and re-layouts: 4.86 us -> 22.8 us
  transfers between devices with their start and end apart: 4 -> 23, of which waited for: 4 -> 15; matrix products, arithmetic and copies ran while one was open for 0% -> 2% of each run, Pallas kernels for 0% -> 7%
where the time goes in v2:
time: 320 us
  waiting for transfers between devices  196 us (61%)
  starting transfers between devices  41.3 us (13%)
  Pallas kernels  34.7 us (11%)
  local copies, waits for them, and re-layouts  27.5 us (9%)
  between operations  15.8 us (5%)
  other arithmetic  4.62 us (1%)
    ppermute x8, waiting for transfers between devices, to_home(): return lax.ppermute(piece, COLUMN, send_pairs(k))  81 us
    all_gather x2, waiting for transfers between devices, whole_rows(): buffers.append(lax.all_gather(own, HOME))  50.7 us
    ppermute x8, waiting for transfers between devices, from_home(): return lax.ppermute(piece, COLUMN, [(b, a) for a, b in send_pairs(k)])  38.2 us
    ppermute x5, waiting for transfers between devices, total(): value = value + lax.ppermute(value, axis, swap)  26.2 us
    unnamed x24, local copies, waits for them, and re-layouts  22.8 us
    ppermute x8, starting transfers between devices, to_home(): return lax.ppermute(piece, COLUMN, send_pairs(k))  18.8 us
    ppermute x8, starting transfers between devices, from_home(): return lax.ppermute(piece, COLUMN, [(b, a) for a, b in send_pairs(k)])  18.4 us
    pallas_call x1, Pallas kernels, whole_rows(): call(change_kernel, 'change', 1.0, [vmem] * 3 + [hbm] * 4, [vmem, smem],...  11.8 us
  transfers between devices with their start and end apart: 23, of which 15 were waited for; matrix products, arithmetic and copies ran while one was open for 2% of the time, Pallas kernels for 7%

profile of v2, /device:TPU:20, one launch (start us, length us, event | category | flops | bytes accessed | tf_op | source)
XLA Modules:
  0.0 319.9 jit_solution(11136454851653232677)
XLA Ops:
  7.2 1.7 dynamic-slice_bitcast_fusion.7
  8.9 2.4 collective-permute-start
  11.3 0.8 collective-permute-start.1
  12.1 22.7 %collective-permute-done = bf16[2,256,512]{2,1,0:T(8,128)(2,1)S(1)} collective-permute-done((bf16[2,256,512]{2,1,0:T(8,128)(2,1)S(1)}, bf16[2,256,512]{2,1,0:T(8,128)(2,1)S(1)}, u32[]{:S(2)}, u32[]{:S(2)}) %collective-permute-start) | collective-permute-done | bytes 524320 | tf_op jit(solution)/shard_map/ppermute | solution.py:84
  34.8 6.5 %collective-permute-done.1 = bf16[2,256,512]{2,1,0:T(8,128)(2,1)S(1)} collective-permute-done((bf16[2,256,512]{2,1,0:T(8,128)(2,1)S(1)}, bf16[2,256,512]{2,1,0:T(8,128)(2,1)S(1)}, u32[]{:S(2)}, u32[]{:S(2)}) %collective-permute-start.1) | collective-permute-done | bytes 524320 | tf_op jit(solution)/shard_map/ppermute | solution.py:84
  41.3 1.1 pad_maximum_fusion
  42.5 2.1 collective-permute-start.7
  44.6 10.3 %collective-permute-done.6 = bf16[2,256,512]{2,1,0:T(8,128)(2,1)S(1)} collective-permute-done((bf16[2,256,512]{2,1,0:T(8,128)(2,1)S(1)}, bf16[2,256,512]{2,1,0:T(8,128)(2,1)S(1)}, u32[]{:S(2)}, u32[]{:S(2)}) %collective-permute-start.6) | collective-permute-done | bytes 524320 | tf_op jit(solution)/shard_map/ppermute | solution.py:84
  54.9 6.5 %collective-permute-done.7 = bf16[2,256,512]{2,1,0:T(8,128)(2,1)S(1)} collective-permute-done((bf16[2,256,512]{2,1,0:T(8,128)(2,1)S(1)}, bf16[2,256,512]{2,1,0:T(8,128)(2,1)S(1)}, u32[]{:S(2)}, u32[]{:S(2)}) %collective-permute-start.7) | collective-permute-done | bytes 524320 | tf_op jit(solution)/shard_map/ppermute | solution.py:84
  61.4 1.1 pad_maximum_fusion.1
  62.5 1.2 dynamic-slice_bitcast_fusion.2
  63.7 1.9 collective-permute-start.2
  65.6 6.2 %collective-permute-start.3 = (bf16[2,256,512]{2,1,0:T(8,128)(2,1)}, bf16[2,256,512]{2,1,0:T(8,128)(2,1)S(1)}, u32[]{:S(2)}, u32[]{:S(2)}) collective-permute-start(bf16[2,256,512]{2,1,0:T(8,128)(2,1)} %get-tuple-element.34), channel_id=1, source_target_pairs={{0,1},{1,9},{2,3},{3,11},{4,0},{5,8},{6,2},{7,10},{8,5},{9,13},{10... | collective-permute-start | bytes 1572872 | tf_op jit(solution)/shard_map/ppermute | solution.py:84
  71.8 5.5 %collective-permute-start.5 = (bf16[2,256,512]{2,1,0:T(8,128)(2,1)S(1)}, bf16[2,256,512]{2,1,0:T(8,128)(2,1)S(1)}, u32[]{:S(2)}, u32[]{:S(2)}) collective-permute-start(bf16[2,256,512]{2,1,0:T(8,128)(2,1)S(1)} %get-tuple-element.32), channel_id=1, source_target_pairs={{0,5},{1,13},{2,7},{3,15},{4,4},{5,12},{6,6},{7,14},{8,1},{9,9},{1... | collective-permute-start | bytes 1572872 | tf_op jit(solution)/shard_map/ppermute | solution.py:84
  77.3 0.1 pad_add_fusion.refs_0_
  77.4 13.1 %collective-permute-done.2.refs_2_ = bf16[2,256,512]{2,1,0:T(8,128)(2,1)S(1)} collective-permute-done((bf16[2,256,512]{2,1,0:T(8,128)(2,1)}, bf16[2,256,512]{2,1,0:T(8,128)(2,1)S(1)}, u32[]{:S(2)}, u32[]{:S(2)}) %collective-permute-start.2) | collective-permute-done | bytes 524320 | tf_op jit(solution)/shard_map/ppermute | solution.py:84
  90.5 21.8 %collective-permute-done.5.refs_5_ = bf16[2,256,512]{2,1,0:T(8,128)(2,1)S(1)} collective-permute-done((bf16[2,256,512]{2,1,0:T(8,128)(2,1)S(1)}, bf16[2,256,512]{2,1,0:T(8,128)(2,1)S(1)}, u32[]{:S(2)}, u32[]{:S(2)}) %collective-permute-start.5) | collective-permute-done | bytes 524320 | tf_op jit(solution)/shard_map/ppermute | solution.py:84
  112.4 15.2 %all-gather.5.cloned.1.call-done = bf16[16,2,256,512]{3,2,1,0:T(8,128)(2,1)} async-done(((bf16[2,2,256,512]{3,2,1,0:T(8,128)(2,1)}), bf16[16,2,256,512]{3,2,1,0:T(8,128)(2,1)}) %all-gather.5.cloned.1.call-update) | async-done | bytes 8388624 | tf_op jit(solution)/shard_map/all_gather | solution.py:255
  127.6 3.4 %copy-done.2 = bf16[16,2,256,512]{3,2,1,0:T(8,128)(2,1)S(1)} copy-done((bf16[16,2,256,512]{3,2,1,0:T(8,128)(2,1)S(1)}, bf16[16,2,256,512]{3,2,1,0:T(8,128)(2,1)}, u32[]{:S(2)}) %copy-start.2) | copy-done | bytes 8388632
  131.0 6.6 %forward.1 = (bf16[4,2,1024,512]{3,2,1,0:T(8,128)(2,1)S(1)}, bf16[512,2048]{1,0:T(8,128)(2,1)S(1)}, f32[4,2,256,512]{3,2,1,0:T(8,128)S(1)}) custom-call(s32[2]{0:T(128)S(1)} %pad_add_fusion.refs_0_, bf16[8,2,2,256,512]{4,3,2,1,0:T(8,128)(2,1)S(1)} %bitcast.98, bf16[2,256,512]{2,1,0:T(8,128)(2,1)S(1)} %collective-permute-done.2.refs_2_, ...), custom_call_target="tpu_custom_call" | custom-call | flops 4294967296 | bytes 16777216 | tf_op jit(solution)/shard_map/forward/pallas_call | solution.py:285
  137.5 3.3 %copy-done = bf16[4,2,1024,512]{3,2,1,0:T(8,128)(2,1)} copy-done((bf16[4,2,1024,512]{3,2,1,0:T(8,128)(2,1)}, bf16[4,2,1024,512]{3,2,1,0:T(8,128)(2,1)S(1)}, u32[]{:S(2)}) %copy-start) | copy-done | bytes 8388632
  140.9 2.1 copy-done.4
  143.0 1.3 copy-done.6
  144.3 35.5 %all-gather.7.cloned.1.call-done = bf16[16,2,256,512]{3,2,1,0:T(8,128)(2,1)} async-done(((bf16[2,2,256,512]{3,2,1,0:T(8,128)(2,1)}), bf16[16,2,256,512]{3,2,1,0:T(8,128)(2,1)}) %all-gather.7.cloned.1.call-update) | async-done | bytes 8388624 | tf_op jit(solution)/shard_map/all_gather | solution.py:255
  179.8 3.4 %copy-done.1 = bf16[4,2,1024,512]{3,2,1,0:T(8,128)(2,1)S(1)} copy-done((bf16[4,2,1024,512]{3,2,1,0:T(8,128)(2,1)S(1)}, bf16[4,2,1024,512]{3,2,1,0:T(8,128)(2,1)}, u32[]{:S(2)}) %copy-start.1) | copy-done | bytes 8388632
  183.2 3.4 %copy-done.3 = bf16[16,2,256,512]{3,2,1,0:T(8,128)(2,1)S(1)} copy-done((bf16[16,2,256,512]{3,2,1,0:T(8,128)(2,1)S(1)}, bf16[16,2,256,512]{3,2,1,0:T(8,128)(2,1)}, u32[]{:S(2)}) %copy-start.3) | copy-done | bytes 8388632
  186.6 2.2 copy-done.5
  188.8 1.6 copy-done.7
  190.4 11.1 %residual.1 = (bf16[4,2,1024,512]{3,2,1,0:T(8,128)(2,1)S(1)}, f32[4,2,256,512]{3,2,1,0:T(8,128)S(1)}, bf16[4,512,512]{2,1,0:T(8,128)(2,1)S(1)}, bf16[2,256,512]{2,1,0:T(8,128)(2,1)S(1)}, bf16[2,256,512]{2,1,0:T(8,128)(2,1)S(1)}) custom-call(s32[2]{0:T(128)S(1)} %pad_add_fusion.refs_0_, bf16[8,2,2,256,512]{4,3,2,1,0:T(8,128)(2,1)S(1)} %bitcast.99, ...), custom_call_target="tpu_custom_call" | custom-call | flops 8589934592 | bytes 16777216 | tf_op jit(solution)/shard_map/residual/pallas_call | solution.py:294
  201.5 2.5 collective-permute-start.13
  204.0 1.9 collective-permute-start.14
  205.9 5.2 %gradient.1 = (bf16[2,256,512]{2,1,0:T(8,128)(2,1)S(1)}, bf16[2,256,512]{2,1,0:T(8,128)(2,1)S(1)}) custom-call(s32[2]{0:T(128)S(1)} %pad_add_fusion.refs_0_, bf16[4,2,1024,512]{3,2,1,0:T(8,128)(2,1)S(1)} %copy-done.1, bf16[4,2,1024,512]{3,2,1,0:T(8,128)(2,1)S(1)} %get-tuple-element.19.refs_2_, f32[4,2,256,512]{3,2,1,0:T(8,128)S(1)} %get-tuple-element.20.refs_3_, ...), custom_call_target="tpu_custom_call" | custom-call | flops 4294967296 | bytes 16777216 | tf_op jit(solution)/shard_map/gradient/pallas_call | solution.py:303
  211.1 0.1 collective-permute-start.15
  211.2 11.8 %change.1 = (f32[4,2,256,512]{3,2,1,0:T(8,128)S(1)}, f32[2]{0:T(128)S(1)}) custom-call(s32[2]{0:T(128)S(1)} %pad_add_fusion.refs_0_, bf16[4,2,1024,512]{3,2,1,0:T(8,128)(2,1)S(1)} %copy-done.1, bf16[4,2,1024,512]{3,2,1,0:T(8,128)(2,1)S(1)} %get-tuple-element.19.refs_2_, f32[4,2,256,512]{3,2,1,0:T(8,128)S(1)} %get-tuple-element.20.refs_3_, ...), custom_call_target="tpu_custom_call" | custom-call | flops 8589934592 | bytes 16777216 | tf_op jit(solution)/shard_map/change/pallas_call | solution.py:314
  222.9 3.1 collective-permute-start.16
  226.0 0.1 collective-permute-start.8
  226.1 1.1 collective-permute-done.8
  227.2 1.8 collective-permute-start.9
  229.0 11.2 %collective-permute-done.9 = f32[2]{0:T(128)S(1)} collective-permute-done((f32[2]{0:T(128)S(1)}, f32[2]{0:T(128)S(1)}, u32[]{:S(2)}, u32[]{:S(2)}) %collective-permute-start.9) | collective-permute-done | bytes 40 | tf_op jit(solution)/shard_map/ppermute | solution.py:94
  240.3 8.8 %collective-permute-done.10 = f32[2]{0:T(128)S(1)} collective-permute-done((f32[2]{0:T(128)S(1)}, f32[2]{0:T(128)S(1)}, u32[]{:S(2)}, u32[]{:S(2)}) %collective-permute-start.10) | collective-permute-done | bytes 40 | tf_op jit(solution)/shard_map/ppermute | solution.py:94
  249.1 1.5 collective-permute-start.11
  250.6 2.1 collective-permute-done.11
  252.7 0.6 collective-permute-start.12
  253.2 3.0 collective-permute-done.12
  256.2 0.6 fusion.16
  258.1 1.2 fusion.7
  259.3 2.1 collective-permute-start.17
  261.4 5.7 %collective-permute-start.18 = (bf16[2,256,512]{2,1,0:T(8,128)(2,1)S(1)}, bf16[2,256,512]{2,1,0:T(8,128)(2,1)S(1)}, u32[]{:S(2)}, u32[]{:S(2)}) collective-permute-start(bf16[2,256,512]{2,1,0:T(8,128)(2,1)S(1)} %get-tuple-element.30), channel_id=1, source_target_pairs={{1,0},{9,1},{3,2},{11,3},{0,4},{8,5},{2,6},{10,7},{5,8},{13,9},{7,... | collective-permute-start | bytes 1572872 | tf_op jit(solution)/shard_map/ppermute | solution.py:88
  267.1 0.2 broadcast_in_dim.44
  267.3 0.2 fusion.9
  267.5 0.2 fusion.11
  267.7 3.1 collective-permute-start.20
  270.8 0.2 fusion.13
  271.0 0.1 copy.24
  271.2 0.2 fusion.15
  271.4 4.5 %collective-permute-done.17 = bf16[2,256,512]{2,1,0:T(8,128)(2,1)S(1)} collective-permute-done((bf16[2,256,512]{2,1,0:T(8,128)(2,1)S(1)}, bf16[2,256,512]{2,1,0:T(8,128)(2,1)S(1)}, u32[]{:S(2)}, u32[]{:S(2)}) %collective-permute-start.17) | collective-permute-done | bytes 524320 | tf_op jit(solution)/shard_map/ppermute | solution.py:88
  275.8 0.5 broadcast_in_dim.49
  276.4 0.1 convert_dynamic-update-slice_fusion.3
  276.5 33.7 %collective-permute-done.18 = bf16[2,256,512]{2,1,0:T(8,128)(2,1)S(1)} collective-permute-done((bf16[2,256,512]{2,1,0:T(8,128)(2,1)S(1)}, bf16[2,256,512]{2,1,0:T(8,128)(2,1)S(1)}, u32[]{:S(2)}, u32[]{:S(2)}) %collective-permute-start.18) | collective-permute-done | bytes 524320 | tf_op jit(solution)/shard_map/ppermute | solution.py:88
  310.2 0.1 convert_dynamic-update-slice_fusion.2
  310.3 0.1 convert_dynamic-update-slice_fusion.1
  310.5 0.4 copy.26
  310.9 0.1 convert_dynamic-update-slice_fusion
  311.1 2.0 copy-done.10
  (36 shorter events, 0.3 us)
Async XLA Ops:
  7.2 120.4 %all-gather.5.cloned.1.call-start = ((), (), s32[]{:S(2)}) async-start(), calls=%async_computation | async-start | bytes 9437184 | tf_op jit(solution)/shard_map/all_gather | solution.py:255
  8.9 25.9 %collective-permute-start = (bf16[2,256,512]{2,1,0:T(8,128)(2,1)S(1)}, bf16[2,256,512]{2,1,0:T(8,128)(2,1)S(1)}, u32[]{:S(2)}, u32[]{:S(2)}) collective-permute-start(bf16[2,256,512]{2,1,0:T(8,128)(2,1)S(1)} %get-tuple-element.36), channel_id=1, source_target_pairs={{0,0},{1,8},{2,2},{3,10},{4,1},{5,9},{6,3},{7,11},{8,4},{9,12},{10... | collective-permute-start | bytes 1572872 | tf_op jit(solution)/shard_map/ppermute | solution.py:84
  11.3 30.0 %collective-permute-start.1 = (bf16[2,256,512]{2,1,0:T(8,128)(2,1)S(1)}, bf16[2,256,512]{2,1,0:T(8,128)(2,1)S(1)}, u32[]{:S(2)}, u32[]{:S(2)}) collective-permute-start(bf16[2,256,512]{2,1,0:T(8,128)(2,1)S(1)} %get-tuple-element.38), channel_id=1, source_target_pairs={{0,1},{1,9},{2,3},{3,11},{4,0},{5,8},{6,2},{7,10},{8,5},{9,13},{10... | collective-permute-start | bytes 1572872 | tf_op jit(solution)/shard_map/ppermute | solution.py:84
  42.4 20.1 %copy-start.8 = (bf16[2,1,1024,512]{3,2,1,0:T(8,128)(2,1)S(1)}, bf16[2,1,1024,512]{3,2,1,0:T(8,128)(2,1)}, u32[]{:S(2)}) copy-start(bf16[2,1,1024,512]{3,2,1,0:T(8,128)(2,1)} %param.3) | copy-start | bytes 6291460
  42.4 137.4 %all-gather.7.cloned.1.call-start = ((), (), s32[]{:S(2)}) async-start(), calls=%async_computation.1 | async-start | bytes 9437184 | tf_op jit(solution)/shard_map/all_gather | solution.py:255
  42.5 12.4 %collective-permute-start.6 = (bf16[2,256,512]{2,1,0:T(8,128)(2,1)S(1)}, bf16[2,256,512]{2,1,0:T(8,128)(2,1)S(1)}, u32[]{:S(2)}, u32[]{:S(2)}) collective-permute-start(bf16[2,256,512]{2,1,0:T(8,128)(2,1)S(1)} %get-tuple-element.37), channel_id=1, source_target_pairs={{0,4},{1,12},{2,6},{3,14},{4,5},{5,13},{6,7},{7,15},{8,0},{9,8},{1... | collective-permute-start | bytes 1572872 | tf_op jit(solution)/shard_map/ppermute | solution.py:84
  42.5 18.8 %collective-permute-start.7 = (bf16[2,256,512]{2,1,0:T(8,128)(2,1)S(1)}, bf16[2,256,512]{2,1,0:T(8,128)(2,1)S(1)}, u32[]{:S(2)}, u32[]{:S(2)}) collective-permute-start(bf16[2,256,512]{2,1,0:T(8,128)(2,1)S(1)} %get-tuple-element.39), channel_id=1, source_target_pairs={{0,5},{1,13},{2,7},{3,15},{4,4},{5,12},{6,6},{7,14},{8,1},{9,9},{1... | collective-permute-start | bytes 1572872 | tf_op jit(solution)/shard_map/ppermute | solution.py:84
  63.7 26.8 %collective-permute-start.2 = (bf16[2,256,512]{2,1,0:T(8,128)(2,1)}, bf16[2,256,512]{2,1,0:T(8,128)(2,1)S(1)}, u32[]{:S(2)}, u32[]{:S(2)}) collective-permute-start(bf16[2,256,512]{2,1,0:T(8,128)(2,1)} %get-tuple-element.35), channel_id=1, source_target_pairs={{0,0},{1,8},{2,2},{3,10},{4,1},{5,9},{6,3},{7,11},{8,4},{9,12},{10... | collective-permute-start | bytes 1572872 | tf_op jit(solution)/shard_map/ppermute | solution.py:84
  65.6 24.9 %collective-permute-start.3 = (bf16[2,256,512]{2,1,0:T(8,128)(2,1)}, bf16[2,256,512]{2,1,0:T(8,128)(2,1)S(1)}, u32[]{:S(2)}, u32[]{:S(2)}) collective-permute-start(bf16[2,256,512]{2,1,0:T(8,128)(2,1)} %get-tuple-element.34), channel_id=1, source_target_pairs={{0,1},{1,9},{2,3},{3,11},{4,0},{5,8},{6,2},{7,10},{8,5},{9,13},{10... | collective-permute-start | bytes 1572872 | tf_op jit(solution)/shard_map/ppermute | solution.py:84
  71.8 18.7 %collective-permute-start.4 = (bf16[2,256,512]{2,1,0:T(8,128)(2,1)}, bf16[2,256,512]{2,1,0:T(8,128)(2,1)S(1)}, u32[]{:S(2)}, u32[]{:S(2)}) collective-permute-start(bf16[2,256,512]{2,1,0:T(8,128)(2,1)} %get-tuple-element.33), channel_id=1, source_target_pairs={{0,4},{1,12},{2,6},{3,14},{4,5},{5,13},{6,7},{7,15},{8,0},{9,8},{1... | collective-permute-start | bytes 1572872 | tf_op jit(solution)/shard_map/ppermute | solution.py:84
  71.8 40.6 %collective-permute-start.5 = (bf16[2,256,512]{2,1,0:T(8,128)(2,1)S(1)}, bf16[2,256,512]{2,1,0:T(8,128)(2,1)S(1)}, u32[]{:S(2)}, u32[]{:S(2)}) collective-permute-start(bf16[2,256,512]{2,1,0:T(8,128)(2,1)S(1)} %get-tuple-element.32), channel_id=1, source_target_pairs={{0,5},{1,13},{2,7},{3,15},{4,4},{5,12},{6,6},{7,14},{8,1},{9,9},{1... | collective-permute-start | bytes 1572872 | tf_op jit(solution)/shard_map/ppermute | solution.py:84
  127.6 3.4 %copy-start.2 = (bf16[16,2,256,512]{3,2,1,0:T(8,128)(2,1)S(1)}, bf16[16,2,256,512]{3,2,1,0:T(8,128)(2,1)}, u32[]{:S(2)}) copy-start(bf16[16,2,256,512]{3,2,1,0:T(8,128)(2,1)} %all-gather.5.cloned.1.call-done) | copy-start | bytes 25165828
  137.5 3.4 %copy-start = (bf16[4,2,1024,512]{3,2,1,0:T(8,128)(2,1)}, bf16[4,2,1024,512]{3,2,1,0:T(8,128)(2,1)S(1)}, u32[]{:S(2)}) copy-start(bf16[4,2,1024,512]{3,2,1,0:T(8,128)(2,1)S(1)} %get-tuple-element.16.refs_2_.refs_1_) | copy-start | bytes 25165828
  140.9 2.1 copy-start.4
  143.0 1.3 copy-start.6
  179.8 3.4 %copy-start.1 = (bf16[4,2,1024,512]{3,2,1,0:T(8,128)(2,1)S(1)}, bf16[4,2,1024,512]{3,2,1,0:T(8,128)(2,1)}, u32[]{:S(2)}) copy-start(bf16[4,2,1024,512]{3,2,1,0:T(8,128)(2,1)} %copy-done) | copy-start | bytes 25165828
  183.2 3.4 %copy-start.3 = (bf16[16,2,256,512]{3,2,1,0:T(8,128)(2,1)S(1)}, bf16[16,2,256,512]{3,2,1,0:T(8,128)(2,1)}, u32[]{:S(2)}) copy-start(bf16[16,2,256,512]{3,2,1,0:T(8,128)(2,1)} %all-gather.7.cloned.1.call-done) | copy-start | bytes 25165828
  186.6 2.2 copy-start.5
  188.8 1.6 copy-start.7
  201.5 59.9 %collective-permute-start.13 = (bf16[2,256,512]{2,1,0:T(8,128)(2,1)S(1)}, bf16[2,256,512]{2,1,0:T(8,128)(2,1)S(1)}, u32[]{:S(2)}, u32[]{:S(2)}) collective-permute-start(bf16[2,256,512]{2,1,0:T(8,128)(2,1)S(1)} %get-tuple-element.21.refs_4_), channel_id=1, source_target_pairs={{0,0},{8,1},{2,2},{10,3},{1,4},{9,5},{3,6},{11,7},{4,8},{12,9},{6,... | collective-permute-start | bytes 1572872 | tf_op jit(solution)/shard_map/ppermute | solution.py:88
  204.0 63.5 %collective-permute-start.14 = (bf16[2,256,512]{2,1,0:T(8,128)(2,1)S(1)}, bf16[2,256,512]{2,1,0:T(8,128)(2,1)S(1)}, u32[]{:S(2)}, u32[]{:S(2)}) collective-permute-start(bf16[2,256,512]{2,1,0:T(8,128)(2,1)S(1)} %get-tuple-element.22.refs_5_), channel_id=1, source_target_pairs={{1,0},{9,1},{3,2},{11,3},{0,4},{8,5},{2,6},{10,7},{5,8},{13,9},{7,... | collective-permute-start | bytes 1572872 | tf_op jit(solution)/shard_map/ppermute | solution.py:88
  211.1 56.6 %collective-permute-start.15 = (bf16[2,256,512]{2,1,0:T(8,128)(2,1)S(1)}, bf16[2,256,512]{2,1,0:T(8,128)(2,1)S(1)}, u32[]{:S(2)}, u32[]{:S(2)}) collective-permute-start(bf16[2,256,512]{2,1,0:T(8,128)(2,1)S(1)} %get-tuple-element.24.refs_6_), channel_id=1, source_target_pairs={{4,0},{12,1},{6,2},{14,3},{5,4},{13,5},{7,6},{15,7},{0,8},{8,9},{2... | collective-permute-start | bytes 1572872 | tf_op jit(solution)/shard_map/ppermute | solution.py:88
  222.9 48.2 %collective-permute-start.16 = (bf16[2,256,512]{2,1,0:T(8,128)(2,1)S(1)}, bf16[2,256,512]{2,1,0:T(8,128)(2,1)S(1)}, u32[]{:S(2)}, u32[]{:S(2)}) collective-permute-start(bf16[2,256,512]{2,1,0:T(8,128)(2,1)S(1)} %get-tuple-element.25.refs_7_), channel_id=1, source_target_pairs={{5,0},{13,1},{7,2},{15,3},{4,4},{12,5},{6,6},{14,7},{1,8},{9,9},{3... | collective-permute-start | bytes 1572872 | tf_op jit(solution)/shard_map/ppermute | solution.py:88
  226.0 1.2 collective-permute-start.8
  227.2 13.1 %collective-permute-start.9 = (f32[2]{0:T(128)S(1)}, f32[2]{0:T(128)S(1)}, u32[]{:S(2)}, u32[]{:S(2)}) collective-permute-start(f32[2]{0:T(128)S(1)} %add.90), channel_id=1, source_target_pairs={{0,4},{4,0},{1,5},{5,1},{2,6},{6,2},{3,7},{7,3},{8,12},{12,8},{9,1... | collective-permute-start | bytes 32 | tf_op jit(solution)/shard_map/ppermute | solution.py:94
  240.3 8.8 %collective-permute-start.10 = (f32[2]{0:T(128)S(1)}, f32[2]{0:T(128)S(1)}, u32[]{:S(2)}, u32[]{:S(2)}) collective-permute-start(f32[2]{0:T(128)S(1)} %add.91), channel_id=1, source_target_pairs={{0,8},{8,0},{1,9},{9,1},{2,10},{10,2},{3,11},{11,3},{4,12},{12,4},... | collective-permute-start | bytes 32 | tf_op jit(solution)/shard_map/ppermute | solution.py:94
  249.1 3.5 %collective-permute-start.11 = (f32[2]{0:T(128)S(1)}, f32[2]{0:T(128)S(1)}, u32[]{:S(2)}, u32[]{:S(2)}) collective-permute-start(f32[2]{0:T(128)S(1)} %add.92), channel_id=1, source_target_pairs={{0,16},{16,0},{1,17},{17,1},{2,18},{18,2},{3,19},{19,3},{4,20},{20... | collective-permute-start | bytes 32 | tf_op jit(solution)/shard_map/ppermute | solution.py:94
  252.7 3.5 %collective-permute-start.12 = (f32[2]{0:T(128)S(1)}, f32[2]{0:T(128)S(1)}, u32[]{:S(2)}, u32[]{:S(2)}) collective-permute-start(f32[2]{0:T(128)S(1)} %add.93), channel_id=1, source_target_pairs={{0,2},{2,0},{1,3},{3,1},{4,6},{6,4},{5,7},{7,5},{8,10},{10,8},{9,1... | collective-permute-start | bytes 32 | tf_op jit(solution)/shard_map/ppermute | solution.py:94
  259.3 8.0 %copy-start.9 = (bf16[2,1,1024,512]{3,2,1,0:T(8,128)(2,1)S(1)}, bf16[2,1,1024,512]{3,2,1,0:T(8,128)(2,1)}, u32[]{:S(2)}) copy-start(bf16[2,1,1024,512]{3,2,1,0:T(8,128)(2,1)} %param.3) | copy-start | bytes 6291460
  259.3 16.5 %collective-permute-start.17 = (bf16[2,256,512]{2,1,0:T(8,128)(2,1)S(1)}, bf16[2,256,512]{2,1,0:T(8,128)(2,1)S(1)}, u32[]{:S(2)}, u32[]{:S(2)}) collective-permute-start(bf16[2,256,512]{2,1,0:T(8,128)(2,1)S(1)} %get-tuple-element.31), channel_id=1, source_target_pairs={{0,0},{8,1},{2,2},{10,3},{1,4},{9,5},{3,6},{11,7},{4,8},{12,9},{6,... | collective-permute-start | bytes 1572872 | tf_op jit(solution)/shard_map/ppermute | solution.py:88
  261.4 48.8 %collective-permute-start.18 = (bf16[2,256,512]{2,1,0:T(8,128)(2,1)S(1)}, bf16[2,256,512]{2,1,0:T(8,128)(2,1)S(1)}, u32[]{:S(2)}, u32[]{:S(2)}) collective-permute-start(bf16[2,256,512]{2,1,0:T(8,128)(2,1)S(1)} %get-tuple-element.30), channel_id=1, source_target_pairs={{1,0},{9,1},{3,2},{11,3},{0,4},{8,5},{2,6},{10,7},{5,8},{13,9},{7,... | collective-permute-start | bytes 1572872 | tf_op jit(solution)/shard_map/ppermute | solution.py:88
  267.5 42.8 %collective-permute-start.19 = (bf16[2,256,512]{2,1,0:T(8,128)(2,1)S(1)}, bf16[2,256,512]{2,1,0:T(8,128)(2,1)S(1)}, u32[]{:S(2)}, u32[]{:S(2)}) collective-permute-start(bf16[2,256,512]{2,1,0:T(8,128)(2,1)S(1)} %get-tuple-element.29), channel_id=1, source_target_pairs={{4,0},{12,1},{6,2},{14,3},{5,4},{13,5},{7,6},{15,7},{0,8},{8,9},{2... | collective-permute-start | bytes 1572872 | tf_op jit(solution)/shard_map/ppermute | solution.py:88
  267.7 43.2 %collective-permute-start.20 = (bf16[2,256,512]{2,1,0:T(8,128)(2,1)S(1)}, bf16[2,256,512]{2,1,0:T(8,128)(2,1)S(1)}, u32[]{:S(2)}, u32[]{:S(2)}) collective-permute-start(bf16[2,256,512]{2,1,0:T(8,128)(2,1)S(1)} %get-tuple-element.28), channel_id=1, source_target_pairs={{5,0},{13,1},{7,2},{15,3},{4,4},{12,5},{6,6},{14,7},{1,8},{9,9},{3... | collective-permute-start | bytes 1572872 | tf_op jit(solution)/shard_map/ppermute | solution.py:88
  271.4 5.0 %copy-start.11 = (bf16[2,4,256,512]{3,2,1,0:T(8,128)(2,1)}, bf16[2,4,256,512]{3,2,1,0:T(8,128)(2,1)S(1)}, u32[]{:S(2)}) copy-start(bf16[2,4,256,512]{3,2,1,0:T(8,128)(2,1)S(1)} %fusion.15) | copy-start | bytes 6291460
  311.0 2.0 copy-start.10
Sparse Core Ops, SparseCore 0:
  42.5 85.0 all-gather.4
  129.2 50.6 all-gather.6

commit v3 on v2

--- a/solution.py
+++ b/solution.py
@@ -7,7 +7,7 @@
 from jax.sharding import Mesh
 from jax.sharding import PartitionSpec as P
 
-VMEM_BYTES = 16 * 1024 * 1024
+MIB = 1024 * 1024
 
 
 def batched(left, right):
@@ -62,9 +62,9 @@
 
 
 FINE = ("row", "half", "pair", "twin", "lane")
-HOME = ("row", "pair", "lane")
 MESSAGES = 4
 GROUPS = ((0, 1), (2, 3))
+OFFSETS = tuple((dx, dp) for dx in range(2) for dp in range(4))
 
 
 def send_pairs(k):
@@ -88,39 +88,39 @@
     return lax.ppermute(piece, COLUMN, [(b, a) for a, b in send_pairs(k)])
 
 
+def swap(value, axis):
+    return lax.ppermute(value, axis, [(0, 1), (1, 0)])
+
+
 def total(value):
-    swap = [(0, 1), (1, 0)]
-    for axis in ("lane", "pair", "half", "row", "twin"):
-        value = value + lax.ppermute(value, axis, swap)
+    for axis in ("lane", "row", "twin", "pair", "half"):
+        value = value + swap(value, axis)
     return value
 
 
-def place_copies(group, buffer, data_v, sems, rows):
+def place_copies(group, buffers, where, data_v, sems, rows):
+    row_index, part = where
     copies = [[] for _ in range(4)]
-    number = 0
-    for device in range(8):
+    for number, ((dx, dp), buffer) in enumerate(zip(OFFSETS, buffers)):
+        start = ((row_index ^ dx) * 2 + (part ^ dp) % 2) * rows
+        at = pl.ds(pl.multiple_of(start, rows), rows)
         for sub, k in enumerate(group):
-            row_index, part = device // 4, device % 4
-            at = pl.ds((row_index * 2 + part % 2) * rows, rows)
-            target = data_v.at[part ^ k, :, at, :]
-            copies[part ^ k].append(
-                pltpu.make_async_copy(buffer.at[device, sub], target, sems.at[number])
+            target = data_v.at[dp ^ k, :, at, :]
+            copies[dp ^ k].append(
+                pltpu.make_async_copy(buffer.at[sub], target, sems.at[2 * number + sub])
             )
-            number += 1
     return copies
 
 
-def column_place(z):
-    return z % 2 * 2 + z // 2
-
-
-def message_copies(refs, part, wide_v, sems, rows, width):
+def message_copies(refs, part, wide_v, blocks_v, sems, rows, width):
     copies = []
     for k in range(4):
-        start = pl.multiple_of(column_place(part ^ k) * width, width)
+        z = part ^ k
+        at = pl.ds(pl.multiple_of(z // 2 * width, width), width)
         for i in range(2):
-            target = wide_v.at[pl.ds(i * rows, rows), pl.ds(start, width)]
-            copies.append(pltpu.make_async_copy(refs[k].at[i], target, sems.at[2 * k + i]))
+            target = wide_v.at[z % 2, pl.ds(i * rows, rows), at]
+            copies.append(pltpu.make_async_copy(refs[k].at[i], target, sems.at[3 * k + i]))
+        copies.append(pltpu.make_async_copy(refs[k], blocks_v.at[k], sems.at[3 * k + 2]))
     return copies
 
 
@@ -130,10 +130,6 @@
     return one[:rows] - two[rows:], one[rows:] + two[:rows]
 
 
-def columns_of(wide_v, pair, width):
-    return wide_v[:, pair * 2 * width : (pair + 1) * 2 * width]
-
-
 def against(left, right):
     dims = (((1,), (1,)), ((), ()))
     return lax.dot_general(left, right, dims, preferred_element_type=jnp.float32)
@@ -141,18 +137,16 @@
 
 def gradient_blocks(second, part, a_v, b_v, r_v, rb_v, g_v, g_outs, sems, rows, width):
     half = part // 2
-    if second:
-        half = 1 - half
-    at = pl.ds(pl.multiple_of(half * width, width), width)
+    at = pl.ds(pl.multiple_of((half ^ second) * width, width), width)
     for odd in range(2):
         one = two = None
-        for n in range(4):
-            source = a_v if odd == n // 2 else b_v
-            first_dot = against(rb_v[n], source[n, 0, at, :])
-            second_dot = against(rb_v[n], source[n, 1, at, :])
+        for t in range(4):
+            source = a_v if odd == t // 2 else b_v
+            first_dot = against(rb_v[t], source[t, 0, at, :])
+            second_dot = against(rb_v[t], source[t, 1, at, :])
             one = first_dot if one is None else one + first_dot
             two = second_dot if two is None else two + second_dot
-        slot = part % 2 ^ odd
+        slot = half ^ odd ^ part % 2
         k = slot + 2 * second
         g_v[slot, 0] = (one[:rows] + two[rows:] - r_v[k, 0]).astype(jnp.bfloat16)
         g_v[slot, 1] = (one[rows:] - two[:rows] - r_v[k, 1]).astype(jnp.bfloat16)
@@ -163,50 +157,61 @@
         copy.wait()
 
 
-def forward_kernel(rows, width, where_ref, a_in, *refs):
-    x_refs, (a_v, wide_v, f_v, sems, x_sems) = refs[:4], refs[4:]
-    copies = place_copies(GROUPS[0], a_in, a_v, sems, rows)
-    x_copies = message_copies(x_refs, where_ref[1], wide_v, x_sems, rows, width)
+def forward_kernel(rows, width, where_ref, *refs):
+    a_in, x_refs, d_refs, (f_out, wide_out) = refs[:8], refs[8:12], refs[12:16], refs[16:18]
+    a_v, wide_v, x_v, d_v, f_v, sems, x_sems, d_sems, out_sems = refs[18:]
+    part = where_ref[1]
+    copies = place_copies(GROUPS[0], a_in, (where_ref[0], part), a_v, sems, rows)
+    x_copies = message_copies(x_refs, part, wide_v, x_v, x_sems, rows, width)
+    for k in range(4):
+        x_copies.append(pltpu.make_async_copy(d_refs[k], d_v.at[k], d_sems.at[k]))
     for copy in copies[0] + x_copies + copies[1]:
         copy.start()
     for copy in x_copies:
         copy.wait()
-    for n in range(4):
-        for copy in copies[n]:
+    outs = [pltpu.make_async_copy(wide_v, wide_out, out_sems.at[4])]
+    outs[0].start()
+    for t in range(4):
+        for copy in copies[t]:
             copy.wait()
-        if n < 2:
-            for copy in copies[n + 2]:
+        if t < 2:
+            for copy in copies[t + 2]:
                 copy.start()
-        forward = product(columns_of(wide_v, n // 2, width), a_v, n, rows)
+        forward = product(wide_v[part // 2 ^ t // 2], a_v, t, rows)
         for i in range(2):
-            f_v[n, i] = forward[i]
-
-
-def residual_kernel(rows, width, where_ref, b_in, a_v, wide_v, f_v, *refs):
-    b_v, r_v, rb_v, g0, g1, g_v, sems, out_sems = refs
-    row_index, part = where_ref[0], where_ref[1]
-    copies = place_copies(GROUPS[1], b_in, b_v, sems, rows)
+            own = d_v[t, i].astype(jnp.float32) - x_v[t, i].astype(jnp.float32)
+            f_v[t, i] = own + forward[i]
+        outs.append(pltpu.make_async_copy(f_v.at[t], f_out.at[t], out_sems.at[t]))
+        outs[-1].start()
+    for copy in outs:
+        copy.wait()
+
+
+def residual_kernel(rows, width, where_ref, *refs):
+    a_in, b_in, (wide_in, f_in), refs = refs[:8], refs[8:16], refs[16:18], refs[18:]
+    a_v, b_v, r_v, rb_v, g0, g1, wide_v, f_v, g_v, a_sems, b_sems, in_sems, out_sems = refs
+    where = (where_ref[0], where_ref[1])
+    part = where[1]
+    copies = place_copies(GROUPS[1], b_in, where, b_v, b_sems, rows)
+    later = place_copies(GROUPS[0], a_in, where, a_v, a_sems, rows)
+    for t in range(4):
+        copies[t].append(pltpu.make_async_copy(f_in.at[t], f_v.at[t], in_sems.at[t]))
+    copies[0].append(pltpu.make_async_copy(wide_in, wide_v, in_sems.at[4]))
     for copy in copies[0] + copies[1]:
         copy.start()
-    own = pl.ds(pl.multiple_of((row_index * 2 + part % 2) * rows, rows), rows)
-    for n in range(4):
-        for copy in copies[n]:
+    for t in range(4):
+        for copy in copies[t]:
             copy.wait()
-        if n < 2:
-            for copy in copies[n + 2]:
-                copy.start()
-        forward = product(columns_of(wide_v, 1 - n // 2, width), b_v, n, rows)
-        place = column_place(n) * width
+        for copy in copies[t + 2] if t < 2 else later[2 * t - 4] + later[2 * t - 3]:
+            copy.start()
+        forward = product(wide_v[1 - (part // 2 ^ t // 2)], b_v, t, rows)
         for i in range(2):
-            data = jnp.where(
-                part // 2 == n // 2,
-                a_v[n, i, own, :].astype(jnp.float32),
-                b_v[n, i, own, :].astype(jnp.float32),
-            )
-            x = wide_v[i * rows : (i + 1) * rows, place : place + width].astype(jnp.float32)
-            residual = data - x + (f_v[n, i] + forward[i])
-            r_v[part ^ n, i] = residual
-            rb_v[n, i * rows : (i + 1) * rows, :] = residual.astype(jnp.bfloat16)
+            residual = f_v[t, i] + forward[i]
+            r_v[t, i] = residual
+            rb_v[t, i * rows : (i + 1) * rows, :] = residual.astype(jnp.bfloat16)
+    for t in range(4):
+        for copy in later[t]:
+            copy.wait()
     gradient_blocks(0, part, a_v, b_v, r_v, rb_v, g_v, (g0, g1), out_sems, rows, width)
 
 
@@ -216,24 +221,23 @@
 
 
 def change_kernel(rows, width, where_ref, a_v, b_v, r_v, *refs):
-    g_refs, (c_v, sums_out, wide_v, g_sems) = refs[:4], refs[4:]
+    g_refs, (c_v, sums_out, wide_v, g_v, g_sems) = refs[:4], refs[4:]
     part = where_ref[1]
-    g_copies = message_copies(g_refs, part, wide_v, g_sems, rows, width)
+    g_copies = message_copies(g_refs, part, wide_v, g_v, g_sems, rows, width)
     for copy in g_copies:
         copy.start()
     for copy in g_copies:
         copy.wait()
     inner = jnp.zeros((rows, width), jnp.float32)
     energy = jnp.zeros((rows, width), jnp.float32)
-    for n in range(4):
-        from_a = product(columns_of(wide_v, n // 2, width), a_v, n, rows)
-        from_b = product(columns_of(wide_v, 1 - n // 2, width), b_v, n, rows)
-        place = column_place(n) * width
+    for t in range(4):
+        pair = part // 2 ^ t // 2
+        from_a = product(wide_v[pair], a_v, t, rows)
+        from_b = product(wide_v[1 - pair], b_v, t, rows)
         for i in range(2):
-            g = wide_v[i * rows : (i + 1) * rows, place : place + width].astype(jnp.float32)
-            change = from_a[i] + from_b[i] - g
-            c_v[part ^ n, i] = change
-            inner = inner + change * r_v[part ^ n, i]
+            change = from_a[i] + from_b[i] - g_v[t, i].astype(jnp.float32)
+            c_v[t, i] = change
+            inner = inner + change * r_v[t, i]
             energy = energy + change * change
     sums_out[0] = jnp.sum(inner)
     sums_out[1] = jnp.sum(energy)
@@ -249,61 +253,86 @@
     prim_blocks = primaries.reshape(2, MESSAGES, rows, width)
 
     arrived = [to_home(data_blocks, z, k) for k in range(MESSAGES)]
-    buffers = []
+    buffers, by_pair = [], []
     for group in GROUPS:
         own = jnp.stack([arrived[k] for k in group])
-        buffers.append(lax.all_gather(own, HOME))
-    later, _ = lax.optimization_barrier((prim_blocks, arrived[1]))
-    x_parts = [to_home(later, z, k) for k in range(MESSAGES)]
-
-    hbm = pl.BlockSpec(memory_space=pl.ANY)
+        held = {(0, 0): own, (0, 2): swap(own, "pair")}
+        by_pair.append(held[0, 2])
+        held.update({(1, dp): swap(v, "row") for (_, dp), v in list(held.items())})
+        held.update({(dx, dp ^ 1): swap(v, "lane") for (dx, dp), v in list(held.items())})
+        buffers.append(
+            [pltpu.with_memory_space_constraint(held[at], pltpu.HBM) for at in OFFSETS]
+        )
+    x_parts = []
+    for k, ready in enumerate((arrived, by_pair[0], by_pair[1], by_pair[1])):
+        later, _ = lax.optimization_barrier((prim_blocks, ready))
+        x_parts.append(to_home(later, z, k))
+
+    hbm = pl.BlockSpec(memory_space=pltpu.HBM)
     vmem = pl.BlockSpec(memory_space=pltpu.VMEM)
     smem = pl.BlockSpec(memory_space=pltpu.SMEM)
     message = jax.ShapeDtypeStruct((2, rows, width), jnp.bfloat16)
     f32_blocks = pltpu.VMEM((4, 2, rows, width), jnp.float32)
     data_half = pltpu.VMEM((4, 2, 4 * rows, width), jnp.bfloat16)
-    wide = pltpu.VMEM((2 * rows, 4 * width), jnp.bfloat16)
+    wide = pltpu.VMEM((2, 2 * rows, 2 * width), jnp.bfloat16)
+    blocks = pltpu.VMEM((4, 2, rows, width), jnp.bfloat16)
     rounded = pltpu.VMEM((4, 2 * rows, width), jnp.bfloat16)
     two_messages = pltpu.VMEM((2, 2, rows, width), jnp.bfloat16)
     dma = pltpu.SemaphoreType.DMA
     one_product = 8 * rows * (4 * width) * (4 * width)
 
-    def call(kernel, name, products, in_specs, out_specs, out_shape, scratch):
+    def call(kernel, name, products, mib, in_specs, out_specs, out_shape, scratch):
         return pl.pallas_call(
             lambda *refs: kernel(rows, width, *refs),
             in_specs=[smem] + in_specs,
             out_specs=out_specs,
             out_shape=out_shape,
             scratch_shapes=scratch,
-            compiler_params=pltpu.CompilerParams(vmem_limit_bytes=VMEM_BYTES),
+            compiler_params=pltpu.CompilerParams(vmem_limit_bytes=mib * MIB),
             cost_estimate=pl.CostEstimate(
                 flops=int(products * one_product), transcendentals=0, bytes_accessed=1 << 24
             ),
             name=name,
         )
 
-    data_a, x_wide, partial = call(
+    partial, x_wide = call(
         forward_kernel,
         "forward",
         0.5,
-        [hbm] * 5,
-        [vmem] * 3,
-        [data_half, wide, f32_blocks],
-        [dma((16,)), dma((8,))],
-    )(where, buffers[0], *x_parts)
-    data_b, residual, res_rounded, g0, g1 = call(
+        26,
+        [hbm] * 16,
+        [hbm] * 2,
+        [
+            pltpu.HBM((4, 2, rows, width), jnp.float32),
+            pltpu.HBM((2, 2 * rows, 2 * width), jnp.bfloat16),
+        ],
+        [
+            data_half,
+            wide,
+            blocks,
+            blocks,
+            f32_blocks,
+            dma((16,)),
+            dma((12,)),
+            dma((4,)),
+            dma((5,)),
+        ],
+    )(where, *buffers[0], *x_parts, *arrived)
+    data_a, data_b, residual, res_rounded, g0, g1 = call(
         residual_kernel,
         "residual",
         1.0,
-        [hbm] + [vmem] * 3,
-        [vmem] * 3 + [hbm] * 2,
-        [data_half, f32_blocks, rounded, message, message],
-        [two_messages, dma((16,)), dma((2,))],
-    )(where, buffers[1], data_a, x_wide, partial)
+        14,
+        [hbm] * 18,
+        [vmem] * 4 + [hbm] * 2,
+        [data_half, data_half, f32_blocks, rounded, message, message],
+        [wide, f32_blocks, two_messages, dma((16,)), dma((16,)), dma((5,)), dma((2,))],
+    )(where, *buffers[0], *buffers[1], x_wide, partial)
     g2, g3 = call(
         gradient_kernel,
         "gradient",
         0.5,
+        8,
         [vmem] * 4,
         [hbm] * 2,
         [message, message],
@@ -315,10 +344,11 @@
         change_kernel,
         "change",
         1.0,
+        12,
         [vmem] * 3 + [hbm] * 4,
         [vmem, smem],
         [f32_blocks, jax.ShapeDtypeStruct((2,), jnp.float32)],
-        [wide, dma((8,))],
+        [wide, blocks, dma((12,))],
     )(where, data_a, data_b, residual, *gradient)
 
     sums = total(sums)

time: 320 us -> 276 us (0.86)
  waiting for transfers between devices: 196 us -> 169 us
  local copies, waits for them, and re-layouts: 27.5 us -> 13.5 us
  between operations: 15.8 us -> 2.45 us
  starting transfers between devices: 41.3 us -> 48.1 us
  Pallas kernels: 34.7 us -> 39.1 us
    all_gather x2 -> x0, waiting for transfers between devices: 50.7 us -> none  [whole_rows(): buffers.append(lax.all_gather(own, HOME))]
    ppermute x5 -> x19, waiting for transfers between devices: 26.2 us -> 47.8 us  [swap(): return lax.ppermute(value, axis, [(0, 1), (1, 0)])]
    unnamed x24 -> x32, local copies, waits for them, and re-layouts: 22.8 us -> 9.79 us
    ppermute x5 -> x19, starting transfers between devices: 3.94 us -> 16 us  [swap(): return lax.ppermute(value, axis, [(0, 1), (1, 0)])]
    pallas_call x4, Pallas kernels: 34.7 us -> 39.1 us  [the longest x1 13.4 us: whole_rows(): call(residual_kernel, 'residual', 1.0, 14, [hbm] * 18, [vmem] * 4 + [hbm]...]
    ppermute x8, starting transfers between devices: 18.8 us -> 15.2 us  [to_home(): return lax.ppermute(piece, COLUMN, send_pairs(k))]
  transfers between devices with their start and end apart: 23 -> 35, of which waited for: 15 -> 19; matrix products, arithmetic and copies ran while one was open for 2% -> 2% of each run, Pallas kernels for 7% -> 9%
where the time goes in v3:
time: 276 us
  waiting for transfers between devices  169 us (61%)
  starting transfers between devices  48.1 us (17%)
  Pallas kernels  39.1 us (14%)
  local copies, waits for them, and re-layouts  13.5 us (5%)
  other arithmetic  3.6 us (1%)
    ppermute x8, waiting for transfers between devices, to_home(): return lax.ppermute(piece, COLUMN, send_pairs(k))  82.1 us
    ppermute x19, waiting for transfers between devices, swap(): return lax.ppermute(value, axis, [(0, 1), (1, 0)])  47.8 us
    ppermute x8, waiting for transfers between devices, from_home(): return lax.ppermute(piece, COLUMN, [(b, a) for a, b in send_pairs(k)])  38.9 us
    ppermute x8, starting transfers between devices, from_home(): return lax.ppermute(piece, COLUMN, [(b, a) for a, b in send_pairs(k)])  16.9 us
    ppermute x19, starting transfers between devices, swap(): return lax.ppermute(value, axis, [(0, 1), (1, 0)])  16 us
    ppermute x8, starting transfers between devices, to_home(): return lax.ppermute(piece, COLUMN, send_pairs(k))  15.2 us
    pallas_call x1, Pallas kernels, whole_rows(): call(residual_kernel, 'residual', 1.0, 14, [hbm] * 18, [vmem] * 4 + [hbm]...  13.4 us
    pallas_call x1, Pallas kernels, whole_rows(): call(change_kernel, 'change', 1.0, 12, [vmem] * 3 + [hbm] * 4, [vmem, sme...  11.7 us
  transfers between devices with their start and end apart: 35, of which 19 were waited for; matrix products, arithmetic and copies ran while one was open for 2% of the time, Pallas kernels for 9%

profile of v3, /device:TPU:20, one launch (start us, length us, event | category | flops | bytes accessed | tf_op | source)
XLA Modules:
  0.0 275.7 jit_solution(5693897919538042790)
XLA Ops:
  0.7 1.7 dynamic-slice_bitcast_fusion.5
  2.3 1.9 collective-permute-start.10
  4.3 1.4 collective-permute-start.9
  5.7 3.7 %collective-permute-start = (bf16[2,256,512]{2,1,0:T(8,128)(2,1)S(1)}, bf16[2,256,512]{2,1,0:T(8,128)(2,1)S(1)}, u32[]{:S(2)}, u32[]{:S(2)}) collective-permute-start(bf16[2,256,512]{2,1,0:T(8,128)(2,1)S(1)} %get-tuple-element.40), channel_id=1, source_target_pairs={{0,0},{1,8},{2,2},{3,10},{4,1},{5,9},{6,3},{7,11},{8,4},{9,12},{10... | collective-permute-start | bytes 1572872 | tf_op jit(solution)/shard_map/ppermute | solution.py:84
  9.4 8.8 %collective-permute-done.10.refs_16_ = bf16[2,256,512]{2,1,0:T(8,128)(2,1)S(1)} collective-permute-done((bf16[2,256,512]{2,1,0:T(8,128)(2,1)S(1)}, bf16[2,256,512]{2,1,0:T(8,128)(2,1)S(1)}, u32[]{:S(2)}, u32[]{:S(2)}) %collective-permute-start.10) | collective-permute-done | bytes 524320 | tf_op jit(solution)/shard_map/ppermute | solution.py:84
  18.2 8.4 %collective-permute-done.9.refs_15_ = bf16[2,256,512]{2,1,0:T(8,128)(2,1)S(1)} collective-permute-done((bf16[2,256,512]{2,1,0:T(8,128)(2,1)S(1)}, bf16[2,256,512]{2,1,0:T(8,128)(2,1)S(1)}, u32[]{:S(2)}, u32[]{:S(2)}) %collective-permute-start.9) | collective-permute-done | bytes 524320 | tf_op jit(solution)/shard_map/ppermute | solution.py:84
  26.6 1.1 pad_maximum_fusion.1.refs_9_
  27.7 4.5 %collective-permute-start.12 = (bf16[2,2,256,512]{3,2,1,0:T(8,128)(2,1)}, bf16[2,2,256,512]{3,2,1,0:T(8,128)(2,1)}, u32[]{:S(2)}, u32[]{:S(2)}) collective-permute-start(bf16[2,2,256,512]{3,2,1,0:T(8,128)(2,1)} %pad_maximum_fusion.1.refs_9_), channel_id=1, source_target_pairs={{0,4},{4,0},{1,5},{5,1},{2,6},{6,2},{3,7},{7,3},{8,12},{12,8},{9,1... | collective-permute-start | bytes 3145736 | tf_op jit(solution)/shard_map/ppermute | solution.py:92
  32.2 12.5 %collective-permute-done.refs_13_ = bf16[2,256,512]{2,1,0:T(8,128)(2,1)S(1)} collective-permute-done((bf16[2,256,512]{2,1,0:T(8,128)(2,1)S(1)}, bf16[2,256,512]{2,1,0:T(8,128)(2,1)S(1)}, u32[]{:S(2)}, u32[]{:S(2)}) %collective-permute-start) | collective-permute-done | bytes 524320 | tf_op jit(solution)/shard_map/ppermute | solution.py:84
  44.7 8.5 %collective-permute-done.1.refs_14_ = bf16[2,256,512]{2,1,0:T(8,128)(2,1)S(1)} collective-permute-done((bf16[2,256,512]{2,1,0:T(8,128)(2,1)S(1)}, bf16[2,256,512]{2,1,0:T(8,128)(2,1)S(1)}, u32[]{:S(2)}, u32[]{:S(2)}) %collective-permute-start.1) | collective-permute-done | bytes 524320 | tf_op jit(solution)/shard_map/ppermute | solution.py:84
  53.4 1.6 collective-permute-start.5
  55.0 1.9 collective-permute-start.18
  56.9 8.6 %collective-permute-done.12.refs_11_ = bf16[2,2,256,512]{3,2,1,0:T(8,128)(2,1)} collective-permute-done((bf16[2,2,256,512]{3,2,1,0:T(8,128)(2,1)}, bf16[2,2,256,512]{3,2,1,0:T(8,128)(2,1)}, u32[]{:S(2)}, u32[]{:S(2)}) %collective-permute-start.12) | collective-permute-done | bytes 1048608 | tf_op jit(solution)/shard_map/ppermute | solution.py:92
  65.6 1.5 collective-permute-start.14
  67.1 24.2 %collective-permute-done.18.refs_9_ = bf16[2,256,512]{2,1,0:T(8,128)(2,1)S(1)} collective-permute-done((bf16[2,256,512]{2,1,0:T(8,128)(2,1)S(1)}, bf16[2,256,512]{2,1,0:T(8,128)(2,1)S(1)}, u32[]{:S(2)}, u32[]{:S(2)}) %collective-permute-start.18) | collective-permute-done | bytes 524320 | tf_op jit(solution)/shard_map/ppermute | solution.py:84
  91.4 1.6 collective-permute-start.7
  92.9 6.2 %collective-permute-start.21 = (bf16[2,256,512]{2,1,0:T(8,128)(2,1)S(1)}, bf16[2,256,512]{2,1,0:T(8,128)(2,1)S(1)}, u32[]{:S(2)}, u32[]{:S(2)}) collective-permute-start(bf16[2,256,512]{2,1,0:T(8,128)(2,1)S(1)} %get-tuple-element.36), channel_id=1, source_target_pairs={{0,5},{1,13},{2,7},{3,15},{4,4},{5,12},{6,6},{7,14},{8,1},{9,9},{1... | collective-permute-start | bytes 1572872 | tf_op jit(solution)/shard_map/ppermute | solution.py:84
  99.3 0.9 collective-permute-done.14.refs_13_
  100.2 1.0 collective-permute-done.20.refs_11_
  101.2 1.5 collective-permute-start.16
  102.7 12.3 %collective-permute-done.21.refs_12_ = bf16[2,256,512]{2,1,0:T(8,128)(2,1)S(1)} collective-permute-done((bf16[2,256,512]{2,1,0:T(8,128)(2,1)S(1)}, bf16[2,256,512]{2,1,0:T(8,128)(2,1)S(1)}, u32[]{:S(2)}, u32[]{:S(2)}) %collective-permute-start.21) | collective-permute-done | bytes 524320 | tf_op jit(solution)/shard_map/ppermute | solution.py:84
  115.0 0.8 copy-done
  115.8 6.9 %collective-permute-done.7.refs_7_ = bf16[2,2,256,512]{3,2,1,0:T(8,128)(2,1)} collective-permute-done((bf16[2,2,256,512]{3,2,1,0:T(8,128)(2,1)S(1)}, bf16[2,2,256,512]{3,2,1,0:T(8,128)(2,1)}, u32[]{:S(2)}, u32[]{:S(2)}) %collective-permute-start.7) | collective-permute-done | bytes 1048608 | tf_op jit(solution)/shard_map/ppermute | solution.py:92
  122.7 6.4 %collective-permute-done.19.refs_10_ = bf16[2,256,512]{2,1,0:T(8,128)(2,1)S(1)} collective-permute-done((bf16[2,256,512]{2,1,0:T(8,128)(2,1)S(1)}, bf16[2,256,512]{2,1,0:T(8,128)(2,1)S(1)}, u32[]{:S(2)}, u32[]{:S(2)}) %collective-permute-start.19) | collective-permute-done | bytes 524320 | tf_op jit(solution)/shard_map/ppermute | solution.py:84
  129.1 0.8 copy-done.2
  129.9 0.6 collective-permute-start.13
  130.5 0.3 copy-done.14
  130.8 12.2 %collective-permute-done.16.refs_15_ = bf16[2,2,256,512]{3,2,1,0:T(8,128)(2,1)} collective-permute-done((bf16[2,2,256,512]{3,2,1,0:T(8,128)(2,1)}, bf16[2,2,256,512]{3,2,1,0:T(8,128)(2,1)}, u32[]{:S(2)}, u32[]{:S(2)}) %collective-permute-start.16) | collective-permute-done | bytes 1048608 | tf_op jit(solution)/shard_map/ppermute | solution.py:92
  143.1 1.0 copy-done.1
  144.2 1.0 copy-done.3
  145.2 8.8 %forward.1 = (f32[4,2,256,512]{3,2,1,0:T(8,128)}, bf16[2,512,1024]{2,1,0:T(8,128)(2,1)}) custom-call(s32[2]{0:T(128)S(1)} %pad_add_fusion.refs_0_, bf16[2,2,256,512]{3,2,1,0:T(8,128)(2,1)} %copy-done.10, bf16[2,2,256,512]{3,2,1,0:T(8,128)(2,1)} %copy-done.13, bf16[2,2,256,512]{3,2,1,0:T(8,128)(2,1)} %copy-done.11, bf16[2,2,256,512]{3,2,1,0:T(8,128)(2,1)} %copy-done.14, ...), custom_call_target="tpu_custom_call" | custom-call | flops 4294967296 | bytes 16777216 | tf_op jit(solution)/shard_map/forward/pallas_call | solution.py:298
  154.1 2.2 copy-done.4
  156.3 1.6 copy-done.5
  157.8 13.4 %residual.1 = (bf16[4,2,1024,512]{3,2,1,0:T(8,128)(2,1)S(1)}, bf16[4,2,1024,512]{3,2,1,0:T(8,128)(2,1)S(1)}, f32[4,2,256,512]{3,2,1,0:T(8,128)S(1)}, bf16[4,512,...) custom-call(s32[2]{0:T(128)S(1)} %pad_add_fusion.refs_0_, ...), custom_call_target="tpu_custom_call" | custom-call | flops 8589934592 | bytes 16777216 | tf_op jit(solution)/shard_map/residual/pallas_call | solution.py:321
  171.3 1.9 collective-permute-start.27
  173.2 1.8 collective-permute-start.28
  175.0 5.2 %gradient.1 = (bf16[2,256,512]{2,1,0:T(8,128)(2,1)S(1)}, bf16[2,256,512]{2,1,0:T(8,128)(2,1)S(1)}) custom-call(s32[2]{0:T(128)S(1)} %pad_add_fusion.refs_0_, bf16[4,2,1024,512]{3,2,1,0:T(8,128)(2,1)S(1)} %get-tuple-element.22.refs_1_, bf16[4,2,1024,512]{3,2,1,0:T(8,128)(2,1)S(1)} %get-tuple-element.23.refs_2_, ...), custom_call_target="tpu_custom_call" | custom-call | flops 4294967296 | bytes 16777216 | tf_op jit(solution)/shard_map/gradient/pallas_call | solution.py:331
  180.3 11.7 %change.1 = (f32[4,2,256,512]{3,2,1,0:T(8,128)S(1)}, f32[2]{0:T(128)S(1)}) custom-call(s32[2]{0:T(128)S(1)} %pad_add_fusion.refs_0_, bf16[4,2,1024,512]{3,2,1,0:T(8,128)(2,1)S(1)} %get-tuple-element.22.refs_1_, bf16[4,2,1024,512]{3,2,1,0:T(8,128)(2,1)S(1)} %get-tuple-element.23.refs_2_, f32[4,2,256,512]{3,2,1,0:T(8,128)S(1)} %get-tuple-element.24.refs_3_, ...), custom_call_target="tpu_custom_call" | custom-call | flops 8589934592 | bytes 16777216 | tf_op jit(solution)/shard_map/change/pallas_call | solution.py:343
  192.0 3.3 %collective-permute-start.30 = (bf16[2,256,512]{2,1,0:T(8,128)(2,1)S(1)}, bf16[2,256,512]{2,1,0:T(8,128)(2,1)S(1)}, u32[]{:S(2)}, u32[]{:S(2)}) collective-permute-start(bf16[2,256,512]{2,1,0:T(8,128)(2,1)S(1)} %get-tuple-element.29.refs_7_), channel_id=1, source_target_pairs={{5,0},{13,1},{7,2},{15,3},{4,4},{12,5},{6,6},{14,7},{1,8},{9,9},{3... | collective-permute-start | bytes 1572872 | tf_op jit(solution)/shard_map/ppermute | solution.py:88
  195.4 1.1 collective-permute-done.22
  196.5 1.5 collective-permute-start.23
  198.0 2.0 collective-permute-done.23
  200.0 0.4 collective-permute-start.24
  200.5 3.1 %collective-permute-done.24 = f32[2]{0:T(128)S(1)} collective-permute-done((f32[2]{0:T(128)S(1)}, f32[2]{0:T(128)S(1)}, u32[]{:S(2)}, u32[]{:S(2)}) %collective-permute-start.24) | collective-permute-done | bytes 40 | tf_op jit(solution)/shard_map/ppermute | solution.py:92
  203.6 2.6 collective-permute-start.25
  206.1 4.2 %collective-permute-done.25 = f32[2]{0:T(128)S(1)} collective-permute-done((f32[2]{0:T(128)S(1)}, f32[2]{0:T(128)S(1)}, u32[]{:S(2)}, u32[]{:S(2)}) %collective-permute-start.25) | collective-permute-done | bytes 40 | tf_op jit(solution)/shard_map/ppermute | solution.py:92
  210.3 8.8 %collective-permute-done.26 = f32[2]{0:T(128)S(1)} collective-permute-done((f32[2]{0:T(128)S(1)}, f32[2]{0:T(128)S(1)}, u32[]{:S(2)}, u32[]{:S(2)}) %collective-permute-start.26) | collective-permute-done | bytes 40 | tf_op jit(solution)/shard_map/ppermute | solution.py:92
  219.1 0.6 fusion.16
  221.0 1.2 fusion.7
  222.2 4.7 %collective-permute-start.31 = (bf16[2,256,512]{2,1,0:T(8,128)(2,1)S(1)}, bf16[2,256,512]{2,1,0:T(8,128)(2,1)S(1)}, u32[]{:S(2)}, u32[]{:S(2)}) collective-permute-start(bf16[2,256,512]{2,1,0:T(8,128)(2,1)S(1)} %get-tuple-element.35), channel_id=1, source_target_pairs={{0,0},{8,1},{2,2},{10,3},{1,4},{9,5},{3,6},{11,7},{4,8},{12,9},{6,... | collective-permute-start | bytes 1572872 | tf_op jit(solution)/shard_map/ppermute | solution.py:88
  226.9 2.0 collective-permute-start.32
  228.9 0.2 broadcast_in_dim.44
  229.1 0.2 fusion.9
  229.3 0.2 fusion.11
  229.5 3.1 %collective-permute-start.34 = (bf16[2,256,512]{2,1,0:T(8,128)(2,1)S(1)}, bf16[2,256,512]{2,1,0:T(8,128)(2,1)S(1)}, u32[]{:S(2)}, u32[]{:S(2)}) collective-permute-start(bf16[2,256,512]{2,1,0:T(8,128)(2,1)S(1)} %get-tuple-element.32), channel_id=1, source_target_pairs={{5,0},{13,1},{7,2},{15,3},{4,4},{12,5},{6,6},{14,7},{1,8},{9,9},{3... | collective-permute-start | bytes 1572872 | tf_op jit(solution)/shard_map/ppermute | solution.py:88
  232.6 0.2 fusion.13
  232.8 0.2 copy.20
  233.0 0.2 fusion.15
  233.2 28.6 %collective-permute-done.31 = bf16[2,256,512]{2,1,0:T(8,128)(2,1)S(1)} collective-permute-done((bf16[2,256,512]{2,1,0:T(8,128)(2,1)S(1)}, bf16[2,256,512]{2,1,0:T(8,128)(2,1)S(1)}, u32[]{:S(2)}, u32[]{:S(2)}) %collective-permute-start.31) | collective-permute-done | bytes 524320 | tf_op jit(solution)/shard_map/ppermute | solution.py:88
  261.8 0.5 broadcast_in_dim.49
  262.5 10.3 %collective-permute-done.32 = bf16[2,256,512]{2,1,0:T(8,128)(2,1)S(1)} collective-permute-done((bf16[2,256,512]{2,1,0:T(8,128)(2,1)S(1)}, bf16[2,256,512]{2,1,0:T(8,128)(2,1)S(1)}, u32[]{:S(2)}, u32[]{:S(2)}) %collective-permute-start.32) | collective-permute-done | bytes 524320 | tf_op jit(solution)/shard_map/ppermute | solution.py:88
  272.9 0.1 convert_dynamic-update-slice_fusion.1
  273.1 0.4 copy.22
  273.7 2.0 copy-done.8
  (68 shorter events, 1.3 us)
Async XLA Ops:
  2.3 15.9 %collective-permute-start.10 = (bf16[2,256,512]{2,1,0:T(8,128)(2,1)S(1)}, bf16[2,256,512]{2,1,0:T(8,128)(2,1)S(1)}, u32[]{:S(2)}, u32[]{:S(2)}) collective-permute-start(bf16[2,256,512]{2,1,0:T(8,128)(2,1)S(1)} %get-tuple-element.41), channel_id=1, source_target_pairs={{0,5},{1,13},{2,7},{3,15},{4,4},{5,12},{6,6},{7,14},{8,1},{9,9},{1... | collective-permute-start | bytes 1572872 | tf_op jit(solution)/shard_map/ppermute | solution.py:84
  4.3 22.3 %collective-permute-start.9 = (bf16[2,256,512]{2,1,0:T(8,128)(2,1)S(1)}, bf16[2,256,512]{2,1,0:T(8,128)(2,1)S(1)}, u32[]{:S(2)}, u32[]{:S(2)}) collective-permute-start(bf16[2,256,512]{2,1,0:T(8,128)(2,1)S(1)} %get-tuple-element.38), channel_id=1, source_target_pairs={{0,4},{1,12},{2,6},{3,14},{4,5},{5,13},{6,7},{7,15},{8,0},{9,8},{1... | collective-permute-start | bytes 1572872 | tf_op jit(solution)/shard_map/ppermute | solution.py:84
  5.7 39.0 %collective-permute-start = (bf16[2,256,512]{2,1,0:T(8,128)(2,1)S(1)}, bf16[2,256,512]{2,1,0:T(8,128)(2,1)S(1)}, u32[]{:S(2)}, u32[]{:S(2)}) collective-permute-start(bf16[2,256,512]{2,1,0:T(8,128)(2,1)S(1)} %get-tuple-element.40), channel_id=1, source_target_pairs={{0,0},{1,8},{2,2},{3,10},{4,1},{5,9},{6,3},{7,11},{8,4},{9,12},{10... | collective-permute-start | bytes 1572872 | tf_op jit(solution)/shard_map/ppermute | solution.py:84
  9.4 43.8 %collective-permute-start.1 = (bf16[2,256,512]{2,1,0:T(8,128)(2,1)S(1)}, bf16[2,256,512]{2,1,0:T(8,128)(2,1)S(1)}, u32[]{:S(2)}, u32[]{:S(2)}) collective-permute-start(bf16[2,256,512]{2,1,0:T(8,128)(2,1)S(1)} %get-tuple-element.39), channel_id=1, source_target_pairs={{0,1},{1,9},{2,3},{3,11},{4,0},{5,8},{6,2},{7,10},{8,5},{9,13},{10... | collective-permute-start | bytes 1572872 | tf_op jit(solution)/shard_map/ppermute | solution.py:84
  26.6 28.4 %copy-start.6 = (bf16[2,1,1024,512]{3,2,1,0:T(8,128)(2,1)S(1)}, bf16[2,1,1024,512]{3,2,1,0:T(8,128)(2,1)}, u32[]{:S(2)}) copy-start(bf16[2,1,1024,512]{3,2,1,0:T(8,128)(2,1)} %param.3) | copy-start | bytes 6291460
  27.7 37.9 %collective-permute-start.12 = (bf16[2,2,256,512]{3,2,1,0:T(8,128)(2,1)}, bf16[2,2,256,512]{3,2,1,0:T(8,128)(2,1)}, u32[]{:S(2)}, u32[]{:S(2)}) collective-permute-start(bf16[2,2,256,512]{3,2,1,0:T(8,128)(2,1)} %pad_maximum_fusion.1.refs_9_), channel_id=1, source_target_pairs={{0,4},{4,0},{1,5},{5,1},{2,6},{6,2},{3,7},{7,3},{8,12},{12,8},{9,1... | collective-permute-start | bytes 3145736 | tf_op jit(solution)/shard_map/ppermute | solution.py:92
  53.3 49.4 %copy-start.10 = (bf16[2,2,256,512]{3,2,1,0:T(8,128)(2,1)}, bf16[2,2,256,512]{3,2,1,0:T(8,128)(2,1)S(1)}, u32[]{:S(2)}) copy-start(bf16[2,2,256,512]{3,2,1,0:T(8,128)(2,1)S(1)} %pad_maximum_fusion.refs_1_) | copy-start | bytes 3145732
  53.3 38.1 %collective-permute-start.3 = (bf16[2,2,256,512]{3,2,1,0:T(8,128)(2,1)S(1)}, bf16[2,2,256,512]{3,2,1,0:T(8,128)(2,1)S(1)}, u32[]{:S(2)}, u32[]{:S(2)}) collective-permute-start(bf16[2,2,256,512]{3,2,1,0:T(8,128)(2,1)S(1)} %pad_maximum_fusion.refs_1_), channel_id=1, source_target_pairs={{0,4},{4,0},{1,5},{5,1},{2,6},{6,2},{3,7},{7,3},{8,12},{12,8},{9,1... | collective-permute-start | bytes 3145736 | tf_op jit(solution)/shard_map/ppermute | solution.py:92
  53.4 39.5 %collective-permute-start.5 = (bf16[2,2,256,512]{3,2,1,0:T(8,128)(2,1)S(1)}, bf16[2,2,256,512]{3,2,1,0:T(8,128)(2,1)S(1)}, u32[]{:S(2)}, u32[]{:S(2)}) collective-permute-start(bf16[2,2,256,512]{3,2,1,0:T(8,128)(2,1)S(1)} %pad_maximum_fusion.refs_1_), channel_id=1, source_target_pairs={{0,16},{16,0},{1,17},{17,1},{2,18},{18,2},{3,19},{19,3},{4,20},{20... | collective-permute-start | bytes 3145736 | tf_op jit(solution)/shard_map/ppermute | solution.py:92
  55.0 44.2 %collective-permute-start.2 = (bf16[2,2,256,512]{3,2,1,0:T(8,128)(2,1)S(1)}, bf16[2,2,256,512]{3,2,1,0:T(8,128)(2,1)S(1)}, u32[]{:S(2)}, u32[]{:S(2)}) collective-permute-start(bf16[2,2,256,512]{3,2,1,0:T(8,128)(2,1)S(1)} %pad_maximum_fusion.refs_1_), channel_id=1, source_target_pairs={{0,1},{1,0},{2,3},{3,2},{4,5},{5,4},{6,7},{7,6},{8,9},{9,8},{10,11... | collective-permute-start | bytes 3145736 | tf_op jit(solution)/shard_map/ppermute | solution.py:92
  55.0 36.4 %collective-permute-start.18 = (bf16[2,256,512]{2,1,0:T(8,128)(2,1)S(1)}, bf16[2,256,512]{2,1,0:T(8,128)(2,1)S(1)}, u32[]{:S(2)}, u32[]{:S(2)}) collective-permute-start(bf16[2,256,512]{2,1,0:T(8,128)(2,1)S(1)} %dynamic-slice_bitcast_fusion.3), channel_id=1, source_target_pairs={{0,0},{1,8},{2,2},{3,10},{4,1},{5,9},{6,3},{7,11},{8,4},{9,12},{10... | collective-permute-start | bytes 1572872 | tf_op jit(solution)/shard_map/ppermute | solution.py:84
  65.6 34.6 %collective-permute-start.14 = (bf16[2,2,256,512]{3,2,1,0:T(8,128)(2,1)}, bf16[2,2,256,512]{3,2,1,0:T(8,128)(2,1)}, u32[]{:S(2)}, u32[]{:S(2)}) collective-permute-start(bf16[2,2,256,512]{3,2,1,0:T(8,128)(2,1)} %pad_maximum_fusion.1.refs_9_), channel_id=1, source_target_pairs={{0,16},{16,0},{1,17},{17,1},{2,18},{18,2},{3,19},{19,3},{4,20},{20... | collective-permute-start | bytes 3145736 | tf_op jit(solution)/shard_map/ppermute | solution.py:92
  91.4 9.8 %collective-permute-start.20 = (bf16[2,256,512]{2,1,0:T(8,128)(2,1)S(1)}, bf16[2,256,512]{2,1,0:T(8,128)(2,1)S(1)}, u32[]{:S(2)}, u32[]{:S(2)}) collective-permute-start(bf16[2,256,512]{2,1,0:T(8,128)(2,1)S(1)} %get-tuple-element.37), channel_id=1, source_target_pairs={{0,4},{1,12},{2,6},{3,14},{4,5},{5,13},{6,7},{7,15},{8,0},{9,8},{1... | collective-permute-start | bytes 1572872 | tf_op jit(solution)/shard_map/ppermute | solution.py:84
  91.4 37.7 %copy-start.11 = (bf16[2,2,256,512]{3,2,1,0:T(8,128)(2,1)}, bf16[2,2,256,512]{3,2,1,0:T(8,128)(2,1)S(1)}, u32[]{:S(2)}) copy-start(bf16[2,2,256,512]{3,2,1,0:T(8,128)(2,1)S(1)} %collective-permute-done.3.refs_3_) | copy-start | bytes 3145732
  91.4 31.3 %collective-permute-start.7 = (bf16[2,2,256,512]{3,2,1,0:T(8,128)(2,1)S(1)}, bf16[2,2,256,512]{3,2,1,0:T(8,128)(2,1)}, u32[]{:S(2)}, u32[]{:S(2)}) collective-permute-start(bf16[2,2,256,512]{3,2,1,0:T(8,128)(2,1)S(1)} %collective-permute-done.3.refs_3_), channel_id=1, source_target_pairs={{0,16},{16,0},{1,17},{17,1},{2,18},{18,2},{3,19},{19,3},{4,20},{20... | collective-permute-start | bytes 3145736 | tf_op jit(solution)/shard_map/ppermute | solution.py:92
  92.9 36.9 %copy-start.12 = (bf16[2,2,256,512]{3,2,1,0:T(8,128)(2,1)}, bf16[2,2,256,512]{3,2,1,0:T(8,128)(2,1)S(1)}, u32[]{:S(2)}) copy-start(bf16[2,2,256,512]{3,2,1,0:T(8,128)(2,1)S(1)} %collective-permute-done.5.refs_5_) | copy-start | bytes 3145732
  92.9 22.0 %collective-permute-start.21 = (bf16[2,256,512]{2,1,0:T(8,128)(2,1)S(1)}, bf16[2,256,512]{2,1,0:T(8,128)(2,1)S(1)}, u32[]{:S(2)}, u32[]{:S(2)}) collective-permute-start(bf16[2,256,512]{2,1,0:T(8,128)(2,1)S(1)} %get-tuple-element.36), channel_id=1, source_target_pairs={{0,5},{1,13},{2,7},{3,15},{4,4},{5,12},{6,6},{7,14},{8,1},{9,9},{1... | collective-permute-start | bytes 1572872 | tf_op jit(solution)/shard_map/ppermute | solution.py:84
  99.2 31.3 %copy-start.13 = (bf16[2,2,256,512]{3,2,1,0:T(8,128)(2,1)}, bf16[2,2,256,512]{3,2,1,0:T(8,128)(2,1)S(1)}, u32[]{:S(2)}) copy-start(bf16[2,2,256,512]{3,2,1,0:T(8,128)(2,1)S(1)} %collective-permute-done.2.refs_2_) | copy-start | bytes 3145732
  99.2 30.7 %collective-permute-start.4 = (bf16[2,2,256,512]{3,2,1,0:T(8,128)(2,1)S(1)}, bf16[2,2,256,512]{3,2,1,0:T(8,128)(2,1)S(1)}, u32[]{:S(2)}, u32[]{:S(2)}) collective-permute-start(bf16[2,2,256,512]{3,2,1,0:T(8,128)(2,1)S(1)} %collective-permute-done.3.refs_3_), channel_id=1, source_target_pairs={{0,1},{1,0},{2,3},{3,2},{4,5},{5,4},{6,7},{7,6},{8,9},{9,8},{10,11... | collective-permute-start | bytes 3145736 | tf_op jit(solution)/shard_map/ppermute | solution.py:92
  100.2 30.3 %collective-permute-start.6 = (bf16[2,2,256,512]{3,2,1,0:T(8,128)(2,1)S(1)}, bf16[2,2,256,512]{3,2,1,0:T(8,128)(2,1)S(1)}, u32[]{:S(2)}, u32[]{:S(2)}) collective-permute-start(bf16[2,2,256,512]{3,2,1,0:T(8,128)(2,1)S(1)} %collective-permute-done.5.refs_5_), channel_id=1, source_target_pairs={{0,1},{1,0},{2,3},{3,2},{4,5},{5,4},{6,7},{7,6},{8,9},{9,8},{10,11... | collective-permute-start | bytes 3145736 | tf_op jit(solution)/shard_map/ppermute | solution.py:92
  101.2 41.8 %collective-permute-start.16 = (bf16[2,2,256,512]{3,2,1,0:T(8,128)(2,1)}, bf16[2,2,256,512]{3,2,1,0:T(8,128)(2,1)}, u32[]{:S(2)}, u32[]{:S(2)}) collective-permute-start(bf16[2,2,256,512]{3,2,1,0:T(8,128)(2,1)} %collective-permute-done.12.refs_11_), channel_id=1, source_target_pairs={{0,16},{16,0},{1,17},{17,1},{2,18},{18,2},{3,19},{19,3},{4,20},{20... | collective-permute-start | bytes 3145736 | tf_op jit(solution)/shard_map/ppermute | solution.py:92
  115.0 0.8 copy-start
  115.8 13.3 %collective-permute-start.19 = (bf16[2,256,512]{2,1,0:T(8,128)(2,1)S(1)}, bf16[2,256,512]{2,1,0:T(8,128)(2,1)S(1)}, u32[]{:S(2)}, u32[]{:S(2)}) collective-permute-start(bf16[2,256,512]{2,1,0:T(8,128)(2,1)S(1)} %dynamic-slice_bitcast_fusion.2), channel_id=1, source_target_pairs={{0,1},{1,9},{2,3},{3,11},{4,0},{5,8},{6,2},{7,10},{8,5},{9,13},{10... | collective-permute-start | bytes 1572872 | tf_op jit(solution)/shard_map/ppermute | solution.py:84
  122.7 20.5 %collective-permute-start.8 = (bf16[2,2,256,512]{3,2,1,0:T(8,128)(2,1)}, bf16[2,2,256,512]{3,2,1,0:T(8,128)(2,1)}, u32[]{:S(2)}, u32[]{:S(2)}) collective-permute-start(bf16[2,2,256,512]{3,2,1,0:T(8,128)(2,1)} %collective-permute-done.7.refs_7_), channel_id=1, source_target_pairs={{0,1},{1,0},{2,3},{3,2},{4,5},{5,4},{6,7},{7,6},{8,9},{9,8},{10,11... | collective-permute-start | bytes 3145736 | tf_op jit(solution)/shard_map/ppermute | solution.py:92
  129.1 0.8 copy-start.2
  129.9 24.2 %collective-permute-start.11 = (bf16[2,2,256,512]{3,2,1,0:T(8,128)(2,1)}, bf16[2,2,256,512]{3,2,1,0:T(8,128)(2,1)}, u32[]{:S(2)}, u32[]{:S(2)}) collective-permute-start(bf16[2,2,256,512]{3,2,1,0:T(8,128)(2,1)} %pad_maximum_fusion.1.refs_9_), channel_id=1, source_target_pairs={{0,1},{1,0},{2,3},{3,2},{4,5},{5,4},{6,7},{7,6},{8,9},{9,8},{10,11... | collective-permute-start | bytes 3145736 | tf_op jit(solution)/shard_map/ppermute | solution.py:92
  129.9 1.0 copy-start.14
  129.9 24.2 %collective-permute-start.13 = (bf16[2,2,256,512]{3,2,1,0:T(8,128)(2,1)}, bf16[2,2,256,512]{3,2,1,0:T(8,128)(2,1)}, u32[]{:S(2)}, u32[]{:S(2)}) collective-permute-start(bf16[2,2,256,512]{3,2,1,0:T(8,128)(2,1)} %collective-permute-done.12.refs_11_), channel_id=1, source_target_pairs={{0,1},{1,0},{2,3},{3,2},{4,5},{5,4},{6,7},{7,6},{8,9},{9,8},{10,11... | collective-permute-start | bytes 3145736 | tf_op jit(solution)/shard_map/ppermute | solution.py:92
  130.4 12.6 %copy-start.15 = (bf16[2,2,256,512]{3,2,1,0:T(8,128)(2,1)}, bf16[2,2,256,512]{3,2,1,0:T(8,128)(2,1)S(1)}, u32[]{:S(2)}) copy-start(bf16[2,2,256,512]{3,2,1,0:T(8,128)(2,1)S(1)} %collective-permute-done.6.refs_6_) | copy-start | bytes 3145732
  130.4 23.6 %collective-permute-start.15 = (bf16[2,2,256,512]{3,2,1,0:T(8,128)(2,1)}, bf16[2,2,256,512]{3,2,1,0:T(8,128)(2,1)}, u32[]{:S(2)}, u32[]{:S(2)}) collective-permute-start(bf16[2,2,256,512]{3,2,1,0:T(8,128)(2,1)} %collective-permute-done.14.refs_13_), channel_id=1, source_target_pairs={{0,1},{1,0},{2,3},{3,2},{4,5},{5,4},{6,7},{7,6},{8,9},{9,8},{10,11... | collective-permute-start | bytes 3145736 | tf_op jit(solution)/shard_map/ppermute | solution.py:92
  143.0 11.0 %collective-permute-start.17 = (bf16[2,2,256,512]{3,2,1,0:T(8,128)(2,1)}, bf16[2,2,256,512]{3,2,1,0:T(8,128)(2,1)}, u32[]{:S(2)}, u32[]{:S(2)}) collective-permute-start(bf16[2,2,256,512]{3,2,1,0:T(8,128)(2,1)} %collective-permute-done.16.refs_15_), channel_id=1, source_target_pairs={{0,1},{1,0},{2,3},{3,2},{4,5},{5,4},{6,7},{7,6},{8,9},{9,8},{10,11... | collective-permute-start | bytes 3145736 | tf_op jit(solution)/shard_map/ppermute | solution.py:92
  143.1 1.0 copy-start.1
  144.2 1.0 copy-start.3
  154.1 2.2 copy-start.4
  156.3 1.6 copy-start.5
  171.3 55.6 %collective-permute-start.27 = (bf16[2,256,512]{2,1,0:T(8,128)(2,1)S(1)}, bf16[2,256,512]{2,1,0:T(8,128)(2,1)S(1)}, u32[]{:S(2)}, u32[]{:S(2)}) collective-permute-start(bf16[2,256,512]{2,1,0:T(8,128)(2,1)S(1)} %get-tuple-element.25.refs_4_), channel_id=1, source_target_pairs={{0,0},{8,1},{2,2},{10,3},{1,4},{9,5},{3,6},{11,7},{4,8},{12,9},{6,... | collective-permute-start | bytes 1572872 | tf_op jit(solution)/shard_map/ppermute | solution.py:88
  173.2 56.0 %collective-permute-start.28 = (bf16[2,256,512]{2,1,0:T(8,128)(2,1)S(1)}, bf16[2,256,512]{2,1,0:T(8,128)(2,1)S(1)}, u32[]{:S(2)}, u32[]{:S(2)}) collective-permute-start(bf16[2,256,512]{2,1,0:T(8,128)(2,1)S(1)} %get-tuple-element.26.refs_5_), channel_id=1, source_target_pairs={{1,0},{9,1},{3,2},{11,3},{0,4},{8,5},{2,6},{10,7},{5,8},{13,9},{7,... | collective-permute-start | bytes 1572872 | tf_op jit(solution)/shard_map/ppermute | solution.py:88
  180.2 49.3 %collective-permute-start.29 = (bf16[2,256,512]{2,1,0:T(8,128)(2,1)S(1)}, bf16[2,256,512]{2,1,0:T(8,128)(2,1)S(1)}, u32[]{:S(2)}, u32[]{:S(2)}) collective-permute-start(bf16[2,256,512]{2,1,0:T(8,128)(2,1)S(1)} %get-tuple-element.28.refs_6_), channel_id=1, source_target_pairs={{4,0},{12,1},{6,2},{14,3},{5,4},{13,5},{7,6},{15,7},{0,8},{8,9},{2... | collective-permute-start | bytes 1572872 | tf_op jit(solution)/shard_map/ppermute | solution.py:88
  192.0 41.0 %collective-permute-start.30 = (bf16[2,256,512]{2,1,0:T(8,128)(2,1)S(1)}, bf16[2,256,512]{2,1,0:T(8,128)(2,1)S(1)}, u32[]{:S(2)}, u32[]{:S(2)}) collective-permute-start(bf16[2,256,512]{2,1,0:T(8,128)(2,1)S(1)} %get-tuple-element.29.refs_7_), channel_id=1, source_target_pairs={{5,0},{13,1},{7,2},{15,3},{4,4},{12,5},{6,6},{14,7},{1,8},{9,9},{3... | collective-permute-start | bytes 1572872 | tf_op jit(solution)/shard_map/ppermute | solution.py:88
  195.3 1.2 collective-permute-start.22
  196.5 3.5 %collective-permute-start.23 = (f32[2]{0:T(128)S(1)}, f32[2]{0:T(128)S(1)}, u32[]{:S(2)}, u32[]{:S(2)}) collective-permute-start(f32[2]{0:T(128)S(1)} %add.90), channel_id=1, source_target_pairs={{0,16},{16,0},{1,17},{17,1},{2,18},{18,2},{3,19},{19,3},{4,20},{20... | collective-permute-start | bytes 32 | tf_op jit(solution)/shard_map/ppermute | solution.py:92
  200.0 3.5 %collective-permute-start.24 = (f32[2]{0:T(128)S(1)}, f32[2]{0:T(128)S(1)}, u32[]{:S(2)}, u32[]{:S(2)}) collective-permute-start(f32[2]{0:T(128)S(1)} %add.91), channel_id=1, source_target_pairs={{0,2},{2,0},{1,3},{3,1},{4,6},{6,4},{5,7},{7,5},{8,10},{10,8},{9,1... | collective-permute-start | bytes 32 | tf_op jit(solution)/shard_map/ppermute | solution.py:92
  203.6 6.8 %collective-permute-start.25 = (f32[2]{0:T(128)S(1)}, f32[2]{0:T(128)S(1)}, u32[]{:S(2)}, u32[]{:S(2)}) collective-permute-start(f32[2]{0:T(128)S(1)} %add.92), channel_id=1, source_target_pairs={{0,4},{4,0},{1,5},{5,1},{2,6},{6,2},{3,7},{7,3},{8,12},{12,8},{9,1... | collective-permute-start | bytes 32 | tf_op jit(solution)/shard_map/ppermute | solution.py:92
  210.3 8.8 %collective-permute-start.26 = (f32[2]{0:T(128)S(1)}, f32[2]{0:T(128)S(1)}, u32[]{:S(2)}, u32[]{:S(2)}) collective-permute-start(f32[2]{0:T(128)S(1)} %add.93), channel_id=1, source_target_pairs={{0,8},{8,0},{1,9},{9,1},{2,10},{10,2},{3,11},{11,3},{4,12},{12,4},... | collective-permute-start | bytes 32 | tf_op jit(solution)/shard_map/ppermute | solution.py:92
  222.2 6.9 %copy-start.7 = (bf16[2,1,1024,512]{3,2,1,0:T(8,128)(2,1)S(1)}, bf16[2,1,1024,512]{3,2,1,0:T(8,128)(2,1)}, u32[]{:S(2)}) copy-start(bf16[2,1,1024,512]{3,2,1,0:T(8,128)(2,1)} %param.3) | copy-start | bytes 6291460
  222.2 39.6 %collective-permute-start.31 = (bf16[2,256,512]{2,1,0:T(8,128)(2,1)S(1)}, bf16[2,256,512]{2,1,0:T(8,128)(2,1)S(1)}, u32[]{:S(2)}, u32[]{:S(2)}) collective-permute-start(bf16[2,256,512]{2,1,0:T(8,128)(2,1)S(1)} %get-tuple-element.35), channel_id=1, source_target_pairs={{0,0},{8,1},{2,2},{10,3},{1,4},{9,5},{3,6},{11,7},{4,8},{12,9},{6,... | collective-permute-start | bytes 1572872 | tf_op jit(solution)/shard_map/ppermute | solution.py:88
  226.9 45.9 %collective-permute-start.32 = (bf16[2,256,512]{2,1,0:T(8,128)(2,1)S(1)}, bf16[2,256,512]{2,1,0:T(8,128)(2,1)S(1)}, u32[]{:S(2)}, u32[]{:S(2)}) collective-permute-start(bf16[2,256,512]{2,1,0:T(8,128)(2,1)S(1)} %get-tuple-element.34), channel_id=1, source_target_pairs={{1,0},{9,1},{3,2},{11,3},{0,4},{8,5},{2,6},{10,7},{5,8},{13,9},{7,... | collective-permute-start | bytes 1572872 | tf_op jit(solution)/shard_map/ppermute | solution.py:88
  229.3 43.6 %collective-permute-start.33 = (bf16[2,256,512]{2,1,0:T(8,128)(2,1)S(1)}, bf16[2,256,512]{2,1,0:T(8,128)(2,1)S(1)}, u32[]{:S(2)}, u32[]{:S(2)}) collective-permute-start(bf16[2,256,512]{2,1,0:T(8,128)(2,1)S(1)} %get-tuple-element.33), channel_id=1, source_target_pairs={{4,0},{12,1},{6,2},{14,3},{5,4},{13,5},{7,6},{15,7},{0,8},{8,9},{2... | collective-permute-start | bytes 1572872 | tf_op jit(solution)/shard_map/ppermute | solution.py:88
  229.5 44.0 %collective-permute-start.34 = (bf16[2,256,512]{2,1,0:T(8,128)(2,1)S(1)}, bf16[2,256,512]{2,1,0:T(8,128)(2,1)S(1)}, u32[]{:S(2)}, u32[]{:S(2)}) collective-permute-start(bf16[2,256,512]{2,1,0:T(8,128)(2,1)S(1)} %get-tuple-element.32), channel_id=1, source_target_pairs={{5,0},{13,1},{7,2},{15,3},{4,4},{12,5},{6,6},{14,7},{1,8},{9,9},{3... | collective-permute-start | bytes 1572872 | tf_op jit(solution)/shard_map/ppermute | solution.py:88
  233.2 29.1 %copy-start.9 = (bf16[2,4,256,512]{3,2,1,0:T(8,128)(2,1)}, bf16[2,4,256,512]{3,2,1,0:T(8,128)(2,1)S(1)}, u32[]{:S(2)}) copy-start(bf16[2,4,256,512]{3,2,1,0:T(8,128)(2,1)S(1)} %fusion.15) | copy-start | bytes 6291460
  273.6 2.0 copy-start.8

commit v4 on v3

--- a/solution.py
+++ b/solution.py
@@ -90,6 +90,10 @@
 
 def swap(value, axis):
     return lax.ppermute(value, axis, [(0, 1), (1, 0)])
+
+
+def pinned(value):
+    return pltpu.with_memory_space_constraint(value, pltpu.HBM)
 
 
 def total(value):
@@ -157,61 +161,48 @@
         copy.wait()
 
 
-def forward_kernel(rows, width, where_ref, *refs):
-    a_in, x_refs, d_refs, (f_out, wide_out) = refs[:8], refs[8:12], refs[12:16], refs[16:18]
-    a_v, wide_v, x_v, d_v, f_v, sems, x_sems, d_sems, out_sems = refs[18:]
-    part = where_ref[1]
-    copies = place_copies(GROUPS[0], a_in, (where_ref[0], part), a_v, sems, rows)
-    x_copies = message_copies(x_refs, part, wide_v, x_v, x_sems, rows, width)
-    for k in range(4):
-        x_copies.append(pltpu.make_async_copy(d_refs[k], d_v.at[k], d_sems.at[k]))
-    for copy in copies[0] + x_copies + copies[1]:
-        copy.start()
-    for copy in x_copies:
-        copy.wait()
-    outs = [pltpu.make_async_copy(wide_v, wide_out, out_sems.at[4])]
-    outs[0].start()
+def collect_kernel(rows, width, where_ref, *refs):
+    a_in, (a_v, sems) = refs[:8], refs[8:]
+    copies = place_copies(GROUPS[0], a_in, (where_ref[0], where_ref[1]), a_v, sems, rows)
+    for t in range(4):
+        for copy in copies[t]:
+            copy.start()
     for t in range(4):
         for copy in copies[t]:
             copy.wait()
-        if t < 2:
-            for copy in copies[t + 2]:
-                copy.start()
-        forward = product(wide_v[part // 2 ^ t // 2], a_v, t, rows)
-        for i in range(2):
-            own = d_v[t, i].astype(jnp.float32) - x_v[t, i].astype(jnp.float32)
-            f_v[t, i] = own + forward[i]
-        outs.append(pltpu.make_async_copy(f_v.at[t], f_out.at[t], out_sems.at[t]))
-        outs[-1].start()
-    for copy in outs:
-        copy.wait()
-
-
-def residual_kernel(rows, width, where_ref, *refs):
-    a_in, b_in, (wide_in, f_in), refs = refs[:8], refs[8:16], refs[16:18], refs[18:]
-    a_v, b_v, r_v, rb_v, g0, g1, wide_v, f_v, g_v, a_sems, b_sems, in_sems, out_sems = refs
+
+
+def residual_kernel(rows, width, where_ref, a_v, *refs):
+    b_in, x_refs, d_refs, refs = refs[:8], refs[8:12], refs[12:16], refs[16:]
+    b_v, r_v, rb_v, g0, g1, wide_v, x_v, d_v, g_v, b_sems, x_sems, d_sems, out_sems = refs
     where = (where_ref[0], where_ref[1])
     part = where[1]
     copies = place_copies(GROUPS[1], b_in, where, b_v, b_sems, rows)
-    later = place_copies(GROUPS[0], a_in, where, a_v, a_sems, rows)
-    for t in range(4):
-        copies[t].append(pltpu.make_async_copy(f_in.at[t], f_v.at[t], in_sems.at[t]))
-    copies[0].append(pltpu.make_async_copy(wide_in, wide_v, in_sems.at[4]))
-    for copy in copies[0] + copies[1]:
+    x_copies = message_copies(x_refs, part, wide_v, x_v, x_sems, rows, width)
+    for k in range(4):
+        copies[0].append(pltpu.make_async_copy(d_refs[k], d_v.at[k], d_sems.at[k]))
+    copies[0] += [x_copies[3 * k + 2] for k in range(4)]
+    wide_copies = [x_copies[3 * k + i] for k in range(4) for i in range(2)]
+    for copy in wide_copies:
         copy.start()
+    for copy in wide_copies:
+        copy.wait()
+    for t in range(4):
+        for copy in copies[t]:
+            copy.start()
+    for t in range(4):
+        forward = product(wide_v[part // 2 ^ t // 2], a_v, t, rows)
+        for i in range(2):
+            r_v[t, i] = forward[i]
     for t in range(4):
         for copy in copies[t]:
             copy.wait()
-        for copy in copies[t + 2] if t < 2 else later[2 * t - 4] + later[2 * t - 3]:
-            copy.start()
         forward = product(wide_v[1 - (part // 2 ^ t // 2)], b_v, t, rows)
         for i in range(2):
-            residual = f_v[t, i] + forward[i]
+            own = d_v[t, i].astype(jnp.float32) - x_v[t, i].astype(jnp.float32)
+            residual = own + (r_v[t, i] + forward[i])
             r_v[t, i] = residual
             rb_v[t, i * rows : (i + 1) * rows, :] = residual.astype(jnp.bfloat16)
-    for t in range(4):
-        for copy in later[t]:
-            copy.wait()
     gradient_blocks(0, part, a_v, b_v, r_v, rb_v, g_v, (g0, g1), out_sems, rows, width)
 
 
@@ -253,20 +244,28 @@
     prim_blocks = primaries.reshape(2, MESSAGES, rows, width)
 
     arrived = [to_home(data_blocks, z, k) for k in range(MESSAGES)]
-    buffers, by_pair = [], []
+    held = []
     for group in GROUPS:
         own = jnp.stack([arrived[k] for k in group])
-        held = {(0, 0): own, (0, 2): swap(own, "pair")}
-        by_pair.append(held[0, 2])
-        held.update({(1, dp): swap(v, "row") for (_, dp), v in list(held.items())})
-        held.update({(dx, dp ^ 1): swap(v, "lane") for (dx, dp), v in list(held.items())})
-        buffers.append(
-            [pltpu.with_memory_space_constraint(held[at], pltpu.HBM) for at in OFFSETS]
-        )
+        pieces = {(0, 0): own, (0, 2): swap(own, "pair"), (1, 0): swap(own, "row")}
+        pieces[1, 2] = swap(pieces[0, 2], "row")
+        held.append(pieces)
+    ready = [[arrived, held[0][1, 0]], [held[1][1, 0], held[0][0, 2]], [held[1][0, 2]], [held[1][0, 2]]]
     x_parts = []
-    for k, ready in enumerate((arrived, by_pair[0], by_pair[1], by_pair[1])):
-        later, _ = lax.optimization_barrier((prim_blocks, ready))
+    for k in range(MESSAGES):
+        later, _ = lax.optimization_barrier((prim_blocks, ready[k]))
         x_parts.append(to_home(later, z, k))
+
+    def complete(pieces, after):
+        for at, value in list(pieces.items()):
+            if at != (1, 2):
+                value, _ = lax.optimization_barrier((value, after))
+            pieces[at[0], at[1] ^ 1] = swap(value, "lane")
+        return [pinned(pieces[at]) for at in OFFSETS]
+
+    held[1][1, 2], _ = lax.optimization_barrier((held[1][1, 2], x_parts))
+    first_buffers = complete(held[0], held[0][1, 2])
+    second_buffers = complete(held[1], first_buffers[3])
 
     hbm = pl.BlockSpec(memory_space=pltpu.HBM)
     vmem = pl.BlockSpec(memory_space=pltpu.VMEM)
@@ -295,39 +294,28 @@
             name=name,
         )
 
-    partial, x_wide = call(
-        forward_kernel,
-        "forward",
-        0.5,
-        26,
-        [hbm] * 16,
-        [hbm] * 2,
+    data_a = call(
+        collect_kernel, "collect", 0.1, 2, [hbm] * 8, vmem, data_half, [dma((16,))]
+    )(where, *first_buffers)
+    data_b, residual, res_rounded, g0, g1 = call(
+        residual_kernel,
+        "residual",
+        1.5,
+        16,
+        [vmem] + [hbm] * 16,
+        [vmem] * 3 + [hbm] * 2,
+        [data_half, f32_blocks, rounded, message, message],
         [
-            pltpu.HBM((4, 2, rows, width), jnp.float32),
-            pltpu.HBM((2, 2 * rows, 2 * width), jnp.bfloat16),
-        ],
-        [
-            data_half,
             wide,
             blocks,
             blocks,
-            f32_blocks,
+            two_messages,
             dma((16,)),
             dma((12,)),
             dma((4,)),
-            dma((5,)),
+            dma((2,)),
         ],
-    )(where, *buffers[0], *x_parts, *arrived)
-    data_a, data_b, residual, res_rounded, g0, g1 = call(
-        residual_kernel,
-        "residual",
-        1.0,
-        14,
-        [hbm] * 18,
-        [vmem] * 4 + [hbm] * 2,
-        [data_half, data_half, f32_blocks, rounded, message, message],
-        [wide, f32_blocks, two_messages, dma((16,)), dma((16,)), dma((5,)), dma((2,))],
-    )(where, *buffers[0], *buffers[1], x_wide, partial)
+    )(where, data_a, *second_buffers, *map(pinned, x_parts), *map(pinned, arrived))
     g2, g3 = call(
         gradient_kernel,
         "gradient",

time: 276 us -> 271 us (0.982)
  waiting for transfers between devices: 169 us -> 146 us
  starting transfers between devices: 48.1 us -> 66.3 us
  local copies, waits for them, and re-layouts: 13.5 us -> 9.28 us
    ppermute x8, waiting for transfers between devices: 82.1 us -> 50.9 us  [to_home(): return lax.ppermute(piece, COLUMN, send_pairs(k))]
    ppermute x19, starting transfers between devices: 16 us -> 27.9 us  [swap(): return lax.ppermute(value, axis, [(0, 1), (1, 0)])]
    ppermute x19, waiting for transfers between devices: 47.8 us -> 56.5 us  [swap(): return lax.ppermute(value, axis, [(0, 1), (1, 0)])]
    unnamed x32 -> x36, local copies, waits for them, and re-layouts: 9.79 us -> 5.61 us
    ppermute x8, starting transfers between devices: 15.2 us -> 18.6 us  [to_home(): return lax.ppermute(piece, COLUMN, send_pairs(k))]
    ppermute x8, starting transfers between devices: 16.9 us -> 19.8 us  [from_home(): return lax.ppermute(piece, COLUMN, [(b, a) for a, b in send_pairs(k)])]
  transfers between devices with their start and end apart: 35 -> 35, of which waited for: 19 -> 18; matrix products, arithmetic and copies ran while one was open for 2% -> 2% of each run, Pallas kernels for 9% -> 8%
where the time goes in v4:
time: 271 us; the launch traced here: 269 us
  waiting for transfers between devices  146 us (54%)
  starting transfers between devices  66.3 us (24%)
  Pallas kernels  41 us (15%)
  local copies, waits for them, and re-layouts  9.28 us (3%)
  other arithmetic  3.72 us (1%)
    ppermute x19, waiting for transfers between devices, swap(): return lax.ppermute(value, axis, [(0, 1), (1, 0)])  56.5 us
    ppermute x8, waiting for transfers between devices, to_home(): return lax.ppermute(piece, COLUMN, send_pairs(k))  50.9 us
    ppermute x8, waiting for transfers between devices, from_home(): return lax.ppermute(piece, COLUMN, [(b, a) for a, b in send_pairs(k)])  38.8 us
    ppermute x19, starting transfers between devices, swap(): return lax.ppermute(value, axis, [(0, 1), (1, 0)])  27.9 us
    pallas_call x1, Pallas kernels, whole_rows(): call(residual_kernel, 'residual', 1.5, 16, [vmem] + [hbm] * 16, [vmem] *...  20.1 us
    ppermute x8, starting transfers between devices, from_home(): return lax.ppermute(piece, COLUMN, [(b, a) for a, b in send_pairs(k)])  19.8 us
    ppermute x8, starting transfers between devices, to_home(): return lax.ppermute(piece, COLUMN, send_pairs(k))  18.6 us
    pallas_call x1, Pallas kernels, whole_rows(): call(change_kernel, 'change', 1.0, 12, [vmem] * 3 + [hbm] * 4, [vmem, sme...  11.7 us
  transfers between devices with their start and end apart: 35, of which 18 were waited for; matrix products, arithmetic and copies ran while one was open for 2% of the time, Pallas kernels for 8%

profile of v4, /device:TPU:20, one launch (start us, length us, event | category | flops | bytes accessed | tf_op | source)
XLA Modules:
  0.0 268.9 jit_solution(3206894647698481419)
XLA Ops:
  0.7 1.7 dynamic-slice_bitcast_fusion.5
  2.3 2.4 collective-permute-start
  4.7 0.8 collective-permute-start.1
  5.5 4.7 %collective-permute-start.10 = (bf16[2,256,512]{2,1,0:T(8,128)(2,1)S(1)}, bf16[2,256,512]{2,1,0:T(8,128)(2,1)S(1)}, u32[]{:S(2)}, u32[]{:S(2)}) collective-permute-start(bf16[2,256,512]{2,1,0:T(8,128)(2,1)S(1)} %get-tuple-element.49), channel_id=1, source_target_pairs={{0,5},{1,13},{2,7},{3,15},{4,4},{5,12},{6,6},{7,14},{8,1},{9,9},{1... | collective-permute-start | bytes 1572872 | tf_op jit(solution)/shard_map/ppermute | solution.py:84
  10.2 9.0 %collective-permute-done.refs_14_ = bf16[2,256,512]{2,1,0:T(8,128)(2,1)S(1)} collective-permute-done((bf16[2,256,512]{2,1,0:T(8,128)(2,1)S(1)}, bf16[2,256,512]{2,1,0:T(8,128)(2,1)S(1)}, u32[]{:S(2)}, u32[]{:S(2)}) %collective-permute-start) | collective-permute-done | bytes 524320 | tf_op jit(solution)/shard_map/ppermute | solution.py:84
  19.3 11.6 %collective-permute-done.1.refs_15_ = bf16[2,256,512]{2,1,0:T(8,128)(2,1)S(1)} collective-permute-done((bf16[2,256,512]{2,1,0:T(8,128)(2,1)S(1)}, bf16[2,256,512]{2,1,0:T(8,128)(2,1)S(1)}, u32[]{:S(2)}, u32[]{:S(2)}) %collective-permute-start.1) | collective-permute-done | bytes 524320 | tf_op jit(solution)/shard_map/ppermute | solution.py:84
  30.9 0.8 copy-done.10
  31.9 1.6 collective-permute-start.6
  33.4 8.4 %collective-permute-done.10.refs_17_ = bf16[2,256,512]{2,1,0:T(8,128)(2,1)S(1)} collective-permute-done((bf16[2,256,512]{2,1,0:T(8,128)(2,1)S(1)}, bf16[2,256,512]{2,1,0:T(8,128)(2,1)S(1)}, u32[]{:S(2)}, u32[]{:S(2)}) %collective-permute-start.10) | collective-permute-done | bytes 524320 | tf_op jit(solution)/shard_map/ppermute | solution.py:84
  41.8 8.9 %collective-permute-done.9.refs_16_ = bf16[2,256,512]{2,1,0:T(8,128)(2,1)S(1)} collective-permute-done((bf16[2,256,512]{2,1,0:T(8,128)(2,1)S(1)}, bf16[2,256,512]{2,1,0:T(8,128)(2,1)S(1)}, u32[]{:S(2)}, u32[]{:S(2)}) %collective-permute-start.9) | collective-permute-done | bytes 524320 | tf_op jit(solution)/shard_map/ppermute | solution.py:84
  50.7 1.2 pad_maximum_fusion.1.refs_2_
  51.9 1.5 collective-permute-start.14
  53.4 0.6 collective-permute-start.12
  54.0 19.2 %collective-permute-done.2.refs_3_ = bf16[2,2,256,512]{3,2,1,0:T(8,128)(2,1)S(1)} collective-permute-done((bf16[2,2,256,512]{3,2,1,0:T(8,128)(2,1)S(1)}, bf16[2,2,256,512]{3,2,1,0:T(8,128)(2,1)S(1)}, u32[]{:S(2)}, u32[]{:S(2)}) %collective-permute-start.2) | collective-permute-done | bytes 1048608 | tf_op jit(solution)/shard_map/ppermute | solution.py:92
  73.2 1.5 collective-permute-start.3
  74.8 1.9 collective-permute-start.17
  76.7 0.6 collective-permute-done.14.refs_6_
  77.3 1.9 collective-permute-start.18
  79.3 16.5 %collective-permute-done.12.refs_4_ = bf16[2,2,256,512]{3,2,1,0:T(8,128)(2,1)} collective-permute-done((bf16[2,2,256,512]{3,2,1,0:T(8,128)(2,1)}, bf16[2,2,256,512]{3,2,1,0:T(8,128)(2,1)}, u32[]{:S(2)}, u32[]{:S(2)}) %collective-permute-start.12) | collective-permute-done | bytes 1048608 | tf_op jit(solution)/shard_map/ppermute | solution.py:92
  95.9 1.5 collective-permute-start.19
  97.3 1.5 collective-permute-start.16
  98.9 1.7 collective-permute-start.7
  100.6 0.8 collective-permute-done.18.refs_11_
  101.4 16.0 %collective-permute-start.4 = (bf16[2,2,256,512]{3,2,1,0:T(8,128)(2,1)S(1)}, bf16[2,2,256,512]{3,2,1,0:T(8,128)(2,1)S(1)}, u32[]{:S(2)}, u32[]{:S(2)}) collective-permute-start(bf16[2,2,256,512]{3,2,1,0:T(8,128)(2,1)S(1)} %pad_maximum_fusion.refs_1_), channel_id=1, source_target_pairs={{0,1},{1,0},{2,3},{3,2},{4,5},{5,4},{6,7},{7,6},{8,9},{9,8},{10,11... | collective-permute-start | bytes 3145736 | tf_op jit(solution)/shard_map/ppermute | solution.py:92
  117.4 5.4 %collective-permute-start.20 = (bf16[2,256,512]{2,1,0:T(8,128)(2,1)S(1)}, bf16[2,256,512]{2,1,0:T(8,128)(2,1)S(1)}, u32[]{:S(2)}, u32[]{:S(2)}) collective-permute-start(bf16[2,256,512]{2,1,0:T(8,128)(2,1)S(1)} %get-tuple-element.44), channel_id=1, source_target_pairs={{0,5},{1,13},{2,7},{3,15},{4,4},{5,12},{6,6},{7,14},{8,1},{9,9},{1... | collective-permute-start | bytes 1572872 | tf_op jit(solution)/shard_map/ppermute | solution.py:84
  122.8 12.1 %collective-permute-done.20.refs_13_ = bf16[2,256,512]{2,1,0:T(8,128)(2,1)S(1)} collective-permute-done((bf16[2,256,512]{2,1,0:T(8,128)(2,1)S(1)}, bf16[2,256,512]{2,1,0:T(8,128)(2,1)S(1)}, u32[]{:S(2)}, u32[]{:S(2)}) %collective-permute-start.20) | collective-permute-done | bytes 524320 | tf_op jit(solution)/shard_map/ppermute | solution.py:84
  134.9 0.5 collective-permute-start.21
  135.5 0.4 collective-permute-start.15
  136.0 0.5 copy-done.6
  136.5 0.3 copy-done.7
  136.8 1.0 copy-done.8
  138.0 4.1 %collect.1.refs_1_ = bf16[4,2,1024,512]{3,2,1,0:T(8,128)(2,1)S(1)} custom-call(s32[2]{0:T(128)S(1)} %pad_add_fusion.refs_0_, bf16[2,2,256,512]{3,2,1,0:T(8,128)(2,1)} %copy-done.1, bf16[2,2,256,512]{3,2,1,0:T(8,128)(2,1)} %copy-done.8, bf16[2,2,256,512]{3,2,1,0:T(8,128)(2,1)} %copy-done.4, bf16[2,2,256,512]{3,2,1,0:T(8,128)(2,1)} %copy-done.6, ...), custom_call_target="tpu_custom_call" | custom-call | flops 858993472 | bytes 16777216 | tf_op jit(solution)/shard_map/collect/pallas_call | solution.py:297
  142.1 0.4 collective-permute-done.13.refs_5_
  142.4 1.5 collective-permute-done.15.refs_7_
  144.0 1.0 copy-done.13
  144.9 20.1 %residual.1 = (bf16[4,2,1024,512]{3,2,1,0:T(8,128)(2,1)S(1)}, f32[4,2,256,512]{3,2,1,0:T(8,128)S(1)}, bf16[4,512,512]{2,1,0:T(8,128)(2,1)S(1)}, bf16[2,256,512]{2,1,0:T(8,128)(2,1)S(1)}, bf16[2,256,512]{2,1,0:T(8,128)(2,1)S(1)}) custom-call(s32[2]{0:T(128)S(1)} %pad_add_fusion.refs_0_, bf16[4,2,1024,512]{3,2,1,0:T(8,128)(2,1)S(1)} %collect.1.refs_1_, ...), custom_call_target="tpu_custom_call" | custom-call | flops 12884901888 | bytes 16777216 | tf_op jit(solution)/shard_map/residual/pallas_call | solution.py:300
  165.0 4.7 %collective-permute-start.27 = (bf16[2,256,512]{2,1,0:T(8,128)(2,1)S(1)}, bf16[2,256,512]{2,1,0:T(8,128)(2,1)S(1)}, u32[]{:S(2)}, u32[]{:S(2)}) collective-permute-start(bf16[2,256,512]{2,1,0:T(8,128)(2,1)S(1)} %get-tuple-element.33.refs_4_), channel_id=1, source_target_pairs={{0,0},{8,1},{2,2},{10,3},{1,4},{9,5},{3,6},{11,7},{4,8},{12,9},{6,... | collective-permute-start | bytes 1572872 | tf_op jit(solution)/shard_map/ppermute | solution.py:88
  169.7 0.7 collective-permute-start.28
  170.5 5.2 %gradient.1 = (bf16[2,256,512]{2,1,0:T(8,128)(2,1)S(1)}, bf16[2,256,512]{2,1,0:T(8,128)(2,1)S(1)}) custom-call(s32[2]{0:T(128)S(1)} %pad_add_fusion.refs_0_, bf16[4,2,1024,512]{3,2,1,0:T(8,128)(2,1)S(1)} %collect.1.refs_1_, bf16[4,2,1024,512]{3,2,1,0:T(8,128)(2,1)S(1)} %get-tuple-element.31.refs_2_, f32[4,2,256,512]{3,2,1,0:T(8,128)S(1)} %get-tuple-element.32.refs_3_, ...), custom_call_target="tpu_custom_call" | custom-call | flops 4294967296 | bytes 16777216 | tf_op jit(solution)/shard_map/gradient/pallas_call | solution.py:319
  175.7 11.7 %change.1 = (f32[4,2,256,512]{3,2,1,0:T(8,128)S(1)}, f32[2]{0:T(128)S(1)}) custom-call(s32[2]{0:T(128)S(1)} %pad_add_fusion.refs_0_, bf16[4,2,1024,512]{3,2,1,0:T(8,128)(2,1)S(1)} %collect.1.refs_1_, bf16[4,2,1024,512]{3,2,1,0:T(8,128)(2,1)S(1)} %get-tuple-element.31.refs_2_, f32[4,2,256,512]{3,2,1,0:T(8,128)S(1)} %get-tuple-element.32.refs_3_, ...), custom_call_target="tpu_custom_call" | custom-call | flops 8589934592 | bytes 16777216 | tf_op jit(solution)/shard_map/change/pallas_call | solution.py:331
  187.4 4.4 %collective-permute-start.30 = (bf16[2,256,512]{2,1,0:T(8,128)(2,1)S(1)}, bf16[2,256,512]{2,1,0:T(8,128)(2,1)S(1)}, u32[]{:S(2)}, u32[]{:S(2)}) collective-permute-start(bf16[2,256,512]{2,1,0:T(8,128)(2,1)S(1)} %get-tuple-element.37.refs_7_), channel_id=1, source_target_pairs={{5,0},{13,1},{7,2},{15,3},{4,4},{12,5},{6,6},{14,7},{1,8},{9,9},{3... | collective-permute-start | bytes 1572872 | tf_op jit(solution)/shard_map/ppermute | solution.py:88
  191.9 1.1 collective-permute-done.22
  193.0 1.5 collective-permute-start.23
  194.5 2.0 collective-permute-done.23
  196.5 0.5 collective-permute-start.24
  197.0 3.0 %collective-permute-done.24 = f32[2]{0:T(128)S(1)} collective-permute-done((f32[2]{0:T(128)S(1)}, f32[2]{0:T(128)S(1)}, u32[]{:S(2)}, u32[]{:S(2)}) %collective-permute-start.24) | collective-permute-done | bytes 40 | tf_op jit(solution)/shard_map/ppermute | solution.py:92
  200.1 0.3 collective-permute-start.25
  200.4 4.5 %collective-permute-done.25 = f32[2]{0:T(128)S(1)} collective-permute-done((f32[2]{0:T(128)S(1)}, f32[2]{0:T(128)S(1)}, u32[]{:S(2)}, u32[]{:S(2)}) %collective-permute-start.25) | collective-permute-done | bytes 40 | tf_op jit(solution)/shard_map/ppermute | solution.py:92
  204.9 7.6 %collective-permute-done.26 = f32[2]{0:T(128)S(1)} collective-permute-done((f32[2]{0:T(128)S(1)}, f32[2]{0:T(128)S(1)}, u32[]{:S(2)}, u32[]{:S(2)}) %collective-permute-start.26) | collective-permute-done | bytes 40 | tf_op jit(solution)/shard_map/ppermute | solution.py:92
  212.5 0.6 fusion.16
  214.4 1.2 fusion.7
  215.6 1.9 collective-permute-start.31
  217.5 4.8 %collective-permute-start.32 = (bf16[2,256,512]{2,1,0:T(8,128)(2,1)S(1)}, bf16[2,256,512]{2,1,0:T(8,128)(2,1)S(1)}, u32[]{:S(2)}, u32[]{:S(2)}) collective-permute-start(bf16[2,256,512]{2,1,0:T(8,128)(2,1)S(1)} %get-tuple-element.42), channel_id=1, source_target_pairs={{1,0},{9,1},{3,2},{11,3},{0,4},{8,5},{2,6},{10,7},{5,8},{13,9},{7,... | collective-permute-start | bytes 1572872 | tf_op jit(solution)/shard_map/ppermute | solution.py:88
  222.4 0.2 broadcast_in_dim.44
  222.6 0.2 fusion.9
  222.8 0.2 fusion.11
  223.0 3.1 %collective-permute-start.34 = (bf16[2,256,512]{2,1,0:T(8,128)(2,1)S(1)}, bf16[2,256,512]{2,1,0:T(8,128)(2,1)S(1)}, u32[]{:S(2)}, u32[]{:S(2)}) collective-permute-start(bf16[2,256,512]{2,1,0:T(8,128)(2,1)S(1)} %get-tuple-element.40), channel_id=1, source_target_pairs={{5,0},{13,1},{7,2},{15,3},{4,4},{12,5},{6,6},{14,7},{1,8},{9,9},{3... | collective-permute-start | bytes 1572872 | tf_op jit(solution)/shard_map/ppermute | solution.py:88
  226.1 0.2 fusion.13
  226.4 0.2 fusion.15
  226.6 3.1 %collective-permute-done.31 = bf16[2,256,512]{2,1,0:T(8,128)(2,1)S(1)} collective-permute-done((bf16[2,256,512]{2,1,0:T(8,128)(2,1)S(1)}, bf16[2,256,512]{2,1,0:T(8,128)(2,1)S(1)}, u32[]{:S(2)}, u32[]{:S(2)}) %collective-permute-start.31) | collective-permute-done | bytes 524320 | tf_op jit(solution)/shard_map/ppermute | solution.py:88
  229.7 0.5 broadcast_in_dim.49
  230.4 35.6 %collective-permute-done.32 = bf16[2,256,512]{2,1,0:T(8,128)(2,1)S(1)} collective-permute-done((bf16[2,256,512]{2,1,0:T(8,128)(2,1)S(1)}, bf16[2,256,512]{2,1,0:T(8,128)(2,1)S(1)}, u32[]{:S(2)}, u32[]{:S(2)}) %collective-permute-start.32) | collective-permute-done | bytes 524320 | tf_op jit(solution)/shard_map/ppermute | solution.py:88
  266.3 0.4 copy.22
  266.9 2.0 copy-done.2
  (72 shorter events, 1.6 us)
Async XLA Ops:
  2.3 16.9 %collective-permute-start = (bf16[2,256,512]{2,1,0:T(8,128)(2,1)S(1)}, bf16[2,256,512]{2,1,0:T(8,128)(2,1)S(1)}, u32[]{:S(2)}, u32[]{:S(2)}) collective-permute-start(bf16[2,256,512]{2,1,0:T(8,128)(2,1)S(1)} %get-tuple-element.48), channel_id=1, source_target_pairs={{0,0},{1,8},{2,2},{3,10},{4,1},{5,9},{6,3},{7,11},{8,4},{9,12},{10... | collective-permute-start | bytes 1572872 | tf_op jit(solution)/shard_map/ppermute | solution.py:84
  4.7 26.2 %collective-permute-start.1 = (bf16[2,256,512]{2,1,0:T(8,128)(2,1)S(1)}, bf16[2,256,512]{2,1,0:T(8,128)(2,1)S(1)}, u32[]{:S(2)}, u32[]{:S(2)}) collective-permute-start(bf16[2,256,512]{2,1,0:T(8,128)(2,1)S(1)} %get-tuple-element.47), channel_id=1, source_target_pairs={{0,1},{1,9},{2,3},{3,11},{4,0},{5,8},{6,2},{7,10},{8,5},{9,13},{10... | collective-permute-start | bytes 1572872 | tf_op jit(solution)/shard_map/ppermute | solution.py:84
  5.5 36.3 %collective-permute-start.10 = (bf16[2,256,512]{2,1,0:T(8,128)(2,1)S(1)}, bf16[2,256,512]{2,1,0:T(8,128)(2,1)S(1)}, u32[]{:S(2)}, u32[]{:S(2)}) collective-permute-start(bf16[2,256,512]{2,1,0:T(8,128)(2,1)S(1)} %get-tuple-element.49), channel_id=1, source_target_pairs={{0,5},{1,13},{2,7},{3,15},{4,4},{5,12},{6,6},{7,14},{8,1},{9,9},{1... | collective-permute-start | bytes 1572872 | tf_op jit(solution)/shard_map/ppermute | solution.py:84
  10.1 40.6 %collective-permute-start.9 = (bf16[2,256,512]{2,1,0:T(8,128)(2,1)S(1)}, bf16[2,256,512]{2,1,0:T(8,128)(2,1)S(1)}, u32[]{:S(2)}, u32[]{:S(2)}) collective-permute-start(bf16[2,256,512]{2,1,0:T(8,128)(2,1)S(1)} %get-tuple-element.46), channel_id=1, source_target_pairs={{0,4},{1,12},{2,6},{3,14},{4,5},{5,13},{6,7},{7,15},{8,0},{9,8},{1... | collective-permute-start | bytes 1572872 | tf_op jit(solution)/shard_map/ppermute | solution.py:84
  19.3 11.6 %copy-start.9 = (bf16[2,256,512]{2,1,0:T(8,128)(2,1)}, bf16[2,256,512]{2,1,0:T(8,128)(2,1)S(1)}, u32[]{:S(2)}) copy-start(bf16[2,256,512]{2,1,0:T(8,128)(2,1)S(1)} %collective-permute-done.refs_14_) | copy-start | bytes 1572868
  30.9 0.8 copy-start.10
  31.7 43.0 %copy-start = (bf16[2,1,1024,512]{3,2,1,0:T(8,128)(2,1)S(1)}, bf16[2,1,1024,512]{3,2,1,0:T(8,128)(2,1)}, u32[]{:S(2)}) copy-start(bf16[2,1,1024,512]{3,2,1,0:T(8,128)(2,1)} %param.3) | copy-start | bytes 6291460
  31.8 69.6 %copy-start.1 = (bf16[2,2,256,512]{3,2,1,0:T(8,128)(2,1)}, bf16[2,2,256,512]{3,2,1,0:T(8,128)(2,1)S(1)}, u32[]{:S(2)}) copy-start(bf16[2,2,256,512]{3,2,1,0:T(8,128)(2,1)S(1)} %pad_maximum_fusion.refs_1_) | copy-start | bytes 3145732
  31.8 41.4 %collective-permute-start.2 = (bf16[2,2,256,512]{3,2,1,0:T(8,128)(2,1)S(1)}, bf16[2,2,256,512]{3,2,1,0:T(8,128)(2,1)S(1)}, u32[]{:S(2)}, u32[]{:S(2)}) collective-permute-start(bf16[2,2,256,512]{3,2,1,0:T(8,128)(2,1)S(1)} %pad_maximum_fusion.refs_1_), channel_id=1, source_target_pairs={{0,4},{4,0},{1,5},{5,1},{2,6},{6,2},{3,7},{7,3},{8,12},{12,8},{9,1... | collective-permute-start | bytes 3145736 | tf_op jit(solution)/shard_map/ppermute | solution.py:92
  31.9 42.8 %collective-permute-start.6 = (bf16[2,2,256,512]{3,2,1,0:T(8,128)(2,1)S(1)}, bf16[2,2,256,512]{3,2,1,0:T(8,128)(2,1)S(1)}, u32[]{:S(2)}, u32[]{:S(2)}) collective-permute-start(bf16[2,2,256,512]{3,2,1,0:T(8,128)(2,1)S(1)} %pad_maximum_fusion.refs_1_), channel_id=1, source_target_pairs={{0,16},{16,0},{1,17},{17,1},{2,18},{18,2},{3,19},{19,3},{4,20},{20... | collective-permute-start | bytes 3145736 | tf_op jit(solution)/shard_map/ppermute | solution.py:92
  41.8 32.9 %copy-start.11 = (bf16[2,256,512]{2,1,0:T(8,128)(2,1)}, bf16[2,256,512]{2,1,0:T(8,128)(2,1)S(1)}, u32[]{:S(2)}) copy-start(bf16[2,256,512]{2,1,0:T(8,128)(2,1)S(1)} %collective-permute-done.10.refs_17_) | copy-start | bytes 1572868
  50.7 26.0 %copy-start.12 = (bf16[2,256,512]{2,1,0:T(8,128)(2,1)}, bf16[2,256,512]{2,1,0:T(8,128)(2,1)S(1)}, u32[]{:S(2)}) copy-start(bf16[2,256,512]{2,1,0:T(8,128)(2,1)S(1)} %collective-permute-done.9.refs_16_) | copy-start | bytes 1572868
  51.9 25.4 %collective-permute-start.14 = (bf16[2,2,256,512]{3,2,1,0:T(8,128)(2,1)}, bf16[2,2,256,512]{3,2,1,0:T(8,128)(2,1)}, u32[]{:S(2)}, u32[]{:S(2)}) collective-permute-start(bf16[2,2,256,512]{3,2,1,0:T(8,128)(2,1)} %pad_maximum_fusion.1.refs_2_), channel_id=1, source_target_pairs={{0,16},{16,0},{1,17},{17,1},{2,18},{18,2},{3,19},{19,3},{4,20},{20... | collective-permute-start | bytes 3145736 | tf_op jit(solution)/shard_map/ppermute | solution.py:92
  53.4 42.4 %collective-permute-start.12 = (bf16[2,2,256,512]{3,2,1,0:T(8,128)(2,1)}, bf16[2,2,256,512]{3,2,1,0:T(8,128)(2,1)}, u32[]{:S(2)}, u32[]{:S(2)}) collective-permute-start(bf16[2,2,256,512]{3,2,1,0:T(8,128)(2,1)} %pad_maximum_fusion.1.refs_2_), channel_id=1, source_target_pairs={{0,4},{4,0},{1,5},{5,1},{2,6},{6,2},{3,7},{7,3},{8,12},{12,8},{9,1... | collective-permute-start | bytes 3145736 | tf_op jit(solution)/shard_map/ppermute | solution.py:92
  73.2 25.6 %copy-start.4 = (bf16[2,2,256,512]{3,2,1,0:T(8,128)(2,1)}, bf16[2,2,256,512]{3,2,1,0:T(8,128)(2,1)S(1)}, u32[]{:S(2)}) copy-start(bf16[2,2,256,512]{3,2,1,0:T(8,128)(2,1)S(1)} %collective-permute-done.2.refs_3_) | copy-start | bytes 3145732
  73.2 25.6 %collective-permute-start.3 = (bf16[2,2,256,512]{3,2,1,0:T(8,128)(2,1)S(1)}, bf16[2,2,256,512]{3,2,1,0:T(8,128)(2,1)}, u32[]{:S(2)}, u32[]{:S(2)}) collective-permute-start(bf16[2,2,256,512]{3,2,1,0:T(8,128)(2,1)S(1)} %collective-permute-done.2.refs_3_), channel_id=1, source_target_pairs={{0,16},{16,0},{1,17},{17,1},{2,18},{18,2},{3,19},{19,3},{4,20},{20... | collective-permute-start | bytes 3145736 | tf_op jit(solution)/shard_map/ppermute | solution.py:92
  74.7 24.2 %copy-start.5 = (bf16[2,2,256,512]{3,2,1,0:T(8,128)(2,1)}, bf16[2,2,256,512]{3,2,1,0:T(8,128)(2,1)S(1)}, u32[]{:S(2)}) copy-start(bf16[2,2,256,512]{3,2,1,0:T(8,128)(2,1)S(1)} %collective-permute-done.6.refs_5_) | copy-start | bytes 3145732
  74.8 24.1 %collective-permute-start.17 = (bf16[2,256,512]{2,1,0:T(8,128)(2,1)S(1)}, bf16[2,256,512]{2,1,0:T(8,128)(2,1)S(1)}, u32[]{:S(2)}, u32[]{:S(2)}) collective-permute-start(bf16[2,256,512]{2,1,0:T(8,128)(2,1)S(1)} %dynamic-slice_bitcast_fusion.3), channel_id=1, source_target_pairs={{0,0},{1,8},{2,2},{3,10},{4,1},{5,9},{6,3},{7,11},{8,4},{9,12},{10... | collective-permute-start | bytes 1572872 | tf_op jit(solution)/shard_map/ppermute | solution.py:84
  77.3 24.1 %collective-permute-start.18 = (bf16[2,256,512]{2,1,0:T(8,128)(2,1)S(1)}, bf16[2,256,512]{2,1,0:T(8,128)(2,1)S(1)}, u32[]{:S(2)}, u32[]{:S(2)}) collective-permute-start(bf16[2,256,512]{2,1,0:T(8,128)(2,1)S(1)} %dynamic-slice_bitcast_fusion.2), channel_id=1, source_target_pairs={{0,1},{1,9},{2,3},{3,11},{4,0},{5,8},{6,2},{7,10},{8,5},{9,13},{10... | collective-permute-start | bytes 1572872 | tf_op jit(solution)/shard_map/ppermute | solution.py:84
  95.9 21.6 %collective-permute-start.19 = (bf16[2,256,512]{2,1,0:T(8,128)(2,1)S(1)}, bf16[2,256,512]{2,1,0:T(8,128)(2,1)S(1)}, u32[]{:S(2)}, u32[]{:S(2)}) collective-permute-start(bf16[2,256,512]{2,1,0:T(8,128)(2,1)S(1)} %get-tuple-element.45), channel_id=1, source_target_pairs={{0,4},{1,12},{2,6},{3,14},{4,5},{5,13},{6,7},{7,15},{8,0},{9,8},{1... | collective-permute-start | bytes 1572872 | tf_op jit(solution)/shard_map/ppermute | solution.py:84
  97.3 37.6 %collective-permute-start.16 = (bf16[2,2,256,512]{3,2,1,0:T(8,128)(2,1)}, bf16[2,2,256,512]{3,2,1,0:T(8,128)(2,1)}, u32[]{:S(2)}, u32[]{:S(2)}) collective-permute-start(bf16[2,2,256,512]{3,2,1,0:T(8,128)(2,1)} %collective-permute-done.12.refs_4_), channel_id=1, source_target_pairs={{0,16},{16,0},{1,17},{17,1},{2,18},{18,2},{3,19},{19,3},{4,20},{20... | collective-permute-start | bytes 3145736 | tf_op jit(solution)/shard_map/ppermute | solution.py:92
  98.8 36.6 %collective-permute-start.5 = (bf16[2,2,256,512]{3,2,1,0:T(8,128)(2,1)S(1)}, bf16[2,2,256,512]{3,2,1,0:T(8,128)(2,1)S(1)}, u32[]{:S(2)}, u32[]{:S(2)}) collective-permute-start(bf16[2,2,256,512]{3,2,1,0:T(8,128)(2,1)S(1)} %collective-permute-done.2.refs_3_), channel_id=1, source_target_pairs={{0,1},{1,0},{2,3},{3,2},{4,5},{5,4},{6,7},{7,6},{8,9},{9,8},{10,11... | collective-permute-start | bytes 3145736 | tf_op jit(solution)/shard_map/ppermute | solution.py:92
  98.9 37.1 %copy-start.14 = (bf16[2,256,512]{2,1,0:T(8,128)(2,1)}, bf16[2,256,512]{2,1,0:T(8,128)(2,1)S(1)}, u32[]{:S(2)}) copy-start(bf16[2,256,512]{2,1,0:T(8,128)(2,1)S(1)} %collective-permute-done.17.refs_10_) | copy-start | bytes 1572868
  98.9 36.7 %collective-permute-start.7 = (bf16[2,2,256,512]{3,2,1,0:T(8,128)(2,1)S(1)}, bf16[2,2,256,512]{3,2,1,0:T(8,128)(2,1)S(1)}, u32[]{:S(2)}, u32[]{:S(2)}) collective-permute-start(bf16[2,2,256,512]{3,2,1,0:T(8,128)(2,1)S(1)} %collective-permute-done.6.refs_5_), channel_id=1, source_target_pairs={{0,1},{1,0},{2,3},{3,2},{4,5},{5,4},{6,7},{7,6},{8,9},{9,8},{10,11... | collective-permute-start | bytes 3145736 | tf_op jit(solution)/shard_map/ppermute | solution.py:92
  101.4 34.6 %copy-start.15 = (bf16[2,256,512]{2,1,0:T(8,128)(2,1)}, bf16[2,256,512]{2,1,0:T(8,128)(2,1)S(1)}, u32[]{:S(2)}) copy-start(bf16[2,256,512]{2,1,0:T(8,128)(2,1)S(1)} %collective-permute-done.18.refs_11_) | copy-start | bytes 1572868
  101.4 34.6 %collective-permute-start.4 = (bf16[2,2,256,512]{3,2,1,0:T(8,128)(2,1)S(1)}, bf16[2,2,256,512]{3,2,1,0:T(8,128)(2,1)S(1)}, u32[]{:S(2)}, u32[]{:S(2)}) collective-permute-start(bf16[2,2,256,512]{3,2,1,0:T(8,128)(2,1)S(1)} %pad_maximum_fusion.refs_1_), channel_id=1, source_target_pairs={{0,1},{1,0},{2,3},{3,2},{4,5},{5,4},{6,7},{7,6},{8,9},{9,8},{10,11... | collective-permute-start | bytes 3145736 | tf_op jit(solution)/shard_map/ppermute | solution.py:92
  117.4 18.6 %copy-start.16 = (bf16[2,256,512]{2,1,0:T(8,128)(2,1)}, bf16[2,256,512]{2,1,0:T(8,128)(2,1)S(1)}, u32[]{:S(2)}) copy-start(bf16[2,256,512]{2,1,0:T(8,128)(2,1)S(1)} %collective-permute-done.19.refs_12_) | copy-start | bytes 1572868
  117.4 17.5 %collective-permute-start.20 = (bf16[2,256,512]{2,1,0:T(8,128)(2,1)S(1)}, bf16[2,256,512]{2,1,0:T(8,128)(2,1)S(1)}, u32[]{:S(2)}, u32[]{:S(2)}) collective-permute-start(bf16[2,256,512]{2,1,0:T(8,128)(2,1)S(1)} %get-tuple-element.44), channel_id=1, source_target_pairs={{0,5},{1,13},{2,7},{3,15},{4,4},{5,12},{6,6},{7,14},{8,1},{9,9},{1... | collective-permute-start | bytes 1572872 | tf_op jit(solution)/shard_map/ppermute | solution.py:84
  134.9 1.1 copy-start.17
  134.9 3.1 %collective-permute-start.8 = (bf16[2,2,256,512]{3,2,1,0:T(8,128)(2,1)}, bf16[2,2,256,512]{3,2,1,0:T(8,128)(2,1)}, u32[]{:S(2)}, u32[]{:S(2)}) collective-permute-start(bf16[2,2,256,512]{3,2,1,0:T(8,128)(2,1)} %collective-permute-done.3.refs_7_), channel_id=1, source_target_pairs={{0,1},{1,0},{2,3},{3,2},{4,5},{5,4},{6,7},{7,6},{8,9},{9,8},{10,11... | collective-permute-start | bytes 3145736 | tf_op jit(solution)/shard_map/ppermute | solution.py:92
  134.9 7.1 %collective-permute-start.21 = (bf16[2,2,256,512]{3,2,1,0:T(8,128)(2,1)}, bf16[2,2,256,512]{3,2,1,0:T(8,128)(2,1)}, u32[]{:S(2)}, u32[]{:S(2)}) collective-permute-start(bf16[2,2,256,512]{3,2,1,0:T(8,128)(2,1)} %collective-permute-done.16.refs_8_), channel_id=1, source_target_pairs={{0,1},{1,0},{2,3},{3,2},{4,5},{5,4},{6,7},{7,6},{8,9},{9,8},{10,11... | collective-permute-start | bytes 3145736 | tf_op jit(solution)/shard_map/ppermute | solution.py:92
  135.5 1.0 copy-start.6
  135.5 7.0 %collective-permute-start.13 = (bf16[2,2,256,512]{3,2,1,0:T(8,128)(2,1)}, bf16[2,2,256,512]{3,2,1,0:T(8,128)(2,1)}, u32[]{:S(2)}, u32[]{:S(2)}) collective-permute-start(bf16[2,2,256,512]{3,2,1,0:T(8,128)(2,1)} %collective-permute-done.12.refs_4_), channel_id=1, source_target_pairs={{0,1},{1,0},{2,3},{3,2},{4,5},{5,4},{6,7},{7,6},{8,9},{9,8},{10,11... | collective-permute-start | bytes 3145736 | tf_op jit(solution)/shard_map/ppermute | solution.py:92
  135.5 1.3 copy-start.7
  135.5 8.4 %collective-permute-start.15 = (bf16[2,2,256,512]{3,2,1,0:T(8,128)(2,1)}, bf16[2,2,256,512]{3,2,1,0:T(8,128)(2,1)}, u32[]{:S(2)}, u32[]{:S(2)}) collective-permute-start(bf16[2,2,256,512]{3,2,1,0:T(8,128)(2,1)} %collective-permute-done.14.refs_6_), channel_id=1, source_target_pairs={{0,1},{1,0},{2,3},{3,2},{4,5},{5,4},{6,7},{7,6},{8,9},{9,8},{10,11... | collective-permute-start | bytes 3145736 | tf_op jit(solution)/shard_map/ppermute | solution.py:92
  136.8 1.0 copy-start.8
  137.8 6.2 %collective-permute-start.11 = (bf16[2,2,256,512]{3,2,1,0:T(8,128)(2,1)}, bf16[2,2,256,512]{3,2,1,0:T(8,128)(2,1)S(1)}, u32[]{:S(2)}, u32[]{:S(2)}) collective-permute-start(bf16[2,2,256,512]{3,2,1,0:T(8,128)(2,1)} %pad_maximum_fusion.1.refs_2_), channel_id=1, source_target_pairs={{0,1},{1,0},{2,3},{3,2},{4,5},{5,4},{6,7},{7,6},{8,9},{9,8},{10,11... | collective-permute-start | bytes 3145736 | tf_op jit(solution)/shard_map/ppermute | solution.py:92
  143.9 1.0 copy-start.13
  165.0 52.5 %collective-permute-start.27 = (bf16[2,256,512]{2,1,0:T(8,128)(2,1)S(1)}, bf16[2,256,512]{2,1,0:T(8,128)(2,1)S(1)}, u32[]{:S(2)}, u32[]{:S(2)}) collective-permute-start(bf16[2,256,512]{2,1,0:T(8,128)(2,1)S(1)} %get-tuple-element.33.refs_4_), channel_id=1, source_target_pairs={{0,0},{8,1},{2,2},{10,3},{1,4},{9,5},{3,6},{11,7},{4,8},{12,9},{6,... | collective-permute-start | bytes 1572872 | tf_op jit(solution)/shard_map/ppermute | solution.py:88
  169.7 53.0 %collective-permute-start.28 = (bf16[2,256,512]{2,1,0:T(8,128)(2,1)S(1)}, bf16[2,256,512]{2,1,0:T(8,128)(2,1)S(1)}, u32[]{:S(2)}, u32[]{:S(2)}) collective-permute-start(bf16[2,256,512]{2,1,0:T(8,128)(2,1)S(1)} %get-tuple-element.34.refs_5_), channel_id=1, source_target_pairs={{1,0},{9,1},{3,2},{11,3},{0,4},{8,5},{2,6},{10,7},{5,8},{13,9},{7,... | collective-permute-start | bytes 1572872 | tf_op jit(solution)/shard_map/ppermute | solution.py:88
  175.7 47.3 %collective-permute-start.29 = (bf16[2,256,512]{2,1,0:T(8,128)(2,1)S(1)}, bf16[2,256,512]{2,1,0:T(8,128)(2,1)S(1)}, u32[]{:S(2)}, u32[]{:S(2)}) collective-permute-start(bf16[2,256,512]{2,1,0:T(8,128)(2,1)S(1)} %get-tuple-element.36.refs_6_), channel_id=1, source_target_pairs={{4,0},{12,1},{6,2},{14,3},{5,4},{13,5},{7,6},{15,7},{0,8},{8,9},{2... | collective-permute-start | bytes 1572872 | tf_op jit(solution)/shard_map/ppermute | solution.py:88
  187.4 39.0 %collective-permute-start.30 = (bf16[2,256,512]{2,1,0:T(8,128)(2,1)S(1)}, bf16[2,256,512]{2,1,0:T(8,128)(2,1)S(1)}, u32[]{:S(2)}, u32[]{:S(2)}) collective-permute-start(bf16[2,256,512]{2,1,0:T(8,128)(2,1)S(1)} %get-tuple-element.37.refs_7_), channel_id=1, source_target_pairs={{5,0},{13,1},{7,2},{15,3},{4,4},{12,5},{6,6},{14,7},{1,8},{9,9},{3... | collective-permute-start | bytes 1572872 | tf_op jit(solution)/shard_map/ppermute | solution.py:88
  191.8 1.2 collective-permute-start.22
  193.0 3.5 %collective-permute-start.23 = (f32[2]{0:T(128)S(1)}, f32[2]{0:T(128)S(1)}, u32[]{:S(2)}, u32[]{:S(2)}) collective-permute-start(f32[2]{0:T(128)S(1)} %add.90), channel_id=1, source_target_pairs={{0,16},{16,0},{1,17},{17,1},{2,18},{18,2},{3,19},{19,3},{4,20},{20... | collective-permute-start | bytes 32 | tf_op jit(solution)/shard_map/ppermute | solution.py:92
  196.5 3.5 %collective-permute-start.24 = (f32[2]{0:T(128)S(1)}, f32[2]{0:T(128)S(1)}, u32[]{:S(2)}, u32[]{:S(2)}) collective-permute-start(f32[2]{0:T(128)S(1)} %add.91), channel_id=1, source_target_pairs={{0,2},{2,0},{1,3},{3,1},{4,6},{6,4},{5,7},{7,5},{8,10},{10,8},{9,1... | collective-permute-start | bytes 32 | tf_op jit(solution)/shard_map/ppermute | solution.py:92
  200.1 4.8 %collective-permute-start.25 = (f32[2]{0:T(128)S(1)}, f32[2]{0:T(128)S(1)}, u32[]{:S(2)}, u32[]{:S(2)}) collective-permute-start(f32[2]{0:T(128)S(1)} %add.92), channel_id=1, source_target_pairs={{0,4},{4,0},{1,5},{5,1},{2,6},{6,2},{3,7},{7,3},{8,12},{12,8},{9,1... | collective-permute-start | bytes 32 | tf_op jit(solution)/shard_map/ppermute | solution.py:92
  204.9 7.6 %collective-permute-start.26 = (f32[2]{0:T(128)S(1)}, f32[2]{0:T(128)S(1)}, u32[]{:S(2)}, u32[]{:S(2)}) collective-permute-start(f32[2]{0:T(128)S(1)} %add.93), channel_id=1, source_target_pairs={{0,8},{8,0},{1,9},{9,1},{2,10},{10,2},{3,11},{11,3},{4,12},{12,4},... | collective-permute-start | bytes 32 | tf_op jit(solution)/shard_map/ppermute | solution.py:92
  215.6 14.1 %collective-permute-start.31 = (bf16[2,256,512]{2,1,0:T(8,128)(2,1)S(1)}, bf16[2,256,512]{2,1,0:T(8,128)(2,1)S(1)}, u32[]{:S(2)}, u32[]{:S(2)}) collective-permute-start(bf16[2,256,512]{2,1,0:T(8,128)(2,1)S(1)} %get-tuple-element.43), channel_id=1, source_target_pairs={{0,0},{8,1},{2,2},{10,3},{1,4},{9,5},{3,6},{11,7},{4,8},{12,9},{6,... | collective-permute-start | bytes 1572872 | tf_op jit(solution)/shard_map/ppermute | solution.py:88
  217.5 48.5 %collective-permute-start.32 = (bf16[2,256,512]{2,1,0:T(8,128)(2,1)S(1)}, bf16[2,256,512]{2,1,0:T(8,128)(2,1)S(1)}, u32[]{:S(2)}, u32[]{:S(2)}) collective-permute-start(bf16[2,256,512]{2,1,0:T(8,128)(2,1)S(1)} %get-tuple-element.42), channel_id=1, source_target_pairs={{1,0},{9,1},{3,2},{11,3},{0,4},{8,5},{2,6},{10,7},{5,8},{13,9},{7,... | collective-permute-start | bytes 1572872 | tf_op jit(solution)/shard_map/ppermute | solution.py:88
  222.7 43.4 %collective-permute-start.33 = (bf16[2,256,512]{2,1,0:T(8,128)(2,1)S(1)}, bf16[2,256,512]{2,1,0:T(8,128)(2,1)S(1)}, u32[]{:S(2)}, u32[]{:S(2)}) collective-permute-start(bf16[2,256,512]{2,1,0:T(8,128)(2,1)S(1)} %get-tuple-element.41), channel_id=1, source_target_pairs={{4,0},{12,1},{6,2},{14,3},{5,4},{13,5},{7,6},{15,7},{0,8},{8,9},{2... | collective-permute-start | bytes 1572872 | tf_op jit(solution)/shard_map/ppermute | solution.py:88
  223.0 43.7 %collective-permute-start.34 = (bf16[2,256,512]{2,1,0:T(8,128)(2,1)S(1)}, bf16[2,256,512]{2,1,0:T(8,128)(2,1)S(1)}, u32[]{:S(2)}, u32[]{:S(2)}) collective-permute-start(bf16[2,256,512]{2,1,0:T(8,128)(2,1)S(1)} %get-tuple-element.40), channel_id=1, source_target_pairs={{5,0},{13,1},{7,2},{15,3},{4,4},{12,5},{6,6},{14,7},{1,8},{9,9},{3... | collective-permute-start | bytes 1572872 | tf_op jit(solution)/shard_map/ppermute | solution.py:88
  226.6 3.6 %copy-start.3 = (bf16[2,4,256,512]{3,2,1,0:T(8,128)(2,1)}, bf16[2,4,256,512]{3,2,1,0:T(8,128)(2,1)S(1)}, u32[]{:S(2)}) copy-start(bf16[2,4,256,512]{3,2,1,0:T(8,128)(2,1)S(1)} %fusion.15) | copy-start | bytes 6291460
  266.9 2.0 copy-start.2

commit v5 on v4

--- a/solution.py
+++ b/solution.py
@@ -162,45 +162,45 @@
 
 
 def collect_kernel(rows, width, where_ref, *refs):
-    a_in, (a_v, sems) = refs[:8], refs[8:]
-    copies = place_copies(GROUPS[0], a_in, (where_ref[0], where_ref[1]), a_v, sems, rows)
-    for t in range(4):
-        for copy in copies[t]:
-            copy.start()
+    a_in, x_refs, d_refs, refs = refs[:8], refs[8:12], refs[12:16], refs[16:]
+    a_v, wide_v, f_v, x_v, d_v, sems, x_sems, d_sems = refs
+    part = where_ref[1]
+    copies = place_copies(GROUPS[0], a_in, (where_ref[0], part), a_v, sems, rows)
+    x_copies = message_copies(x_refs, part, wide_v, x_v, x_sems, rows, width)
+    for k in range(4):
+        x_copies.append(pltpu.make_async_copy(d_refs[k], d_v.at[k], d_sems.at[k]))
+    for copy in copies[0] + x_copies + copies[1]:
+        copy.start()
+    for copy in x_copies:
+        copy.wait()
     for t in range(4):
         for copy in copies[t]:
             copy.wait()
-
-
-def residual_kernel(rows, width, where_ref, a_v, *refs):
-    b_in, x_refs, d_refs, refs = refs[:8], refs[8:12], refs[12:16], refs[16:]
-    b_v, r_v, rb_v, g0, g1, wide_v, x_v, d_v, g_v, b_sems, x_sems, d_sems, out_sems = refs
+        if t < 2:
+            for copy in copies[t + 2]:
+                copy.start()
+        forward = product(wide_v[part // 2 ^ t // 2], a_v, t, rows)
+        for i in range(2):
+            own = d_v[t, i].astype(jnp.float32) - x_v[t, i].astype(jnp.float32)
+            f_v[t, i] = own + forward[i]
+
+
+def residual_kernel(rows, width, where_ref, a_v, wide_v, f_v, *refs):
+    b_in, (b_v, r_v, rb_v, g0, g1, g_v, b_sems, out_sems) = refs[:8], refs[8:]
     where = (where_ref[0], where_ref[1])
     part = where[1]
     copies = place_copies(GROUPS[1], b_in, where, b_v, b_sems, rows)
-    x_copies = message_copies(x_refs, part, wide_v, x_v, x_sems, rows, width)
-    for k in range(4):
-        copies[0].append(pltpu.make_async_copy(d_refs[k], d_v.at[k], d_sems.at[k]))
-    copies[0] += [x_copies[3 * k + 2] for k in range(4)]
-    wide_copies = [x_copies[3 * k + i] for k in range(4) for i in range(2)]
-    for copy in wide_copies:
+    for copy in copies[0] + copies[1]:
         copy.start()
-    for copy in wide_copies:
-        copy.wait()
-    for t in range(4):
-        for copy in copies[t]:
-            copy.start()
-    for t in range(4):
-        forward = product(wide_v[part // 2 ^ t // 2], a_v, t, rows)
-        for i in range(2):
-            r_v[t, i] = forward[i]
     for t in range(4):
         for copy in copies[t]:
             copy.wait()
+        if t < 2:
+            for copy in copies[t + 2]:
+                copy.start()
         forward = product(wide_v[1 - (part // 2 ^ t // 2)], b_v, t, rows)
         for i in range(2):
-            own = d_v[t, i].astype(jnp.float32) - x_v[t, i].astype(jnp.float32)
-            residual = own + (r_v[t, i] + forward[i])
+            residual = f_v[t, i] + forward[i]
             r_v[t, i] = residual
             rb_v[t, i * rows : (i + 1) * rows, :] = residual.astype(jnp.bfloat16)
     gradient_blocks(0, part, a_v, b_v, r_v, rb_v, g_v, (g0, g1), out_sems, rows, width)
@@ -264,7 +264,7 @@
         return [pinned(pieces[at]) for at in OFFSETS]
 
     held[1][1, 2], _ = lax.optimization_barrier((held[1][1, 2], x_parts))
-    first_buffers = complete(held[0], held[0][1, 2])
+    first_buffers = complete(held[0], [held[0][1, 2], x_parts[1]])
     second_buffers = complete(held[1], first_buffers[3])
 
     hbm = pl.BlockSpec(memory_space=pltpu.HBM)
@@ -294,28 +294,26 @@
             name=name,
         )
 
-    data_a = call(
-        collect_kernel, "collect", 0.1, 2, [hbm] * 8, vmem, data_half, [dma((16,))]
-    )(where, *first_buffers)
+    data_a, x_wide, partial = call(
+        collect_kernel,
+        "collect",
+        0.5,
+        13,
+        [hbm] * 16,
+        [vmem] * 3,
+        [data_half, wide, f32_blocks],
+        [blocks, blocks, dma((16,)), dma((12,)), dma((4,))],
+    )(where, *first_buffers, *map(pinned, x_parts), *map(pinned, arrived))
     data_b, residual, res_rounded, g0, g1 = call(
         residual_kernel,
         "residual",
-        1.5,
-        16,
-        [vmem] + [hbm] * 16,
+        1.0,
+        11,
+        [vmem] * 3 + [hbm] * 8,
         [vmem] * 3 + [hbm] * 2,
         [data_half, f32_blocks, rounded, message, message],
-        [
-            wide,
-            blocks,
-            blocks,
-            two_messages,
-            dma((16,)),
-            dma((12,)),
-            dma((4,)),
-            dma((2,)),
-        ],
-    )(where, data_a, *second_buffers, *map(pinned, x_parts), *map(pinned, arrived))
+        [two_messages, dma((16,)), dma((2,))],
+    )(where, data_a, x_wide, partial, *second_buffers)
     g2, g3 = call(
         gradient_kernel,
         "gradient",

time: 271 us -> 268 us (0.989)
  starting transfers between devices: 66.3 us -> 70.8 us
  waiting for transfers between devices: 146 us -> 143 us
    ppermute x19, waiting for transfers between devices: 56.5 us -> 52.9 us  [swap(): return lax.ppermute(value, axis, [(0, 1), (1, 0)])]
    ppermute x8, starting transfers between devices: 18.6 us -> 21.4 us  [to_home(): return lax.ppermute(piece, COLUMN, send_pairs(k))]
  transfers between devices with their start and end apart: 35 -> 35, of which waited for: 18 -> 15; matrix products, arithmetic and copies ran while one was open for 2% -> 2% of each run, Pallas kernels for 8% -> 10%
where the time goes in v5:
time: 268 us; the launch traced here: 266 us
  waiting for transfers between devices  143 us (53%)
  starting transfers between devices  70.8 us (26%)
  Pallas kernels  38.5 us (14%)
  local copies, waits for them, and re-layouts  8.26 us (3%)
    ppermute x19, waiting for transfers between devices, swap(): return lax.ppermute(value, axis, [(0, 1), (1, 0)])  52.9 us
    ppermute x8, waiting for transfers between devices, to_home(): return lax.ppermute(piece, COLUMN, send_pairs(k))  52.1 us
    ppermute x8, waiting for transfers between devices, from_home(): return lax.ppermute(piece, COLUMN, [(b, a) for a, b in send_pairs(k)])  38.4 us
    ppermute x19, starting transfers between devices, swap(): return lax.ppermute(value, axis, [(0, 1), (1, 0)])  29.2 us
    ppermute x8, starting transfers between devices, to_home(): return lax.ppermute(piece, COLUMN, send_pairs(k))  21.4 us
    ppermute x8, starting transfers between devices, from_home(): return lax.ppermute(piece, COLUMN, [(b, a) for a, b in send_pairs(k)])  20.2 us
    pallas_call x1, Pallas kernels, whole_rows(): call(residual_kernel, 'residual', 1.0, 11, [vmem] * 3 + [hbm] * 8, [vmem]...  11.8 us
    pallas_call x1, Pallas kernels, whole_rows(): call(change_kernel, 'change', 1.0, 12, [vmem] * 3 + [hbm] * 4, [vmem, sme...  11.7 us
  transfers between devices with their start and end apart: 35, of which 15 were waited for; matrix products, arithmetic and copies ran while one was open for 2% of the time, Pallas kernels for 10%

profile of v5, /device:TPU:20, one launch (start us, length us, event | category | flops | bytes accessed | tf_op | source)
XLA Modules:
  0.0 266.1 jit_solution(5317795343006798164)
XLA Ops:
  0.7 1.7 dynamic-slice_bitcast_fusion.5
  2.3 2.4 collective-permute-start
  4.7 0.8 collective-permute-start.1
  5.5 1.9 collective-permute-start.4
  7.3 2.9 %collective-permute-start.5 = (bf16[2,256,512]{2,1,0:T(8,128)(2,1)S(1)}, bf16[2,256,512]{2,1,0:T(8,128)(2,1)S(1)}, u32[]{:S(2)}, u32[]{:S(2)}) collective-permute-start(bf16[2,256,512]{2,1,0:T(8,128)(2,1)S(1)} %get-tuple-element.55), channel_id=1, source_target_pairs={{0,5},{1,13},{2,7},{3,15},{4,4},{5,12},{6,6},{7,14},{8,1},{9,9},{1... | collective-permute-start | bytes 1572872 | tf_op jit(solution)/shard_map/ppermute | solution.py:84
  10.2 8.4 %collective-permute-done.refs_13_ = bf16[2,256,512]{2,1,0:T(8,128)(2,1)S(1)} collective-permute-done((bf16[2,256,512]{2,1,0:T(8,128)(2,1)S(1)}, bf16[2,256,512]{2,1,0:T(8,128)(2,1)S(1)}, u32[]{:S(2)}, u32[]{:S(2)}) %collective-permute-start) | collective-permute-done | bytes 524320 | tf_op jit(solution)/shard_map/ppermute | solution.py:84
  18.6 10.2 %collective-permute-done.1.refs_14_ = bf16[2,256,512]{2,1,0:T(8,128)(2,1)S(1)} collective-permute-done((bf16[2,256,512]{2,1,0:T(8,128)(2,1)S(1)}, bf16[2,256,512]{2,1,0:T(8,128)(2,1)S(1)}, u32[]{:S(2)}, u32[]{:S(2)}) %collective-permute-start.1) | collective-permute-done | bytes 524320 | tf_op jit(solution)/shard_map/ppermute | solution.py:84
  29.0 1.6 collective-permute-start.10
  30.5 10.9 %collective-permute-done.4.refs_15_ = bf16[2,256,512]{2,1,0:T(8,128)(2,1)S(1)} collective-permute-done((bf16[2,256,512]{2,1,0:T(8,128)(2,1)S(1)}, bf16[2,256,512]{2,1,0:T(8,128)(2,1)S(1)}, u32[]{:S(2)}, u32[]{:S(2)}) %collective-permute-start.4) | collective-permute-done | bytes 524320 | tf_op jit(solution)/shard_map/ppermute | solution.py:84
  41.4 9.3 %collective-permute-done.5.refs_16_ = bf16[2,256,512]{2,1,0:T(8,128)(2,1)S(1)} collective-permute-done((bf16[2,256,512]{2,1,0:T(8,128)(2,1)S(1)}, bf16[2,256,512]{2,1,0:T(8,128)(2,1)S(1)}, u32[]{:S(2)}, u32[]{:S(2)}) %collective-permute-start.5) | collective-permute-done | bytes 524320 | tf_op jit(solution)/shard_map/ppermute | solution.py:84
  50.9 1.6 collective-permute-start.6
  52.4 2.4 collective-permute-start.14
  54.8 18.2 %collective-permute-done.2.refs_3_ = bf16[2,2,256,512]{3,2,1,0:T(8,128)(2,1)S(1)} collective-permute-done((bf16[2,2,256,512]{3,2,1,0:T(8,128)(2,1)S(1)}, bf16[2,2,256,512]{3,2,1,0:T(8,128)(2,1)S(1)}, u32[]{:S(2)}, u32[]{:S(2)}) %collective-permute-start.2) | collective-permute-done | bytes 1048608 | tf_op jit(solution)/shard_map/ppermute | solution.py:92
  73.0 1.5 collective-permute-start.3
  74.6 3.5 %collective-permute-start.13 = (bf16[2,256,512]{2,1,0:T(8,128)(2,1)S(1)}, bf16[2,256,512]{2,1,0:T(8,128)(2,1)S(1)}, u32[]{:S(2)}, u32[]{:S(2)}) collective-permute-start(bf16[2,256,512]{2,1,0:T(8,128)(2,1)S(1)} %dynamic-slice_bitcast_fusion.2), channel_id=1, source_target_pairs={{0,0},{1,8},{2,2},{3,10},{4,1},{5,9},{6,3},{7,11},{8,4},{9,12},{10... | collective-permute-start | bytes 1572872 | tf_op jit(solution)/shard_map/ppermute | solution.py:84
  78.1 0.8 collective-permute-start.7
  78.9 16.6 %collective-permute-done.14.refs_6_ = bf16[2,2,256,512]{3,2,1,0:T(8,128)(2,1)} collective-permute-done((bf16[2,2,256,512]{3,2,1,0:T(8,128)(2,1)S(1)}, bf16[2,2,256,512]{3,2,1,0:T(8,128)(2,1)}, u32[]{:S(2)}, u32[]{:S(2)}) %collective-permute-start.14) | collective-permute-done | bytes 1048608 | tf_op jit(solution)/shard_map/ppermute | solution.py:92
  95.6 3.6 %collective-permute-start.15 = (bf16[2,256,512]{2,1,0:T(8,128)(2,1)S(1)}, bf16[2,256,512]{2,1,0:T(8,128)(2,1)S(1)}, u32[]{:S(2)}, u32[]{:S(2)}) collective-permute-start(bf16[2,256,512]{2,1,0:T(8,128)(2,1)S(1)} %get-tuple-element.51), channel_id=1, source_target_pairs={{0,4},{1,12},{2,6},{3,14},{4,5},{5,13},{6,7},{7,15},{8,0},{9,8},{1... | collective-permute-start | bytes 1572872 | tf_op jit(solution)/shard_map/ppermute | solution.py:84
  99.2 1.5 collective-permute-start.20
  100.7 1.3 collective-permute-done.7.refs_10_
  102.0 0.8 copy-done.15
  102.8 16.1 %collective-permute-start.9 = (bf16[2,2,256,512]{3,2,1,0:T(8,128)(2,1)S(1)}, bf16[2,2,256,512]{3,2,1,0:T(8,128)(2,1)S(1)}, u32[]{:S(2)}, u32[]{:S(2)}) collective-permute-start(bf16[2,2,256,512]{3,2,1,0:T(8,128)(2,1)S(1)} %collective-permute-done.2.refs_3_), channel_id=1, source_target_pairs={{0,1},{1,0},{2,3},{3,2},{4,5},{5,4},{6,7},{7,6},{8,9},{9,8},{10,11... | collective-permute-start | bytes 3145736 | tf_op jit(solution)/shard_map/ppermute | solution.py:92
  119.0 0.5 collective-permute-start.8
  119.5 5.6 %collective-permute-start.16 = (bf16[2,256,512]{2,1,0:T(8,128)(2,1)S(1)}, bf16[2,256,512]{2,1,0:T(8,128)(2,1)S(1)}, u32[]{:S(2)}, u32[]{:S(2)}) collective-permute-start(bf16[2,256,512]{2,1,0:T(8,128)(2,1)S(1)} %get-tuple-element.50), channel_id=1, source_target_pairs={{0,5},{1,13},{2,7},{3,15},{4,4},{5,12},{6,6},{7,14},{8,1},{9,9},{1... | collective-permute-start | bytes 1572872 | tf_op jit(solution)/shard_map/ppermute | solution.py:84
  125.1 12.1 %collective-permute-done.16.refs_12_ = bf16[2,256,512]{2,1,0:T(8,128)(2,1)S(1)} collective-permute-done((bf16[2,256,512]{2,1,0:T(8,128)(2,1)S(1)}, bf16[2,256,512]{2,1,0:T(8,128)(2,1)S(1)}, u32[]{:S(2)}, u32[]{:S(2)}) %collective-permute-start.16) | collective-permute-done | bytes 524320 | tf_op jit(solution)/shard_map/ppermute | solution.py:84
  137.2 0.5 collective-permute-start.21
  137.8 0.4 collective-permute-start.19
  138.3 0.4 copy-done.11
  138.7 0.3 copy-done.12
  139.0 1.0 copy-done.13
  140.0 0.2 collective-permute-start.17
  140.3 9.9 %collect.1 = (bf16[4,2,1024,512]{3,2,1,0:T(8,128)(2,1)S(1)}, bf16[2,512,1024]{2,1,0:T(8,128)(2,1)S(1)}, f32[4,2,256,512]{3,2,1,0:T(8,128)S(1)}) custom-call(s32[2]{0:T(128)S(1)} %pad_add_fusion.refs_0_, bf16[2,2,256,512]{3,2,1,0:T(8,128)(2,1)} %copy-done.4, bf16[2,2,256,512]{3,2,1,0:T(8,128)(2,1)} %copy-done.13, bf16[2,2,256,512]{3,2,1,0:T(8,128)(2,1)} %copy-done.9, ...), custom_call_target="tpu_custom_call" | custom-call | flops 4294967296 | bytes 16777216 | tf_op jit(solution)/shard_map/collect/pallas_call | solution.py:297
  150.2 11.8 %residual.1 = (bf16[4,2,1024,512]{3,2,1,0:T(8,128)(2,1)S(1)}, f32[4,2,256,512]{3,2,1,0:T(8,128)S(1)}, bf16[4,512,512]{2,1,0:T(8,128)(2,1)S(1)}, bf16[2,256,512]{2,1,0:T(8,128)(2,1)S(1)}, bf16[2,256,512]{2,1,0:T(8,128)(2,1)S(1)}) custom-call(s32[2]{0:T(128)S(1)} %pad_add_fusion.refs_0_, bf16[4,2,1024,512]{3,2,1,0:T(8,128)(2,1)S(1)} %get-tuple-element.30.refs_1_, ...), custom_call_target="tpu_custom_call" | custom-call | flops 8589934592 | bytes 16777216 | tf_op jit(solution)/shard_map/residual/pallas_call | solution.py:307
  162.0 4.7 %collective-permute-start.27 = (bf16[2,256,512]{2,1,0:T(8,128)(2,1)S(1)}, bf16[2,256,512]{2,1,0:T(8,128)(2,1)S(1)}, u32[]{:S(2)}, u32[]{:S(2)}) collective-permute-start(bf16[2,256,512]{2,1,0:T(8,128)(2,1)S(1)} %get-tuple-element.39.refs_4_), channel_id=1, source_target_pairs={{0,0},{8,1},{2,2},{10,3},{1,4},{9,5},{3,6},{11,7},{4,8},{12,9},{6,... | collective-permute-start | bytes 1572872 | tf_op jit(solution)/shard_map/ppermute | solution.py:88
  166.7 0.3 collective-permute-start.28
  167.0 5.2 %gradient.1 = (bf16[2,256,512]{2,1,0:T(8,128)(2,1)S(1)}, bf16[2,256,512]{2,1,0:T(8,128)(2,1)S(1)}) custom-call(s32[2]{0:T(128)S(1)} %pad_add_fusion.refs_0_, bf16[4,2,1024,512]{3,2,1,0:T(8,128)(2,1)S(1)} %get-tuple-element.30.refs_1_, bf16[4,2,1024,512]{3,2,1,0:T(8,128)(2,1)S(1)} %get-tuple-element.37.refs_2_, ...), custom_call_target="tpu_custom_call" | custom-call | flops 4294967296 | bytes 16777216 | tf_op jit(solution)/shard_map/gradient/pallas_call | solution.py:317
  172.2 0.2 collective-permute-start.29
  172.4 11.7 %change.1 = (f32[4,2,256,512]{3,2,1,0:T(8,128)S(1)}, f32[2]{0:T(128)S(1)}) custom-call(s32[2]{0:T(128)S(1)} %pad_add_fusion.refs_0_, bf16[4,2,1024,512]{3,2,1,0:T(8,128)(2,1)S(1)} %get-tuple-element.30.refs_1_, bf16[4,2,1024,512]{3,2,1,0:T(8,128)(2,1)S(1)} %get-tuple-element.37.refs_2_, f32[4,2,256,512]{3,2,1,0:T(8,128)S(1)} %get-tuple-element.38.refs_3_, ...), custom_call_target="tpu_custom_call" | custom-call | flops 8589934592 | bytes 16777216 | tf_op jit(solution)/shard_map/change/pallas_call | solution.py:329
  184.1 4.7 %collective-permute-start.30 = (bf16[2,256,512]{2,1,0:T(8,128)(2,1)S(1)}, bf16[2,256,512]{2,1,0:T(8,128)(2,1)S(1)}, u32[]{:S(2)}, u32[]{:S(2)}) collective-permute-start(bf16[2,256,512]{2,1,0:T(8,128)(2,1)S(1)} %get-tuple-element.43.refs_7_), channel_id=1, source_target_pairs={{5,0},{13,1},{7,2},{15,3},{4,4},{12,5},{6,6},{14,7},{1,8},{9,9},{3... | collective-permute-start | bytes 1572872 | tf_op jit(solution)/shard_map/ppermute | solution.py:88
  188.9 1.1 collective-permute-done.22
  190.0 1.5 collective-permute-start.23
  191.5 2.1 collective-permute-done.23
  193.5 0.5 collective-permute-start.24
  194.0 3.0 %collective-permute-done.24 = f32[2]{0:T(128)S(1)} collective-permute-done((f32[2]{0:T(128)S(1)}, f32[2]{0:T(128)S(1)}, u32[]{:S(2)}, u32[]{:S(2)}) %collective-permute-start.24) | collective-permute-done | bytes 40 | tf_op jit(solution)/shard_map/ppermute | solution.py:92
  197.1 0.3 collective-permute-start.25
  197.4 4.0 %collective-permute-done.25 = f32[2]{0:T(128)S(1)} collective-permute-done((f32[2]{0:T(128)S(1)}, f32[2]{0:T(128)S(1)}, u32[]{:S(2)}, u32[]{:S(2)}) %collective-permute-start.25) | collective-permute-done | bytes 40 | tf_op jit(solution)/shard_map/ppermute | solution.py:92
  201.3 0.3 collective-permute-start.26
  201.7 8.0 %collective-permute-done.26 = f32[2]{0:T(128)S(1)} collective-permute-done((f32[2]{0:T(128)S(1)}, f32[2]{0:T(128)S(1)}, u32[]{:S(2)}, u32[]{:S(2)}) %collective-permute-start.26) | collective-permute-done | bytes 40 | tf_op jit(solution)/shard_map/ppermute | solution.py:92
  209.6 0.6 fusion.16
  211.5 1.2 fusion.7
  212.7 1.9 collective-permute-start.31
  214.7 5.2 %collective-permute-start.32 = (bf16[2,256,512]{2,1,0:T(8,128)(2,1)S(1)}, bf16[2,256,512]{2,1,0:T(8,128)(2,1)S(1)}, u32[]{:S(2)}, u32[]{:S(2)}) collective-permute-start(bf16[2,256,512]{2,1,0:T(8,128)(2,1)S(1)} %get-tuple-element.48), channel_id=1, source_target_pairs={{1,0},{9,1},{3,2},{11,3},{0,4},{8,5},{2,6},{10,7},{5,8},{13,9},{7,... | collective-permute-start | bytes 1572872 | tf_op jit(solution)/shard_map/ppermute | solution.py:88
  219.9 0.2 broadcast_in_dim.44
  220.1 0.2 fusion.9
  220.3 0.2 fusion.11
  220.5 3.1 %collective-permute-start.34 = (bf16[2,256,512]{2,1,0:T(8,128)(2,1)S(1)}, bf16[2,256,512]{2,1,0:T(8,128)(2,1)S(1)}, u32[]{:S(2)}, u32[]{:S(2)}) collective-permute-start(bf16[2,256,512]{2,1,0:T(8,128)(2,1)S(1)} %get-tuple-element.46), channel_id=1, source_target_pairs={{5,0},{13,1},{7,2},{15,3},{4,4},{12,5},{6,6},{14,7},{1,8},{9,9},{3... | collective-permute-start | bytes 1572872 | tf_op jit(solution)/shard_map/ppermute | solution.py:88
  223.6 0.2 fusion.13
  223.8 0.1 copy.20
  224.0 0.2 fusion.15
  224.2 2.4 collective-permute-done.31
  226.6 0.5 broadcast_in_dim.49
  227.3 36.0 %collective-permute-done.32 = bf16[2,256,512]{2,1,0:T(8,128)(2,1)S(1)} collective-permute-done((bf16[2,256,512]{2,1,0:T(8,128)(2,1)S(1)}, bf16[2,256,512]{2,1,0:T(8,128)(2,1)S(1)}, u32[]{:S(2)}, u32[]{:S(2)}) %collective-permute-start.32) | collective-permute-done | bytes 524320 | tf_op jit(solution)/shard_map/ppermute | solution.py:88
  263.5 0.4 copy.22
  264.1 2.0 copy-done.1
  (72 shorter events, 1.4 us)
Async XLA Ops:
  2.3 16.3 %collective-permute-start = (bf16[2,256,512]{2,1,0:T(8,128)(2,1)S(1)}, bf16[2,256,512]{2,1,0:T(8,128)(2,1)S(1)}, u32[]{:S(2)}, u32[]{:S(2)}) collective-permute-start(bf16[2,256,512]{2,1,0:T(8,128)(2,1)S(1)} %get-tuple-element.54), channel_id=1, source_target_pairs={{0,0},{1,8},{2,2},{3,10},{4,1},{5,9},{6,3},{7,11},{8,4},{9,12},{10... | collective-permute-start | bytes 1572872 | tf_op jit(solution)/shard_map/ppermute | solution.py:84
  4.7 24.1 %collective-permute-start.1 = (bf16[2,256,512]{2,1,0:T(8,128)(2,1)S(1)}, bf16[2,256,512]{2,1,0:T(8,128)(2,1)S(1)}, u32[]{:S(2)}, u32[]{:S(2)}) collective-permute-start(bf16[2,256,512]{2,1,0:T(8,128)(2,1)S(1)} %get-tuple-element.53), channel_id=1, source_target_pairs={{0,1},{1,9},{2,3},{3,11},{4,0},{5,8},{6,2},{7,10},{8,5},{9,13},{10... | collective-permute-start | bytes 1572872 | tf_op jit(solution)/shard_map/ppermute | solution.py:84
  5.5 35.9 %collective-permute-start.4 = (bf16[2,256,512]{2,1,0:T(8,128)(2,1)S(1)}, bf16[2,256,512]{2,1,0:T(8,128)(2,1)S(1)}, u32[]{:S(2)}, u32[]{:S(2)}) collective-permute-start(bf16[2,256,512]{2,1,0:T(8,128)(2,1)S(1)} %get-tuple-element.52), channel_id=1, source_target_pairs={{0,4},{1,12},{2,6},{3,14},{4,5},{5,13},{6,7},{7,15},{8,0},{9,8},{1... | collective-permute-start | bytes 1572872 | tf_op jit(solution)/shard_map/ppermute | solution.py:84
  7.3 43.4 %collective-permute-start.5 = (bf16[2,256,512]{2,1,0:T(8,128)(2,1)S(1)}, bf16[2,256,512]{2,1,0:T(8,128)(2,1)S(1)}, u32[]{:S(2)}, u32[]{:S(2)}) collective-permute-start(bf16[2,256,512]{2,1,0:T(8,128)(2,1)S(1)} %get-tuple-element.55), channel_id=1, source_target_pairs={{0,5},{1,13},{2,7},{3,15},{4,4},{5,12},{6,6},{7,14},{8,1},{9,9},{1... | collective-permute-start | bytes 1572872 | tf_op jit(solution)/shard_map/ppermute | solution.py:84
  18.6 32.2 %copy-start.5 = (bf16[2,256,512]{2,1,0:T(8,128)(2,1)}, bf16[2,256,512]{2,1,0:T(8,128)(2,1)S(1)}, u32[]{:S(2)}) copy-start(bf16[2,256,512]{2,1,0:T(8,128)(2,1)S(1)} %collective-permute-done.refs_13_) | copy-start | bytes 1572868
  28.8 22.1 %copy-start.6 = (bf16[2,256,512]{2,1,0:T(8,128)(2,1)}, bf16[2,256,512]{2,1,0:T(8,128)(2,1)S(1)}, u32[]{:S(2)}) copy-start(bf16[2,256,512]{2,1,0:T(8,128)(2,1)S(1)} %collective-permute-done.1.refs_14_) | copy-start | bytes 1572868
  28.8 45.8 %copy-start = (bf16[2,1,1024,512]{3,2,1,0:T(8,128)(2,1)S(1)}, bf16[2,1,1024,512]{3,2,1,0:T(8,128)(2,1)}, u32[]{:S(2)}) copy-start(bf16[2,1,1024,512]{3,2,1,0:T(8,128)(2,1)} %param.3) | copy-start | bytes 6291460
  28.9 90.1 %copy-start.4 = (bf16[2,2,256,512]{3,2,1,0:T(8,128)(2,1)}, bf16[2,2,256,512]{3,2,1,0:T(8,128)(2,1)S(1)}, u32[]{:S(2)}) copy-start(bf16[2,2,256,512]{3,2,1,0:T(8,128)(2,1)S(1)} %pad_maximum_fusion.refs_1_) | copy-start | bytes 3145732
  28.9 44.1 %collective-permute-start.2 = (bf16[2,2,256,512]{3,2,1,0:T(8,128)(2,1)S(1)}, bf16[2,2,256,512]{3,2,1,0:T(8,128)(2,1)S(1)}, u32[]{:S(2)}, u32[]{:S(2)}) collective-permute-start(bf16[2,2,256,512]{3,2,1,0:T(8,128)(2,1)S(1)} %pad_maximum_fusion.refs_1_), channel_id=1, source_target_pairs={{0,4},{4,0},{1,5},{5,1},{2,6},{6,2},{3,7},{7,3},{8,12},{12,8},{9,1... | collective-permute-start | bytes 3145736 | tf_op jit(solution)/shard_map/ppermute | solution.py:92
  29.0 45.6 %collective-permute-start.10 = (bf16[2,2,256,512]{3,2,1,0:T(8,128)(2,1)S(1)}, bf16[2,2,256,512]{3,2,1,0:T(8,128)(2,1)S(1)}, u32[]{:S(2)}, u32[]{:S(2)}) collective-permute-start(bf16[2,2,256,512]{3,2,1,0:T(8,128)(2,1)S(1)} %pad_maximum_fusion.refs_1_), channel_id=1, source_target_pairs={{0,16},{16,0},{1,17},{17,1},{2,18},{18,2},{3,19},{19,3},{4,20},{20... | collective-permute-start | bytes 3145736 | tf_op jit(solution)/shard_map/ppermute | solution.py:92
  41.4 36.7 %copy-start.7 = (bf16[2,256,512]{2,1,0:T(8,128)(2,1)}, bf16[2,256,512]{2,1,0:T(8,128)(2,1)S(1)}, u32[]{:S(2)}) copy-start(bf16[2,256,512]{2,1,0:T(8,128)(2,1)S(1)} %collective-permute-done.4.refs_15_) | copy-start | bytes 1572868
  50.7 27.4 %copy-start.8 = (bf16[2,256,512]{2,1,0:T(8,128)(2,1)}, bf16[2,256,512]{2,1,0:T(8,128)(2,1)S(1)}, u32[]{:S(2)}) copy-start(bf16[2,256,512]{2,1,0:T(8,128)(2,1)S(1)} %collective-permute-done.5.refs_16_) | copy-start | bytes 1572868
  50.9 87.4 %copy-start.3 = (bf16[2,2,256,512]{3,2,1,0:T(8,128)(2,1)}, bf16[2,2,256,512]{3,2,1,0:T(8,128)(2,1)S(1)}, u32[]{:S(2)}) copy-start(bf16[2,2,256,512]{3,2,1,0:T(8,128)(2,1)S(1)} %pad_maximum_fusion.1.refs_4_) | copy-start | bytes 3145732
  50.9 27.2 %collective-permute-start.6 = (bf16[2,2,256,512]{3,2,1,0:T(8,128)(2,1)S(1)}, bf16[2,2,256,512]{3,2,1,0:T(8,128)(2,1)}, u32[]{:S(2)}, u32[]{:S(2)}) collective-permute-start(bf16[2,2,256,512]{3,2,1,0:T(8,128)(2,1)S(1)} %pad_maximum_fusion.1.refs_4_), channel_id=1, source_target_pairs={{0,16},{16,0},{1,17},{17,1},{2,18},{18,2},{3,19},{19,3},{4,20},{20... | collective-permute-start | bytes 3145736 | tf_op jit(solution)/shard_map/ppermute | solution.py:92
  52.4 43.1 %collective-permute-start.14 = (bf16[2,2,256,512]{3,2,1,0:T(8,128)(2,1)S(1)}, bf16[2,2,256,512]{3,2,1,0:T(8,128)(2,1)}, u32[]{:S(2)}, u32[]{:S(2)}) collective-permute-start(bf16[2,2,256,512]{3,2,1,0:T(8,128)(2,1)S(1)} %pad_maximum_fusion.1.refs_4_), channel_id=1, source_target_pairs={{0,4},{4,0},{1,5},{5,1},{2,6},{6,2},{3,7},{7,3},{8,12},{12,8},{9,1... | collective-permute-start | bytes 3145736 | tf_op jit(solution)/shard_map/ppermute | solution.py:92
  73.0 29.7 %copy-start.9 = (bf16[2,2,256,512]{3,2,1,0:T(8,128)(2,1)}, bf16[2,2,256,512]{3,2,1,0:T(8,128)(2,1)S(1)}, u32[]{:S(2)}) copy-start(bf16[2,2,256,512]{3,2,1,0:T(8,128)(2,1)S(1)} %collective-permute-done.2.refs_3_) | copy-start | bytes 3145732
  73.0 29.7 %collective-permute-start.3 = (bf16[2,2,256,512]{3,2,1,0:T(8,128)(2,1)S(1)}, bf16[2,2,256,512]{3,2,1,0:T(8,128)(2,1)}, u32[]{:S(2)}, u32[]{:S(2)}) collective-permute-start(bf16[2,2,256,512]{3,2,1,0:T(8,128)(2,1)S(1)} %collective-permute-done.2.refs_3_), channel_id=1, source_target_pairs={{0,16},{16,0},{1,17},{17,1},{2,18},{18,2},{3,19},{19,3},{4,20},{20... | collective-permute-start | bytes 3145736 | tf_op jit(solution)/shard_map/ppermute | solution.py:92
  74.5 44.4 %copy-start.10 = (bf16[2,2,256,512]{3,2,1,0:T(8,128)(2,1)}, bf16[2,2,256,512]{3,2,1,0:T(8,128)(2,1)S(1)}, u32[]{:S(2)}) copy-start(bf16[2,2,256,512]{3,2,1,0:T(8,128)(2,1)S(1)} %collective-permute-done.10.refs_5_) | copy-start | bytes 3145732
  74.6 44.4 %collective-permute-start.13 = (bf16[2,256,512]{2,1,0:T(8,128)(2,1)S(1)}, bf16[2,256,512]{2,1,0:T(8,128)(2,1)S(1)}, u32[]{:S(2)}, u32[]{:S(2)}) collective-permute-start(bf16[2,256,512]{2,1,0:T(8,128)(2,1)S(1)} %dynamic-slice_bitcast_fusion.2), channel_id=1, source_target_pairs={{0,0},{1,8},{2,2},{3,10},{4,1},{5,9},{6,3},{7,11},{8,4},{9,12},{10... | collective-permute-start | bytes 1572872 | tf_op jit(solution)/shard_map/ppermute | solution.py:84
  78.1 23.8 %collective-permute-start.7 = (bf16[2,256,512]{2,1,0:T(8,128)(2,1)S(1)}, bf16[2,256,512]{2,1,0:T(8,128)(2,1)S(1)}, u32[]{:S(2)}, u32[]{:S(2)}) collective-permute-start(bf16[2,256,512]{2,1,0:T(8,128)(2,1)S(1)} %dynamic-slice_bitcast_fusion.3), channel_id=1, source_target_pairs={{0,1},{1,9},{2,3},{3,11},{4,0},{5,8},{6,2},{7,10},{8,5},{9,13},{10... | collective-permute-start | bytes 1572872 | tf_op jit(solution)/shard_map/ppermute | solution.py:84
  95.6 23.9 %collective-permute-start.15 = (bf16[2,256,512]{2,1,0:T(8,128)(2,1)S(1)}, bf16[2,256,512]{2,1,0:T(8,128)(2,1)S(1)}, u32[]{:S(2)}, u32[]{:S(2)}) collective-permute-start(bf16[2,256,512]{2,1,0:T(8,128)(2,1)S(1)} %get-tuple-element.51), channel_id=1, source_target_pairs={{0,4},{1,12},{2,6},{3,14},{4,5},{5,13},{6,7},{7,15},{8,0},{9,8},{1... | collective-permute-start | bytes 1572872 | tf_op jit(solution)/shard_map/ppermute | solution.py:84
  99.2 38.0 %collective-permute-start.20 = (bf16[2,2,256,512]{3,2,1,0:T(8,128)(2,1)}, bf16[2,2,256,512]{3,2,1,0:T(8,128)(2,1)}, u32[]{:S(2)}, u32[]{:S(2)}) collective-permute-start(bf16[2,2,256,512]{3,2,1,0:T(8,128)(2,1)} %collective-permute-done.14.refs_6_), channel_id=1, source_target_pairs={{0,16},{16,0},{1,17},{17,1},{2,18},{18,2},{3,19},{19,3},{4,20},{20... | collective-permute-start | bytes 3145736 | tf_op jit(solution)/shard_map/ppermute | solution.py:92
  102.0 0.8 copy-start.15
  102.8 35.0 %collective-permute-start.9 = (bf16[2,2,256,512]{3,2,1,0:T(8,128)(2,1)S(1)}, bf16[2,2,256,512]{3,2,1,0:T(8,128)(2,1)S(1)}, u32[]{:S(2)}, u32[]{:S(2)}) collective-permute-start(bf16[2,2,256,512]{3,2,1,0:T(8,128)(2,1)S(1)} %collective-permute-done.2.refs_3_), channel_id=1, source_target_pairs={{0,1},{1,0},{2,3},{3,2},{4,5},{5,4},{6,7},{7,6},{8,9},{9,8},{10,11... | collective-permute-start | bytes 3145736 | tf_op jit(solution)/shard_map/ppermute | solution.py:92
  118.9 18.9 %collective-permute-start.11 = (bf16[2,2,256,512]{3,2,1,0:T(8,128)(2,1)S(1)}, bf16[2,2,256,512]{3,2,1,0:T(8,128)(2,1)S(1)}, u32[]{:S(2)}, u32[]{:S(2)}) collective-permute-start(bf16[2,2,256,512]{3,2,1,0:T(8,128)(2,1)S(1)} %collective-permute-done.10.refs_5_), channel_id=1, source_target_pairs={{0,1},{1,0},{2,3},{3,2},{4,5},{5,4},{6,7},{7,6},{8,9},{9,8},{10,11... | collective-permute-start | bytes 3145736 | tf_op jit(solution)/shard_map/ppermute | solution.py:92
  119.0 19.3 %copy-start.14 = (bf16[2,256,512]{2,1,0:T(8,128)(2,1)}, bf16[2,256,512]{2,1,0:T(8,128)(2,1)S(1)}, u32[]{:S(2)}) copy-start(bf16[2,256,512]{2,1,0:T(8,128)(2,1)S(1)} %collective-permute-done.13.refs_9_) | copy-start | bytes 1572868
  119.0 19.2 %collective-permute-start.8 = (bf16[2,2,256,512]{3,2,1,0:T(8,128)(2,1)S(1)}, bf16[2,2,256,512]{3,2,1,0:T(8,128)(2,1)S(1)}, u32[]{:S(2)}, u32[]{:S(2)}) collective-permute-start(bf16[2,2,256,512]{3,2,1,0:T(8,128)(2,1)S(1)} %pad_maximum_fusion.refs_1_), channel_id=1, source_target_pairs={{0,1},{1,0},{2,3},{3,2},{4,5},{5,4},{6,7},{7,6},{8,9},{9,8},{10,11... | collective-permute-start | bytes 3145736 | tf_op jit(solution)/shard_map/ppermute | solution.py:92
  119.5 18.8 %copy-start.16 = (bf16[2,256,512]{2,1,0:T(8,128)(2,1)}, bf16[2,256,512]{2,1,0:T(8,128)(2,1)S(1)}, u32[]{:S(2)}) copy-start(bf16[2,256,512]{2,1,0:T(8,128)(2,1)S(1)} %collective-permute-done.15.refs_11_) | copy-start | bytes 1572868
  119.5 17.7 %collective-permute-start.16 = (bf16[2,256,512]{2,1,0:T(8,128)(2,1)S(1)}, bf16[2,256,512]{2,1,0:T(8,128)(2,1)S(1)}, u32[]{:S(2)}, u32[]{:S(2)}) collective-permute-start(bf16[2,256,512]{2,1,0:T(8,128)(2,1)S(1)} %get-tuple-element.50), channel_id=1, source_target_pairs={{0,5},{1,13},{2,7},{3,15},{4,4},{5,12},{6,6},{7,14},{8,1},{9,9},{1... | collective-permute-start | bytes 1572872 | tf_op jit(solution)/shard_map/ppermute | solution.py:84
  137.2 1.1 copy-start.17
  137.2 3.1 %collective-permute-start.12 = (bf16[2,2,256,512]{3,2,1,0:T(8,128)(2,1)}, bf16[2,2,256,512]{3,2,1,0:T(8,128)(2,1)}, u32[]{:S(2)}, u32[]{:S(2)}) collective-permute-start(bf16[2,2,256,512]{3,2,1,0:T(8,128)(2,1)} %collective-permute-done.3.refs_7_), channel_id=1, source_target_pairs={{0,1},{1,0},{2,3},{3,2},{4,5},{5,4},{6,7},{7,6},{8,9},{9,8},{10,11... | collective-permute-start | bytes 3145736 | tf_op jit(solution)/shard_map/ppermute | solution.py:92
  137.2 12.9 %collective-permute-start.21 = (bf16[2,2,256,512]{3,2,1,0:T(8,128)(2,1)}, bf16[2,2,256,512]{3,2,1,0:T(8,128)(2,1)}, u32[]{:S(2)}, u32[]{:S(2)}) collective-permute-start(bf16[2,2,256,512]{3,2,1,0:T(8,128)(2,1)} %collective-permute-done.20.refs_10_), channel_id=1, source_target_pairs={{0,1},{1,0},{2,3},{3,2},{4,5},{5,4},{6,7},{7,6},{8,9},{9,8},{10,11... | collective-permute-start | bytes 3145736 | tf_op jit(solution)/shard_map/ppermute | solution.py:92
  137.7 1.0 copy-start.11
  137.7 12.4 %collective-permute-start.18 = (bf16[2,2,256,512]{3,2,1,0:T(8,128)(2,1)}, bf16[2,2,256,512]{3,2,1,0:T(8,128)(2,1)}, u32[]{:S(2)}, u32[]{:S(2)}) collective-permute-start(bf16[2,2,256,512]{3,2,1,0:T(8,128)(2,1)} %collective-permute-done.14.refs_6_), channel_id=1, source_target_pairs={{0,1},{1,0},{2,3},{3,2},{4,5},{5,4},{6,7},{7,6},{8,9},{9,8},{10,11... | collective-permute-start | bytes 3145736 | tf_op jit(solution)/shard_map/ppermute | solution.py:92
  137.8 1.2 copy-start.12
  137.8 12.4 %collective-permute-start.19 = (bf16[2,2,256,512]{3,2,1,0:T(8,128)(2,1)}, bf16[2,2,256,512]{3,2,1,0:T(8,128)(2,1)}, u32[]{:S(2)}, u32[]{:S(2)}) collective-permute-start(bf16[2,2,256,512]{3,2,1,0:T(8,128)(2,1)} %collective-permute-done.6.refs_8_), channel_id=1, source_target_pairs={{0,1},{1,0},{2,3},{3,2},{4,5},{5,4},{6,7},{7,6},{8,9},{9,8},{10,11... | collective-permute-start | bytes 3145736 | tf_op jit(solution)/shard_map/ppermute | solution.py:92
  139.0 1.0 copy-start.13
  140.0 10.2 %collective-permute-start.17 = (bf16[2,2,256,512]{3,2,1,0:T(8,128)(2,1)S(1)}, bf16[2,2,256,512]{3,2,1,0:T(8,128)(2,1)}, u32[]{:S(2)}, u32[]{:S(2)}) collective-permute-start(bf16[2,2,256,512]{3,2,1,0:T(8,128)(2,1)S(1)} %pad_maximum_fusion.1.refs_4_), channel_id=1, source_target_pairs={{0,1},{1,0},{2,3},{3,2},{4,5},{5,4},{6,7},{7,6},{8,9},{9,8},{10,11... | collective-permute-start | bytes 3145736 | tf_op jit(solution)/shard_map/ppermute | solution.py:92
  162.0 52.7 %collective-permute-start.27 = (bf16[2,256,512]{2,1,0:T(8,128)(2,1)S(1)}, bf16[2,256,512]{2,1,0:T(8,128)(2,1)S(1)}, u32[]{:S(2)}, u32[]{:S(2)}) collective-permute-start(bf16[2,256,512]{2,1,0:T(8,128)(2,1)S(1)} %get-tuple-element.39.refs_4_), channel_id=1, source_target_pairs={{0,0},{8,1},{2,2},{10,3},{1,4},{9,5},{3,6},{11,7},{4,8},{12,9},{6,... | collective-permute-start | bytes 1572872 | tf_op jit(solution)/shard_map/ppermute | solution.py:88
  166.7 53.6 %collective-permute-start.28 = (bf16[2,256,512]{2,1,0:T(8,128)(2,1)S(1)}, bf16[2,256,512]{2,1,0:T(8,128)(2,1)S(1)}, u32[]{:S(2)}, u32[]{:S(2)}) collective-permute-start(bf16[2,256,512]{2,1,0:T(8,128)(2,1)S(1)} %get-tuple-element.40.refs_5_), channel_id=1, source_target_pairs={{1,0},{9,1},{3,2},{11,3},{0,4},{8,5},{2,6},{10,7},{5,8},{13,9},{7,... | collective-permute-start | bytes 1572872 | tf_op jit(solution)/shard_map/ppermute | solution.py:88
  172.2 48.3 %collective-permute-start.29 = (bf16[2,256,512]{2,1,0:T(8,128)(2,1)S(1)}, bf16[2,256,512]{2,1,0:T(8,128)(2,1)S(1)}, u32[]{:S(2)}, u32[]{:S(2)}) collective-permute-start(bf16[2,256,512]{2,1,0:T(8,128)(2,1)S(1)} %get-tuple-element.42.refs_6_), channel_id=1, source_target_pairs={{4,0},{12,1},{6,2},{14,3},{5,4},{13,5},{7,6},{15,7},{0,8},{8,9},{2... | collective-permute-start | bytes 1572872 | tf_op jit(solution)/shard_map/ppermute | solution.py:88
  184.1 39.9 %collective-permute-start.30 = (bf16[2,256,512]{2,1,0:T(8,128)(2,1)S(1)}, bf16[2,256,512]{2,1,0:T(8,128)(2,1)S(1)}, u32[]{:S(2)}, u32[]{:S(2)}) collective-permute-start(bf16[2,256,512]{2,1,0:T(8,128)(2,1)S(1)} %get-tuple-element.43.refs_7_), channel_id=1, source_target_pairs={{5,0},{13,1},{7,2},{15,3},{4,4},{12,5},{6,6},{14,7},{1,8},{9,9},{3... | collective-permute-start | bytes 1572872 | tf_op jit(solution)/shard_map/ppermute | solution.py:88
  188.8 1.2 collective-permute-start.22
  190.0 3.5 %collective-permute-start.23 = (f32[2]{0:T(128)S(1)}, f32[2]{0:T(128)S(1)}, u32[]{:S(2)}, u32[]{:S(2)}) collective-permute-start(f32[2]{0:T(128)S(1)} %add.90), channel_id=1, source_target_pairs={{0,16},{16,0},{1,17},{17,1},{2,18},{18,2},{3,19},{19,3},{4,20},{20... | collective-permute-start | bytes 32 | tf_op jit(solution)/shard_map/ppermute | solution.py:92
  193.5 3.5 %collective-permute-start.24 = (f32[2]{0:T(128)S(1)}, f32[2]{0:T(128)S(1)}, u32[]{:S(2)}, u32[]{:S(2)}) collective-permute-start(f32[2]{0:T(128)S(1)} %add.91), channel_id=1, source_target_pairs={{0,2},{2,0},{1,3},{3,1},{4,6},{6,4},{5,7},{7,5},{8,10},{10,8},{9,1... | collective-permute-start | bytes 32 | tf_op jit(solution)/shard_map/ppermute | solution.py:92
  197.1 4.3 %collective-permute-start.25 = (f32[2]{0:T(128)S(1)}, f32[2]{0:T(128)S(1)}, u32[]{:S(2)}, u32[]{:S(2)}) collective-permute-start(f32[2]{0:T(128)S(1)} %add.92), channel_id=1, source_target_pairs={{0,4},{4,0},{1,5},{5,1},{2,6},{6,2},{3,7},{7,3},{8,12},{12,8},{9,1... | collective-permute-start | bytes 32 | tf_op jit(solution)/shard_map/ppermute | solution.py:92
  201.3 8.3 %collective-permute-start.26 = (f32[2]{0:T(128)S(1)}, f32[2]{0:T(128)S(1)}, u32[]{:S(2)}, u32[]{:S(2)}) collective-permute-start(f32[2]{0:T(128)S(1)} %add.93), channel_id=1, source_target_pairs={{0,8},{8,0},{1,9},{9,1},{2,10},{10,2},{3,11},{11,3},{4,12},{12,4},... | collective-permute-start | bytes 32 | tf_op jit(solution)/shard_map/ppermute | solution.py:92
  212.7 13.9 %collective-permute-start.31 = (bf16[2,256,512]{2,1,0:T(8,128)(2,1)S(1)}, bf16[2,256,512]{2,1,0:T(8,128)(2,1)S(1)}, u32[]{:S(2)}, u32[]{:S(2)}) collective-permute-start(bf16[2,256,512]{2,1,0:T(8,128)(2,1)S(1)} %get-tuple-element.49), channel_id=1, source_target_pairs={{0,0},{8,1},{2,2},{10,3},{1,4},{9,5},{3,6},{11,7},{4,8},{12,9},{6,... | collective-permute-start | bytes 1572872 | tf_op jit(solution)/shard_map/ppermute | solution.py:88
  214.7 48.6 %collective-permute-start.32 = (bf16[2,256,512]{2,1,0:T(8,128)(2,1)S(1)}, bf16[2,256,512]{2,1,0:T(8,128)(2,1)S(1)}, u32[]{:S(2)}, u32[]{:S(2)}) collective-permute-start(bf16[2,256,512]{2,1,0:T(8,128)(2,1)S(1)} %get-tuple-element.48), channel_id=1, source_target_pairs={{1,0},{9,1},{3,2},{11,3},{0,4},{8,5},{2,6},{10,7},{5,8},{13,9},{7,... | collective-permute-start | bytes 1572872 | tf_op jit(solution)/shard_map/ppermute | solution.py:88
  220.3 43.1 %collective-permute-start.33 = (bf16[2,256,512]{2,1,0:T(8,128)(2,1)S(1)}, bf16[2,256,512]{2,1,0:T(8,128)(2,1)S(1)}, u32[]{:S(2)}, u32[]{:S(2)}) collective-permute-start(bf16[2,256,512]{2,1,0:T(8,128)(2,1)S(1)} %get-tuple-element.47), channel_id=1, source_target_pairs={{4,0},{12,1},{6,2},{14,3},{5,4},{13,5},{7,6},{15,7},{0,8},{8,9},{2... | collective-permute-start | bytes 1572872 | tf_op jit(solution)/shard_map/ppermute | solution.py:88
  220.5 43.4 %collective-permute-start.34 = (bf16[2,256,512]{2,1,0:T(8,128)(2,1)S(1)}, bf16[2,256,512]{2,1,0:T(8,128)(2,1)S(1)}, u32[]{:S(2)}, u32[]{:S(2)}) collective-permute-start(bf16[2,256,512]{2,1,0:T(8,128)(2,1)S(1)} %get-tuple-element.46), channel_id=1, source_target_pairs={{5,0},{13,1},{7,2},{15,3},{4,4},{12,5},{6,6},{14,7},{1,8},{9,9},{3... | collective-permute-start | bytes 1572872 | tf_op jit(solution)/shard_map/ppermute | solution.py:88
  224.1 3.0 %copy-start.2 = (bf16[2,4,256,512]{3,2,1,0:T(8,128)(2,1)}, bf16[2,4,256,512]{3,2,1,0:T(8,128)(2,1)S(1)}, u32[]{:S(2)}) copy-start(bf16[2,4,256,512]{3,2,1,0:T(8,128)(2,1)S(1)} %fusion.15) | copy-start | bytes 6291460
  264.1 2.0 copy-start.1

commit v6 on v5

--- a/solution.py
+++ b/solution.py
@@ -97,8 +97,10 @@
 
 
 def total(value):
-    for axis in ("lane", "row", "twin", "pair", "half"):
-        value = value + swap(value, axis)
+    value = value + swap(value, "lane")
+    for axes in (("row", "twin"), ("half", "pair")):
+        across = lax.ppermute(value, axes, [(i, 3 - i) for i in range(4)])
+        value = (value + swap(value, axes[1])) + (swap(value, axes[0]) + across)
     return value
 
 

time: 268 us -> 270 us (level)
  starting transfers between devices: 70.8 us -> 76.6 us
    ppermute x19, waiting for transfers between devices: 52.9 us -> 47.9 us  [swap(): return lax.ppermute(value, axis, [(0, 1), (1, 0)])]
    ppermute x0 -> x2, waiting for transfers between devices: none -> 4.52 us  [total(): across = lax.ppermute(value, axes, [(i, 3 - i) for i in range(4)])]
    ppermute x0 -> x2, starting transfers between devices: none -> 3.49 us  [total(): across = lax.ppermute(value, axes, [(i, 3 - i) for i in range(4)])]
  transfers between devices with their start and end apart: 35 -> 37, of which waited for: 15 -> 17; matrix products, arithmetic and copies ran while one was open for 2% -> 2% of each run, Pallas kernels for 10% -> 10%
where the time goes in v6:
time: 270 us
  waiting for transfers between devices  141 us (52%)
  starting transfers between devices  76.6 us (28%)
  Pallas kernels  38.6 us (14%)
  local copies, waits for them, and re-layouts  8.29 us (3%)
    ppermute x8, waiting for transfers between devices, to_home(): return lax.ppermute(piece, COLUMN, send_pairs(k))  52.1 us
    ppermute x19, waiting for transfers between devices, swap(): return lax.ppermute(value, axis, [(0, 1), (1, 0)])  47.9 us
    ppermute x8, waiting for transfers between devices, from_home(): return lax.ppermute(piece, COLUMN, [(b, a) for a, b in send_pairs(k)])  36.6 us
    ppermute x19, starting transfers between devices, swap(): return lax.ppermute(value, axis, [(0, 1), (1, 0)])  29.8 us
    ppermute x8, starting transfers between devices, from_home(): return lax.ppermute(piece, COLUMN, [(b, a) for a, b in send_pairs(k)])  21.9 us
    ppermute x8, starting transfers between devices, to_home(): return lax.ppermute(piece, COLUMN, send_pairs(k))  21.4 us
    pallas_call x1, Pallas kernels, whole_rows(): call(residual_kernel, 'residual', 1.0, 11, [vmem] * 3 + [hbm] * 8, [vmem]...  11.8 us
    pallas_call x1, Pallas kernels, whole_rows(): call(change_kernel, 'change', 1.0, 12, [vmem] * 3 + [hbm] * 4, [vmem, sme...  11.7 us
  transfers between devices with their start and end apart: 37, of which 17 were waited for; matrix products, arithmetic and copies ran while one was open for 2% of the time, Pallas kernels for 10%

profile of v6, /device:TPU:20, one launch (start us, length us, event | category | flops | bytes accessed | tf_op | source)
XLA Modules:
  0.0 269.7 jit_solution(13972184865250350903)
XLA Ops:
  0.7 1.7 dynamic-slice_bitcast_fusion.5
  2.3 2.4 collective-permute-start
  4.7 0.8 collective-permute-start.1
  5.5 1.9 collective-permute-start.4
  7.3 2.9 %collective-permute-start.5 = (bf16[2,256,512]{2,1,0:T(8,128)(2,1)S(1)}, bf16[2,256,512]{2,1,0:T(8,128)(2,1)S(1)}, u32[]{:S(2)}, u32[]{:S(2)}) collective-permute-start(bf16[2,256,512]{2,1,0:T(8,128)(2,1)S(1)} %get-tuple-element.55), channel_id=1, source_target_pairs={{0,5},{1,13},{2,7},{3,15},{4,4},{5,12},{6,6},{7,14},{8,1},{9,9},{1... | collective-permute-start | bytes 1572872 | tf_op jit(solution)/shard_map/ppermute | solution.py:84
  10.2 8.4 %collective-permute-done.refs_13_ = bf16[2,256,512]{2,1,0:T(8,128)(2,1)S(1)} collective-permute-done((bf16[2,256,512]{2,1,0:T(8,128)(2,1)S(1)}, bf16[2,256,512]{2,1,0:T(8,128)(2,1)S(1)}, u32[]{:S(2)}, u32[]{:S(2)}) %collective-permute-start) | collective-permute-done | bytes 524320 | tf_op jit(solution)/shard_map/ppermute | solution.py:84
  18.6 10.2 %collective-permute-done.1.refs_14_ = bf16[2,256,512]{2,1,0:T(8,128)(2,1)S(1)} collective-permute-done((bf16[2,256,512]{2,1,0:T(8,128)(2,1)S(1)}, bf16[2,256,512]{2,1,0:T(8,128)(2,1)S(1)}, u32[]{:S(2)}, u32[]{:S(2)}) %collective-permute-start.1) | collective-permute-done | bytes 524320 | tf_op jit(solution)/shard_map/ppermute | solution.py:84
  29.0 1.6 collective-permute-start.10
  30.5 10.9 %collective-permute-done.4.refs_15_ = bf16[2,256,512]{2,1,0:T(8,128)(2,1)S(1)} collective-permute-done((bf16[2,256,512]{2,1,0:T(8,128)(2,1)S(1)}, bf16[2,256,512]{2,1,0:T(8,128)(2,1)S(1)}, u32[]{:S(2)}, u32[]{:S(2)}) %collective-permute-start.4) | collective-permute-done | bytes 524320 | tf_op jit(solution)/shard_map/ppermute | solution.py:84
  41.4 9.3 %collective-permute-done.5.refs_16_ = bf16[2,256,512]{2,1,0:T(8,128)(2,1)S(1)} collective-permute-done((bf16[2,256,512]{2,1,0:T(8,128)(2,1)S(1)}, bf16[2,256,512]{2,1,0:T(8,128)(2,1)S(1)}, u32[]{:S(2)}, u32[]{:S(2)}) %collective-permute-start.5) | collective-permute-done | bytes 524320 | tf_op jit(solution)/shard_map/ppermute | solution.py:84
  50.9 1.6 collective-permute-start.6
  52.4 2.4 collective-permute-start.14
  54.8 18.2 %collective-permute-done.2.refs_3_ = bf16[2,2,256,512]{3,2,1,0:T(8,128)(2,1)S(1)} collective-permute-done((bf16[2,2,256,512]{3,2,1,0:T(8,128)(2,1)S(1)}, bf16[2,2,256,512]{3,2,1,0:T(8,128)(2,1)S(1)}, u32[]{:S(2)}, u32[]{:S(2)}) %collective-permute-start.2) | collective-permute-done | bytes 1048608 | tf_op jit(solution)/shard_map/ppermute | solution.py:92
  73.0 1.5 collective-permute-start.3
  74.6 3.5 %collective-permute-start.13 = (bf16[2,256,512]{2,1,0:T(8,128)(2,1)S(1)}, bf16[2,256,512]{2,1,0:T(8,128)(2,1)S(1)}, u32[]{:S(2)}, u32[]{:S(2)}) collective-permute-start(bf16[2,256,512]{2,1,0:T(8,128)(2,1)S(1)} %dynamic-slice_bitcast_fusion.2), channel_id=1, source_target_pairs={{0,0},{1,8},{2,2},{3,10},{4,1},{5,9},{6,3},{7,11},{8,4},{9,12},{10... | collective-permute-start | bytes 1572872 | tf_op jit(solution)/shard_map/ppermute | solution.py:84
  78.1 0.8 collective-permute-start.7
  78.9 16.6 %collective-permute-done.14.refs_6_ = bf16[2,2,256,512]{3,2,1,0:T(8,128)(2,1)} collective-permute-done((bf16[2,2,256,512]{3,2,1,0:T(8,128)(2,1)S(1)}, bf16[2,2,256,512]{3,2,1,0:T(8,128)(2,1)}, u32[]{:S(2)}, u32[]{:S(2)}) %collective-permute-start.14) | collective-permute-done | bytes 1048608 | tf_op jit(solution)/shard_map/ppermute | solution.py:92
  95.6 3.6 %collective-permute-start.15 = (bf16[2,256,512]{2,1,0:T(8,128)(2,1)S(1)}, bf16[2,256,512]{2,1,0:T(8,128)(2,1)S(1)}, u32[]{:S(2)}, u32[]{:S(2)}) collective-permute-start(bf16[2,256,512]{2,1,0:T(8,128)(2,1)S(1)} %get-tuple-element.51), channel_id=1, source_target_pairs={{0,4},{1,12},{2,6},{3,14},{4,5},{5,13},{6,7},{7,15},{8,0},{9,8},{1... | collective-permute-start | bytes 1572872 | tf_op jit(solution)/shard_map/ppermute | solution.py:84
  99.2 1.5 collective-permute-start.20
  100.7 1.3 collective-permute-done.7.refs_10_
  102.0 0.8 copy-done.15
  102.8 16.1 %collective-permute-start.9 = (bf16[2,2,256,512]{3,2,1,0:T(8,128)(2,1)S(1)}, bf16[2,2,256,512]{3,2,1,0:T(8,128)(2,1)S(1)}, u32[]{:S(2)}, u32[]{:S(2)}) collective-permute-start(bf16[2,2,256,512]{3,2,1,0:T(8,128)(2,1)S(1)} %collective-permute-done.2.refs_3_), channel_id=1, source_target_pairs={{0,1},{1,0},{2,3},{3,2},{4,5},{5,4},{6,7},{7,6},{8,9},{9,8},{10,11... | collective-permute-start | bytes 3145736 | tf_op jit(solution)/shard_map/ppermute | solution.py:92
  119.0 0.5 collective-permute-start.8
  119.5 5.6 %collective-permute-start.16 = (bf16[2,256,512]{2,1,0:T(8,128)(2,1)S(1)}, bf16[2,256,512]{2,1,0:T(8,128)(2,1)S(1)}, u32[]{:S(2)}, u32[]{:S(2)}) collective-permute-start(bf16[2,256,512]{2,1,0:T(8,128)(2,1)S(1)} %get-tuple-element.50), channel_id=1, source_target_pairs={{0,5},{1,13},{2,7},{3,15},{4,4},{5,12},{6,6},{7,14},{8,1},{9,9},{1... | collective-permute-start | bytes 1572872 | tf_op jit(solution)/shard_map/ppermute | solution.py:84
  125.1 12.1 %collective-permute-done.16.refs_12_ = bf16[2,256,512]{2,1,0:T(8,128)(2,1)S(1)} collective-permute-done((bf16[2,256,512]{2,1,0:T(8,128)(2,1)S(1)}, bf16[2,256,512]{2,1,0:T(8,128)(2,1)S(1)}, u32[]{:S(2)}, u32[]{:S(2)}) %collective-permute-start.16) | collective-permute-done | bytes 524320 | tf_op jit(solution)/shard_map/ppermute | solution.py:84
  137.2 0.5 collective-permute-start.21
  137.8 0.4 collective-permute-start.19
  138.3 0.4 copy-done.11
  138.7 0.3 copy-done.12
  139.0 1.0 copy-done.13
  140.0 0.2 collective-permute-start.17
  140.3 9.9 %collect.1 = (bf16[4,2,1024,512]{3,2,1,0:T(8,128)(2,1)S(1)}, bf16[2,512,1024]{2,1,0:T(8,128)(2,1)S(1)}, f32[4,2,256,512]{3,2,1,0:T(8,128)S(1)}) custom-call(s32[2]{0:T(128)S(1)} %pad_add_fusion.refs_0_, bf16[2,2,256,512]{3,2,1,0:T(8,128)(2,1)} %copy-done.4, bf16[2,2,256,512]{3,2,1,0:T(8,128)(2,1)} %copy-done.13, bf16[2,2,256,512]{3,2,1,0:T(8,128)(2,1)} %copy-done.9, ...), custom_call_target="tpu_custom_call" | custom-call | flops 4294967296 | bytes 16777216 | tf_op jit(solution)/shard_map/collect/pallas_call | solution.py:299
  150.3 11.8 %residual.1 = (bf16[4,2,1024,512]{3,2,1,0:T(8,128)(2,1)S(1)}, f32[4,2,256,512]{3,2,1,0:T(8,128)S(1)}, bf16[4,512,512]{2,1,0:T(8,128)(2,1)S(1)}, bf16[2,256,512]{2,1,0:T(8,128)(2,1)S(1)}, bf16[2,256,512]{2,1,0:T(8,128)(2,1)S(1)}) custom-call(s32[2]{0:T(128)S(1)} %pad_add_fusion.refs_0_, bf16[4,2,1024,512]{3,2,1,0:T(8,128)(2,1)S(1)} %get-tuple-element.30.refs_1_, ...), custom_call_target="tpu_custom_call" | custom-call | flops 8589934592 | bytes 16777216 | tf_op jit(solution)/shard_map/residual/pallas_call | solution.py:309
  162.1 4.7 %collective-permute-start.29 = (bf16[2,256,512]{2,1,0:T(8,128)(2,1)S(1)}, bf16[2,256,512]{2,1,0:T(8,128)(2,1)S(1)}, u32[]{:S(2)}, u32[]{:S(2)}) collective-permute-start(bf16[2,256,512]{2,1,0:T(8,128)(2,1)S(1)} %get-tuple-element.39.refs_4_), channel_id=1, source_target_pairs={{0,0},{8,1},{2,2},{10,3},{1,4},{9,5},{3,6},{11,7},{4,8},{12,9},{6,... | collective-permute-start | bytes 1572872 | tf_op jit(solution)/shard_map/ppermute | solution.py:88
  166.8 0.3 collective-permute-start.30
  167.1 5.2 %gradient.1 = (bf16[2,256,512]{2,1,0:T(8,128)(2,1)S(1)}, bf16[2,256,512]{2,1,0:T(8,128)(2,1)S(1)}) custom-call(s32[2]{0:T(128)S(1)} %pad_add_fusion.refs_0_, bf16[4,2,1024,512]{3,2,1,0:T(8,128)(2,1)S(1)} %get-tuple-element.30.refs_1_, bf16[4,2,1024,512]{3,2,1,0:T(8,128)(2,1)S(1)} %get-tuple-element.37.refs_2_, ...), custom_call_target="tpu_custom_call" | custom-call | flops 4294967296 | bytes 16777216 | tf_op jit(solution)/shard_map/gradient/pallas_call | solution.py:319
  172.4 11.7 %change.1 = (f32[4,2,256,512]{3,2,1,0:T(8,128)S(1)}, f32[2]{0:T(128)S(1)}) custom-call(s32[2]{0:T(128)S(1)} %pad_add_fusion.refs_0_, bf16[4,2,1024,512]{3,2,1,0:T(8,128)(2,1)S(1)} %get-tuple-element.30.refs_1_, bf16[4,2,1024,512]{3,2,1,0:T(8,128)(2,1)S(1)} %get-tuple-element.37.refs_2_, f32[4,2,256,512]{3,2,1,0:T(8,128)S(1)} %get-tuple-element.38.refs_3_, ...), custom_call_target="tpu_custom_call" | custom-call | flops 8589934592 | bytes 16777216 | tf_op jit(solution)/shard_map/change/pallas_call | solution.py:331
  184.2 4.7 %collective-permute-start.32 = (bf16[2,256,512]{2,1,0:T(8,128)(2,1)S(1)}, bf16[2,256,512]{2,1,0:T(8,128)(2,1)S(1)}, u32[]{:S(2)}, u32[]{:S(2)}) collective-permute-start(bf16[2,256,512]{2,1,0:T(8,128)(2,1)S(1)} %get-tuple-element.43.refs_7_), channel_id=1, source_target_pairs={{5,0},{13,1},{7,2},{15,3},{4,4},{12,5},{6,6},{14,7},{1,8},{9,9},{3... | collective-permute-start | bytes 1572872 | tf_op jit(solution)/shard_map/ppermute | solution.py:88
  188.9 1.1 collective-permute-done.22
  190.1 0.5 collective-permute-start.23
  190.6 3.0 %collective-permute-done.23 = f32[2]{0:T(128)S(1)} collective-permute-done((f32[2]{0:T(128)S(1)}, f32[2]{0:T(128)S(1)}, u32[]{:S(2)}, u32[]{:S(2)}) %collective-permute-start.23) | collective-permute-done | bytes 40 | tf_op jit(solution)/shard_map/ppermute | solution.py:92
  193.6 1.5 collective-permute-start.24
  195.1 2.0 collective-permute-done.24
  197.1 1.4 collective-permute-start.25
  198.6 3.0 %collective-permute-done.25 = f32[2]{0:T(128)S(1)} collective-permute-done((f32[2]{0:T(128)S(1)}, f32[2]{0:T(128)S(1)}, u32[]{:S(2)}, u32[]{:S(2)}) %collective-permute-start.25) | collective-permute-done | bytes 40 | tf_op jit(solution)/shard_map/ppermute | solution.py:102
  201.6 0.3 collective-permute-start.26
  201.9 3.2 %collective-permute-done.26 = f32[2]{0:T(128)S(1)} collective-permute-done((f32[2]{0:T(128)S(1)}, f32[2]{0:T(128)S(1)}, u32[]{:S(2)}, u32[]{:S(2)}) %collective-permute-start.26) | collective-permute-done | bytes 40 | tf_op jit(solution)/shard_map/ppermute | solution.py:92
  205.1 0.9 collective-permute-start.27
  206.0 3.7 %collective-permute-done.27 = f32[2]{0:T(128)S(1)} collective-permute-done((f32[2]{0:T(128)S(1)}, f32[2]{0:T(128)S(1)}, u32[]{:S(2)}, u32[]{:S(2)}) %collective-permute-start.27) | collective-permute-done | bytes 40 | tf_op jit(solution)/shard_map/ppermute | solution.py:92
  209.7 2.1 collective-permute-start.28
  211.8 1.5 collective-permute-done.28
  213.3 0.6 fusion.16
  215.2 1.2 fusion.7
  216.4 5.0 %collective-permute-start.33 = (bf16[2,256,512]{2,1,0:T(8,128)(2,1)S(1)}, bf16[2,256,512]{2,1,0:T(8,128)(2,1)S(1)}, u32[]{:S(2)}, u32[]{:S(2)}) collective-permute-start(bf16[2,256,512]{2,1,0:T(8,128)(2,1)S(1)} %get-tuple-element.49), channel_id=1, source_target_pairs={{0,0},{8,1},{2,2},{10,3},{1,4},{9,5},{3,6},{11,7},{4,8},{12,9},{6,... | collective-permute-start | bytes 1572872 | tf_op jit(solution)/shard_map/ppermute | solution.py:88
  221.4 3.9 %collective-permute-start.34 = (bf16[2,256,512]{2,1,0:T(8,128)(2,1)S(1)}, bf16[2,256,512]{2,1,0:T(8,128)(2,1)S(1)}, u32[]{:S(2)}, u32[]{:S(2)}) collective-permute-start(bf16[2,256,512]{2,1,0:T(8,128)(2,1)S(1)} %get-tuple-element.48), channel_id=1, source_target_pairs={{1,0},{9,1},{3,2},{11,3},{0,4},{8,5},{2,6},{10,7},{5,8},{13,9},{7,... | collective-permute-start | bytes 1572872 | tf_op jit(solution)/shard_map/ppermute | solution.py:88
  225.5 0.2 fusion.9
  225.8 0.2 fusion.11
  226.0 3.1 %collective-permute-start.36 = (bf16[2,256,512]{2,1,0:T(8,128)(2,1)S(1)}, bf16[2,256,512]{2,1,0:T(8,128)(2,1)S(1)}, u32[]{:S(2)}, u32[]{:S(2)}) collective-permute-start(bf16[2,256,512]{2,1,0:T(8,128)(2,1)S(1)} %get-tuple-element.46), channel_id=1, source_target_pairs={{5,0},{13,1},{7,2},{15,3},{4,4},{12,5},{6,6},{14,7},{1,8},{9,9},{3... | collective-permute-start | bytes 1572872 | tf_op jit(solution)/shard_map/ppermute | solution.py:88
  229.1 0.2 fusion.13
  229.6 26.7 %collective-permute-done.33 = bf16[2,256,512]{2,1,0:T(8,128)(2,1)S(1)} collective-permute-done((bf16[2,256,512]{2,1,0:T(8,128)(2,1)S(1)}, bf16[2,256,512]{2,1,0:T(8,128)(2,1)S(1)}, u32[]{:S(2)}, u32[]{:S(2)}) %collective-permute-start.33) | collective-permute-done | bytes 524320 | tf_op jit(solution)/shard_map/ppermute | solution.py:88
  256.3 0.5 broadcast_in_dim.49
  256.9 9.9 %collective-permute-done.34 = bf16[2,256,512]{2,1,0:T(8,128)(2,1)S(1)} collective-permute-done((bf16[2,256,512]{2,1,0:T(8,128)(2,1)S(1)}, bf16[2,256,512]{2,1,0:T(8,128)(2,1)S(1)}, u32[]{:S(2)}, u32[]{:S(2)}) %collective-permute-start.34) | collective-permute-done | bytes 524320 | tf_op jit(solution)/shard_map/ppermute | solution.py:88
  267.1 0.4 copy.22
  267.7 2.0 copy-done.1
  (74 shorter events, 2.1 us)
Async XLA Ops:
  2.3 16.3 %collective-permute-start = (bf16[2,256,512]{2,1,0:T(8,128)(2,1)S(1)}, bf16[2,256,512]{2,1,0:T(8,128)(2,1)S(1)}, u32[]{:S(2)}, u32[]{:S(2)}) collective-permute-start(bf16[2,256,512]{2,1,0:T(8,128)(2,1)S(1)} %get-tuple-element.54), channel_id=1, source_target_pairs={{0,0},{1,8},{2,2},{3,10},{4,1},{5,9},{6,3},{7,11},{8,4},{9,12},{10... | collective-permute-start | bytes 1572872 | tf_op jit(solution)/shard_map/ppermute | solution.py:84
  4.7 24.1 %collective-permute-start.1 = (bf16[2,256,512]{2,1,0:T(8,128)(2,1)S(1)}, bf16[2,256,512]{2,1,0:T(8,128)(2,1)S(1)}, u32[]{:S(2)}, u32[]{:S(2)}) collective-permute-start(bf16[2,256,512]{2,1,0:T(8,128)(2,1)S(1)} %get-tuple-element.53), channel_id=1, source_target_pairs={{0,1},{1,9},{2,3},{3,11},{4,0},{5,8},{6,2},{7,10},{8,5},{9,13},{10... | collective-permute-start | bytes 1572872 | tf_op jit(solution)/shard_map/ppermute | solution.py:84
  5.5 35.9 %collective-permute-start.4 = (bf16[2,256,512]{2,1,0:T(8,128)(2,1)S(1)}, bf16[2,256,512]{2,1,0:T(8,128)(2,1)S(1)}, u32[]{:S(2)}, u32[]{:S(2)}) collective-permute-start(bf16[2,256,512]{2,1,0:T(8,128)(2,1)S(1)} %get-tuple-element.52), channel_id=1, source_target_pairs={{0,4},{1,12},{2,6},{3,14},{4,5},{5,13},{6,7},{7,15},{8,0},{9,8},{1... | collective-permute-start | bytes 1572872 | tf_op jit(solution)/shard_map/ppermute | solution.py:84
  7.3 43.4 %collective-permute-start.5 = (bf16[2,256,512]{2,1,0:T(8,128)(2,1)S(1)}, bf16[2,256,512]{2,1,0:T(8,128)(2,1)S(1)}, u32[]{:S(2)}, u32[]{:S(2)}) collective-permute-start(bf16[2,256,512]{2,1,0:T(8,128)(2,1)S(1)} %get-tuple-element.55), channel_id=1, source_target_pairs={{0,5},{1,13},{2,7},{3,15},{4,4},{5,12},{6,6},{7,14},{8,1},{9,9},{1... | collective-permute-start | bytes 1572872 | tf_op jit(solution)/shard_map/ppermute | solution.py:84
  18.6 32.2 %copy-start.5 = (bf16[2,256,512]{2,1,0:T(8,128)(2,1)}, bf16[2,256,512]{2,1,0:T(8,128)(2,1)S(1)}, u32[]{:S(2)}) copy-start(bf16[2,256,512]{2,1,0:T(8,128)(2,1)S(1)} %collective-permute-done.refs_13_) | copy-start | bytes 1572868
  28.8 22.1 %copy-start.6 = (bf16[2,256,512]{2,1,0:T(8,128)(2,1)}, bf16[2,256,512]{2,1,0:T(8,128)(2,1)S(1)}, u32[]{:S(2)}) copy-start(bf16[2,256,512]{2,1,0:T(8,128)(2,1)S(1)} %collective-permute-done.1.refs_14_) | copy-start | bytes 1572868
  28.8 45.8 %copy-start = (bf16[2,1,1024,512]{3,2,1,0:T(8,128)(2,1)S(1)}, bf16[2,1,1024,512]{3,2,1,0:T(8,128)(2,1)}, u32[]{:S(2)}) copy-start(bf16[2,1,1024,512]{3,2,1,0:T(8,128)(2,1)} %param.3) | copy-start | bytes 6291460
  28.9 90.2 %copy-start.4 = (bf16[2,2,256,512]{3,2,1,0:T(8,128)(2,1)}, bf16[2,2,256,512]{3,2,1,0:T(8,128)(2,1)S(1)}, u32[]{:S(2)}) copy-start(bf16[2,2,256,512]{3,2,1,0:T(8,128)(2,1)S(1)} %pad_maximum_fusion.refs_1_) | copy-start | bytes 3145732
  28.9 44.1 %collective-permute-start.2 = (bf16[2,2,256,512]{3,2,1,0:T(8,128)(2,1)S(1)}, bf16[2,2,256,512]{3,2,1,0:T(8,128)(2,1)S(1)}, u32[]{:S(2)}, u32[]{:S(2)}) collective-permute-start(bf16[2,2,256,512]{3,2,1,0:T(8,128)(2,1)S(1)} %pad_maximum_fusion.refs_1_), channel_id=1, source_target_pairs={{0,4},{4,0},{1,5},{5,1},{2,6},{6,2},{3,7},{7,3},{8,12},{12,8},{9,1... | collective-permute-start | bytes 3145736 | tf_op jit(solution)/shard_map/ppermute | solution.py:92
  29.0 45.6 %collective-permute-start.10 = (bf16[2,2,256,512]{3,2,1,0:T(8,128)(2,1)S(1)}, bf16[2,2,256,512]{3,2,1,0:T(8,128)(2,1)S(1)}, u32[]{:S(2)}, u32[]{:S(2)}) collective-permute-start(bf16[2,2,256,512]{3,2,1,0:T(8,128)(2,1)S(1)} %pad_maximum_fusion.refs_1_), channel_id=1, source_target_pairs={{0,16},{16,0},{1,17},{17,1},{2,18},{18,2},{3,19},{19,3},{4,20},{20... | collective-permute-start | bytes 3145736 | tf_op jit(solution)/shard_map/ppermute | solution.py:92
  41.4 36.7 %copy-start.7 = (bf16[2,256,512]{2,1,0:T(8,128)(2,1)}, bf16[2,256,512]{2,1,0:T(8,128)(2,1)S(1)}, u32[]{:S(2)}) copy-start(bf16[2,256,512]{2,1,0:T(8,128)(2,1)S(1)} %collective-permute-done.4.refs_15_) | copy-start | bytes 1572868
  50.7 27.4 %copy-start.8 = (bf16[2,256,512]{2,1,0:T(8,128)(2,1)}, bf16[2,256,512]{2,1,0:T(8,128)(2,1)S(1)}, u32[]{:S(2)}) copy-start(bf16[2,256,512]{2,1,0:T(8,128)(2,1)S(1)} %collective-permute-done.5.refs_16_) | copy-start | bytes 1572868
  50.9 87.4 %copy-start.3 = (bf16[2,2,256,512]{3,2,1,0:T(8,128)(2,1)}, bf16[2,2,256,512]{3,2,1,0:T(8,128)(2,1)S(1)}, u32[]{:S(2)}) copy-start(bf16[2,2,256,512]{3,2,1,0:T(8,128)(2,1)S(1)} %pad_maximum_fusion.1.refs_4_) | copy-start | bytes 3145732
  50.9 27.2 %collective-permute-start.6 = (bf16[2,2,256,512]{3,2,1,0:T(8,128)(2,1)S(1)}, bf16[2,2,256,512]{3,2,1,0:T(8,128)(2,1)}, u32[]{:S(2)}, u32[]{:S(2)}) collective-permute-start(bf16[2,2,256,512]{3,2,1,0:T(8,128)(2,1)S(1)} %pad_maximum_fusion.1.refs_4_), channel_id=1, source_target_pairs={{0,16},{16,0},{1,17},{17,1},{2,18},{18,2},{3,19},{19,3},{4,20},{20... | collective-permute-start | bytes 3145736 | tf_op jit(solution)/shard_map/ppermute | solution.py:92
  52.4 43.1 %collective-permute-start.14 = (bf16[2,2,256,512]{3,2,1,0:T(8,128)(2,1)S(1)}, bf16[2,2,256,512]{3,2,1,0:T(8,128)(2,1)}, u32[]{:S(2)}, u32[]{:S(2)}) collective-permute-start(bf16[2,2,256,512]{3,2,1,0:T(8,128)(2,1)S(1)} %pad_maximum_fusion.1.refs_4_), channel_id=1, source_target_pairs={{0,4},{4,0},{1,5},{5,1},{2,6},{6,2},{3,7},{7,3},{8,12},{12,8},{9,1... | collective-permute-start | bytes 3145736 | tf_op jit(solution)/shard_map/ppermute | solution.py:92
  73.0 29.8 %copy-start.9 = (bf16[2,2,256,512]{3,2,1,0:T(8,128)(2,1)}, bf16[2,2,256,512]{3,2,1,0:T(8,128)(2,1)S(1)}, u32[]{:S(2)}) copy-start(bf16[2,2,256,512]{3,2,1,0:T(8,128)(2,1)S(1)} %collective-permute-done.2.refs_3_) | copy-start | bytes 3145732
  73.0 29.8 %collective-permute-start.3 = (bf16[2,2,256,512]{3,2,1,0:T(8,128)(2,1)S(1)}, bf16[2,2,256,512]{3,2,1,0:T(8,128)(2,1)}, u32[]{:S(2)}, u32[]{:S(2)}) collective-permute-start(bf16[2,2,256,512]{3,2,1,0:T(8,128)(2,1)S(1)} %collective-permute-done.2.refs_3_), channel_id=1, source_target_pairs={{0,16},{16,0},{1,17},{17,1},{2,18},{18,2},{3,19},{19,3},{4,20},{20... | collective-permute-start | bytes 3145736 | tf_op jit(solution)/shard_map/ppermute | solution.py:92
  74.5 44.4 %copy-start.10 = (bf16[2,2,256,512]{3,2,1,0:T(8,128)(2,1)}, bf16[2,2,256,512]{3,2,1,0:T(8,128)(2,1)S(1)}, u32[]{:S(2)}) copy-start(bf16[2,2,256,512]{3,2,1,0:T(8,128)(2,1)S(1)} %collective-permute-done.10.refs_5_) | copy-start | bytes 3145732
  74.6 44.4 %collective-permute-start.13 = (bf16[2,256,512]{2,1,0:T(8,128)(2,1)S(1)}, bf16[2,256,512]{2,1,0:T(8,128)(2,1)S(1)}, u32[]{:S(2)}, u32[]{:S(2)}) collective-permute-start(bf16[2,256,512]{2,1,0:T(8,128)(2,1)S(1)} %dynamic-slice_bitcast_fusion.2), channel_id=1, source_target_pairs={{0,0},{1,8},{2,2},{3,10},{4,1},{5,9},{6,3},{7,11},{8,4},{9,12},{10... | collective-permute-start | bytes 1572872 | tf_op jit(solution)/shard_map/ppermute | solution.py:84
  78.1 23.8 %collective-permute-start.7 = (bf16[2,256,512]{2,1,0:T(8,128)(2,1)S(1)}, bf16[2,256,512]{2,1,0:T(8,128)(2,1)S(1)}, u32[]{:S(2)}, u32[]{:S(2)}) collective-permute-start(bf16[2,256,512]{2,1,0:T(8,128)(2,1)S(1)} %dynamic-slice_bitcast_fusion.3), channel_id=1, source_target_pairs={{0,1},{1,9},{2,3},{3,11},{4,0},{5,8},{6,2},{7,10},{8,5},{9,13},{10... | collective-permute-start | bytes 1572872 | tf_op jit(solution)/shard_map/ppermute | solution.py:84
  95.6 24.0 %collective-permute-start.15 = (bf16[2,256,512]{2,1,0:T(8,128)(2,1)S(1)}, bf16[2,256,512]{2,1,0:T(8,128)(2,1)S(1)}, u32[]{:S(2)}, u32[]{:S(2)}) collective-permute-start(bf16[2,256,512]{2,1,0:T(8,128)(2,1)S(1)} %get-tuple-element.51), channel_id=1, source_target_pairs={{0,4},{1,12},{2,6},{3,14},{4,5},{5,13},{6,7},{7,15},{8,0},{9,8},{1... | collective-permute-start | bytes 1572872 | tf_op jit(solution)/shard_map/ppermute | solution.py:84
  99.2 38.0 %collective-permute-start.20 = (bf16[2,2,256,512]{3,2,1,0:T(8,128)(2,1)}, bf16[2,2,256,512]{3,2,1,0:T(8,128)(2,1)}, u32[]{:S(2)}, u32[]{:S(2)}) collective-permute-start(bf16[2,2,256,512]{3,2,1,0:T(8,128)(2,1)} %collective-permute-done.14.refs_6_), channel_id=1, source_target_pairs={{0,16},{16,0},{1,17},{17,1},{2,18},{18,2},{3,19},{19,3},{4,20},{20... | collective-permute-start | bytes 3145736 | tf_op jit(solution)/shard_map/ppermute | solution.py:92
  102.0 0.8 copy-start.15
  102.8 35.0 %collective-permute-start.9 = (bf16[2,2,256,512]{3,2,1,0:T(8,128)(2,1)S(1)}, bf16[2,2,256,512]{3,2,1,0:T(8,128)(2,1)S(1)}, u32[]{:S(2)}, u32[]{:S(2)}) collective-permute-start(bf16[2,2,256,512]{3,2,1,0:T(8,128)(2,1)S(1)} %collective-permute-done.2.refs_3_), channel_id=1, source_target_pairs={{0,1},{1,0},{2,3},{3,2},{4,5},{5,4},{6,7},{7,6},{8,9},{9,8},{10,11... | collective-permute-start | bytes 3145736 | tf_op jit(solution)/shard_map/ppermute | solution.py:92
  118.9 18.9 %collective-permute-start.11 = (bf16[2,2,256,512]{3,2,1,0:T(8,128)(2,1)S(1)}, bf16[2,2,256,512]{3,2,1,0:T(8,128)(2,1)S(1)}, u32[]{:S(2)}, u32[]{:S(2)}) collective-permute-start(bf16[2,2,256,512]{3,2,1,0:T(8,128)(2,1)S(1)} %collective-permute-done.10.refs_5_), channel_id=1, source_target_pairs={{0,1},{1,0},{2,3},{3,2},{4,5},{5,4},{6,7},{7,6},{8,9},{9,8},{10,11... | collective-permute-start | bytes 3145736 | tf_op jit(solution)/shard_map/ppermute | solution.py:92
  119.0 19.3 %copy-start.14 = (bf16[2,256,512]{2,1,0:T(8,128)(2,1)}, bf16[2,256,512]{2,1,0:T(8,128)(2,1)S(1)}, u32[]{:S(2)}) copy-start(bf16[2,256,512]{2,1,0:T(8,128)(2,1)S(1)} %collective-permute-done.13.refs_9_) | copy-start | bytes 1572868
  119.0 19.2 %collective-permute-start.8 = (bf16[2,2,256,512]{3,2,1,0:T(8,128)(2,1)S(1)}, bf16[2,2,256,512]{3,2,1,0:T(8,128)(2,1)S(1)}, u32[]{:S(2)}, u32[]{:S(2)}) collective-permute-start(bf16[2,2,256,512]{3,2,1,0:T(8,128)(2,1)S(1)} %pad_maximum_fusion.refs_1_), channel_id=1, source_target_pairs={{0,1},{1,0},{2,3},{3,2},{4,5},{5,4},{6,7},{7,6},{8,9},{9,8},{10,11... | collective-permute-start | bytes 3145736 | tf_op jit(solution)/shard_map/ppermute | solution.py:92
  119.5 18.8 %copy-start.16 = (bf16[2,256,512]{2,1,0:T(8,128)(2,1)}, bf16[2,256,512]{2,1,0:T(8,128)(2,1)S(1)}, u32[]{:S(2)}) copy-start(bf16[2,256,512]{2,1,0:T(8,128)(2,1)S(1)} %collective-permute-done.15.refs_11_) | copy-start | bytes 1572868
  119.5 17.7 %collective-permute-start.16 = (bf16[2,256,512]{2,1,0:T(8,128)(2,1)S(1)}, bf16[2,256,512]{2,1,0:T(8,128)(2,1)S(1)}, u32[]{:S(2)}, u32[]{:S(2)}) collective-permute-start(bf16[2,256,512]{2,1,0:T(8,128)(2,1)S(1)} %get-tuple-element.50), channel_id=1, source_target_pairs={{0,5},{1,13},{2,7},{3,15},{4,4},{5,12},{6,6},{7,14},{8,1},{9,9},{1... | collective-permute-start | bytes 1572872 | tf_op jit(solution)/shard_map/ppermute | solution.py:84
  137.2 1.1 copy-start.17
  137.2 3.1 %collective-permute-start.12 = (bf16[2,2,256,512]{3,2,1,0:T(8,128)(2,1)}, bf16[2,2,256,512]{3,2,1,0:T(8,128)(2,1)}, u32[]{:S(2)}, u32[]{:S(2)}) collective-permute-start(bf16[2,2,256,512]{3,2,1,0:T(8,128)(2,1)} %collective-permute-done.3.refs_7_), channel_id=1, source_target_pairs={{0,1},{1,0},{2,3},{3,2},{4,5},{5,4},{6,7},{7,6},{8,9},{9,8},{10,11... | collective-permute-start | bytes 3145736 | tf_op jit(solution)/shard_map/ppermute | solution.py:92
  137.2 13.0 %collective-permute-start.21 = (bf16[2,2,256,512]{3,2,1,0:T(8,128)(2,1)}, bf16[2,2,256,512]{3,2,1,0:T(8,128)(2,1)}, u32[]{:S(2)}, u32[]{:S(2)}) collective-permute-start(bf16[2,2,256,512]{3,2,1,0:T(8,128)(2,1)} %collective-permute-done.20.refs_10_), channel_id=1, source_target_pairs={{0,1},{1,0},{2,3},{3,2},{4,5},{5,4},{6,7},{7,6},{8,9},{9,8},{10,11... | collective-permute-start | bytes 3145736 | tf_op jit(solution)/shard_map/ppermute | solution.py:92
  137.7 1.0 copy-start.11
  137.7 12.5 %collective-permute-start.18 = (bf16[2,2,256,512]{3,2,1,0:T(8,128)(2,1)}, bf16[2,2,256,512]{3,2,1,0:T(8,128)(2,1)}, u32[]{:S(2)}, u32[]{:S(2)}) collective-permute-start(bf16[2,2,256,512]{3,2,1,0:T(8,128)(2,1)} %collective-permute-done.14.refs_6_), channel_id=1, source_target_pairs={{0,1},{1,0},{2,3},{3,2},{4,5},{5,4},{6,7},{7,6},{8,9},{9,8},{10,11... | collective-permute-start | bytes 3145736 | tf_op jit(solution)/shard_map/ppermute | solution.py:92
  137.8 1.2 copy-start.12
  137.8 12.4 %collective-permute-start.19 = (bf16[2,2,256,512]{3,2,1,0:T(8,128)(2,1)}, bf16[2,2,256,512]{3,2,1,0:T(8,128)(2,1)}, u32[]{:S(2)}, u32[]{:S(2)}) collective-permute-start(bf16[2,2,256,512]{3,2,1,0:T(8,128)(2,1)} %collective-permute-done.6.refs_8_), channel_id=1, source_target_pairs={{0,1},{1,0},{2,3},{3,2},{4,5},{5,4},{6,7},{7,6},{8,9},{9,8},{10,11... | collective-permute-start | bytes 3145736 | tf_op jit(solution)/shard_map/ppermute | solution.py:92
  139.0 1.0 copy-start.13
  140.0 10.3 %collective-permute-start.17 = (bf16[2,2,256,512]{3,2,1,0:T(8,128)(2,1)S(1)}, bf16[2,2,256,512]{3,2,1,0:T(8,128)(2,1)}, u32[]{:S(2)}, u32[]{:S(2)}) collective-permute-start(bf16[2,2,256,512]{3,2,1,0:T(8,128)(2,1)S(1)} %pad_maximum_fusion.1.refs_4_), channel_id=1, source_target_pairs={{0,1},{1,0},{2,3},{3,2},{4,5},{5,4},{6,7},{7,6},{8,9},{9,8},{10,11... | collective-permute-start | bytes 3145736 | tf_op jit(solution)/shard_map/ppermute | solution.py:92
  162.1 59.3 %collective-permute-start.29 = (bf16[2,256,512]{2,1,0:T(8,128)(2,1)S(1)}, bf16[2,256,512]{2,1,0:T(8,128)(2,1)S(1)}, u32[]{:S(2)}, u32[]{:S(2)}) collective-permute-start(bf16[2,256,512]{2,1,0:T(8,128)(2,1)S(1)} %get-tuple-element.39.refs_4_), channel_id=1, source_target_pairs={{0,0},{8,1},{2,2},{10,3},{1,4},{9,5},{3,6},{11,7},{4,8},{12,9},{6,... | collective-permute-start | bytes 1572872 | tf_op jit(solution)/shard_map/ppermute | solution.py:88
  166.8 58.9 %collective-permute-start.30 = (bf16[2,256,512]{2,1,0:T(8,128)(2,1)S(1)}, bf16[2,256,512]{2,1,0:T(8,128)(2,1)S(1)}, u32[]{:S(2)}, u32[]{:S(2)}) collective-permute-start(bf16[2,256,512]{2,1,0:T(8,128)(2,1)S(1)} %get-tuple-element.40.refs_5_), channel_id=1, source_target_pairs={{1,0},{9,1},{3,2},{11,3},{0,4},{8,5},{2,6},{10,7},{5,8},{13,9},{7,... | collective-permute-start | bytes 1572872 | tf_op jit(solution)/shard_map/ppermute | solution.py:88
  172.3 53.7 %collective-permute-start.31 = (bf16[2,256,512]{2,1,0:T(8,128)(2,1)S(1)}, bf16[2,256,512]{2,1,0:T(8,128)(2,1)S(1)}, u32[]{:S(2)}, u32[]{:S(2)}) collective-permute-start(bf16[2,256,512]{2,1,0:T(8,128)(2,1)S(1)} %get-tuple-element.42.refs_6_), channel_id=1, source_target_pairs={{4,0},{12,1},{6,2},{14,3},{5,4},{13,5},{7,6},{15,7},{0,8},{8,9},{2... | collective-permute-start | bytes 1572872 | tf_op jit(solution)/shard_map/ppermute | solution.py:88
  184.2 45.2 %collective-permute-start.32 = (bf16[2,256,512]{2,1,0:T(8,128)(2,1)S(1)}, bf16[2,256,512]{2,1,0:T(8,128)(2,1)S(1)}, u32[]{:S(2)}, u32[]{:S(2)}) collective-permute-start(bf16[2,256,512]{2,1,0:T(8,128)(2,1)S(1)} %get-tuple-element.43.refs_7_), channel_id=1, source_target_pairs={{5,0},{13,1},{7,2},{15,3},{4,4},{12,5},{6,6},{14,7},{1,8},{9,9},{3... | collective-permute-start | bytes 1572872 | tf_op jit(solution)/shard_map/ppermute | solution.py:88
  188.9 1.2 collective-permute-start.22
  190.1 3.5 %collective-permute-start.23 = (f32[2]{0:T(128)S(1)}, f32[2]{0:T(128)S(1)}, u32[]{:S(2)}, u32[]{:S(2)}) collective-permute-start(f32[2]{0:T(128)S(1)} %add.96), channel_id=1, source_target_pairs={{0,2},{2,0},{1,3},{3,1},{4,6},{6,4},{5,7},{7,5},{8,10},{10,8},{9,1... | collective-permute-start | bytes 32 | tf_op jit(solution)/shard_map/ppermute | solution.py:92
  193.6 3.5 %collective-permute-start.24 = (f32[2]{0:T(128)S(1)}, f32[2]{0:T(128)S(1)}, u32[]{:S(2)}, u32[]{:S(2)}) collective-permute-start(f32[2]{0:T(128)S(1)} %add.96), channel_id=1, source_target_pairs={{0,16},{16,0},{1,17},{17,1},{2,18},{18,2},{3,19},{19,3},{4,20},{20... | collective-permute-start | bytes 32 | tf_op jit(solution)/shard_map/ppermute | solution.py:92
  197.1 4.4 %collective-permute-start.25 = (f32[2]{0:T(128)S(1)}, f32[2]{0:T(128)S(1)}, u32[]{:S(2)}, u32[]{:S(2)}) collective-permute-start(f32[2]{0:T(128)S(1)} %add.96), channel_id=1, source_target_pairs={{0,18},{2,16},{16,2},{18,0},{1,19},{3,17},{17,3},{19,1},{4,22},{6,... | collective-permute-start | bytes 32 | tf_op jit(solution)/shard_map/ppermute | solution.py:102
  201.6 3.5 %collective-permute-start.26 = (f32[2]{0:T(128)S(1)}, f32[2]{0:T(128)S(1)}, u32[]{:S(2)}, u32[]{:S(2)}) collective-permute-start(f32[2]{0:T(128)S(1)} %add_add_fusion.1), channel_id=1, source_target_pairs={{0,4},{4,0},{1,5},{5,1},{2,6},{6,2},{3,7},{7,3},{8,12},{12,8},{9,1... | collective-permute-start | bytes 32 | tf_op jit(solution)/shard_map/ppermute | solution.py:92
  205.1 4.6 %collective-permute-start.27 = (f32[2]{0:T(128)S(1)}, f32[2]{0:T(128)S(1)}, u32[]{:S(2)}, u32[]{:S(2)}) collective-permute-start(f32[2]{0:T(128)S(1)} %add_add_fusion.1), channel_id=1, source_target_pairs={{0,8},{8,0},{1,9},{9,1},{2,10},{10,2},{3,11},{11,3},{4,12},{12,4},... | collective-permute-start | bytes 32 | tf_op jit(solution)/shard_map/ppermute | solution.py:92
  209.7 3.6 %collective-permute-start.28 = (f32[2]{0:T(128)S(1)}, f32[2]{0:T(128)S(1)}, u32[]{:S(2)}, u32[]{:S(2)}) collective-permute-start(f32[2]{0:T(128)S(1)} %add_add_fusion.1), channel_id=1, source_target_pairs={{0,12},{4,8},{8,4},{12,0},{1,13},{5,9},{9,5},{13,1},{2,14},{6,10},... | collective-permute-start | bytes 32 | tf_op jit(solution)/shard_map/ppermute | solution.py:102
  216.4 39.9 %collective-permute-start.33 = (bf16[2,256,512]{2,1,0:T(8,128)(2,1)S(1)}, bf16[2,256,512]{2,1,0:T(8,128)(2,1)S(1)}, u32[]{:S(2)}, u32[]{:S(2)}) collective-permute-start(bf16[2,256,512]{2,1,0:T(8,128)(2,1)S(1)} %get-tuple-element.49), channel_id=1, source_target_pairs={{0,0},{8,1},{2,2},{10,3},{1,4},{9,5},{3,6},{11,7},{4,8},{12,9},{6,... | collective-permute-start | bytes 1572872 | tf_op jit(solution)/shard_map/ppermute | solution.py:88
  221.4 45.4 %collective-permute-start.34 = (bf16[2,256,512]{2,1,0:T(8,128)(2,1)S(1)}, bf16[2,256,512]{2,1,0:T(8,128)(2,1)S(1)}, u32[]{:S(2)}, u32[]{:S(2)}) collective-permute-start(bf16[2,256,512]{2,1,0:T(8,128)(2,1)S(1)} %get-tuple-element.48), channel_id=1, source_target_pairs={{1,0},{9,1},{3,2},{11,3},{0,4},{8,5},{2,6},{10,7},{5,8},{13,9},{7,... | collective-permute-start | bytes 1572872 | tf_op jit(solution)/shard_map/ppermute | solution.py:88
  225.7 41.3 %collective-permute-start.35 = (bf16[2,256,512]{2,1,0:T(8,128)(2,1)S(1)}, bf16[2,256,512]{2,1,0:T(8,128)(2,1)S(1)}, u32[]{:S(2)}, u32[]{:S(2)}) collective-permute-start(bf16[2,256,512]{2,1,0:T(8,128)(2,1)S(1)} %get-tuple-element.47), channel_id=1, source_target_pairs={{4,0},{12,1},{6,2},{14,3},{5,4},{13,5},{7,6},{15,7},{0,8},{8,9},{2... | collective-permute-start | bytes 1572872 | tf_op jit(solution)/shard_map/ppermute | solution.py:88
  226.0 41.6 %collective-permute-start.36 = (bf16[2,256,512]{2,1,0:T(8,128)(2,1)S(1)}, bf16[2,256,512]{2,1,0:T(8,128)(2,1)S(1)}, u32[]{:S(2)}, u32[]{:S(2)}) collective-permute-start(bf16[2,256,512]{2,1,0:T(8,128)(2,1)S(1)} %get-tuple-element.46), channel_id=1, source_target_pairs={{5,0},{13,1},{7,2},{15,3},{4,4},{12,5},{6,6},{14,7},{1,8},{9,9},{3... | collective-permute-start | bytes 1572872 | tf_op jit(solution)/shard_map/ppermute | solution.py:88
  229.6 27.2 %copy-start.2 = (bf16[2,4,256,512]{3,2,1,0:T(8,128)(2,1)}, bf16[2,4,256,512]{3,2,1,0:T(8,128)(2,1)S(1)}, u32[]{:S(2)}) copy-start(bf16[2,4,256,512]{3,2,1,0:T(8,128)(2,1)S(1)} %fusion.15) | copy-start | bytes 6291460
  267.7 2.0 copy-start.1
